TPU v7x, 32 devices: a whole 2x2x4 slice. The times are simulated.
32 devices in a mesh: wide: 8 (over z, x), narrow: 4 (over y, core).
Axes of the slice: x: 2, y: 2, z: 4, core: 2. Of those that a mesh axis runs over, the one named last changes fastest.
Arguments:
- tokens: bfloat16 [24, 512, 768], P('wide', 'narrow'), may hold values from -6 to 6
- lengths: int32 [24], P('wide'), may hold values from 1 to 512, as said below
- qkv_weight: bfloat16 [768, 2304], replicated, may hold values from -0.21875 to 0.21875
- qv_bias: float32 [2, 768], replicated, may hold values from -3 to 3
- out_weight: bfloat16 [768, 768], replicated, may hold values from -0.875 to 0.875
- out_bias: float32 [768], replicated, may hold values from -2 to 2
- norm1_gain: float32 [768], replicated, may hold values from 0.25 to 1.75
- norm1_shift: float32 [768], replicated, may hold values from -2 to 2
- up_weight: bfloat16 [768, 3072], replicated, may hold values from -0.21875 to 0.21875
- up_bias: float32 [3072], replicated, may hold values from -3 to 3
- down_weight: bfloat16 [3072, 768], replicated, may hold values from -0.109375 to 0.109375
- down_bias: float32 [768], replicated, may hold values from -2 to 2
- norm2_gain: float32 [768], replicated, may hold values from 0.25 to 1.75
- norm2_shift: float32 [768], replicated, may hold values from -2 to 2
- cotangent: bfloat16 [24, 512, 768], P('wide', 'narrow'), may hold values from -6 to 6
Outputs:
- output: bfloat16 [24, 512, 768], P('wide', 'narrow')
- input_grad: bfloat16 [24, 512, 768], P('wide', 'narrow')
- qkv_weight_grad: float32 [768, 2304], P('narrow')
- qv_bias_grad: float32 [2, 768], P(None, 'narrow')
- out_weight_grad: float32 [768, 768], P('narrow')
- out_bias_grad: float32 [768], P('narrow')
- norm1_gain_grad: float32 [768], P('narrow')
- norm1_shift_grad: float32 [768], P('narrow')
- up_weight_grad: float32 [768, 3072], P('narrow')
- up_bias_grad: float32 [3072], P('narrow')
- down_weight_grad: float32 [3072, 768], P('narrow')
- down_bias_grad: float32 [768], P('narrow')
- norm2_gain_grad: float32 [768], P('narrow')
- norm2_shift_grad: float32 [768], P('narrow')
Inputs may be any that keep to these rules, and one draw needn't show every extreme that they name: The slots of one group of 3 (aligned blocks) share a bucket b from 1 to 4, with lengths from (b - 1) * 128 + 1 to b * 128; slot 0 has length 512.
All inputs are finite; a program needn't handle non-finite values.
Results may differ from a plain program's by a relative error of at most 0.014.
Values may be sent and summed in bfloat16 or wider, within the bound.
A program may use at most 192 MiB of HBM per device.

v0:
```python
import jax
import jax.numpy as jnp
from jax import lax
from jax.sharding import PartitionSpec as P

H = 12
HD = 64


epsilon = 1e-12
root_half = 0.7071067811865476
inv_root_two_pi = 0.3989422804014327


def norm_forward(values, norm_gain, norm_shift):
    center = values - jnp.mean(values, axis=-1, keepdims=True)
    row_scale = lax.rsqrt(jnp.mean(center * center, axis=-1, keepdims=True) + epsilon)
    normed = center * row_scale
    return (normed * norm_gain + norm_shift, normed, row_scale)


def norm_backward(upstream, normed, row_scale, norm_gain):
    gain_grad = jnp.sum(upstream * normed, axis=0)
    shift_grad = jnp.sum(upstream, axis=0)
    scaled = upstream * norm_gain
    inner = scaled - jnp.mean(scaled, axis=-1, keepdims=True)
    inner = inner - normed * jnp.mean(scaled * normed, axis=-1, keepdims=True)
    return (row_scale * inner, gain_grad, shift_grad)


def split_packed(packed_seq):
    head_size = packed_seq.shape[2] // 3
    return (
        packed_seq[:, :, :head_size],
        packed_seq[:, :, head_size : 2 * head_size],
        packed_seq[:, :, 2 * head_size :],
    )


def masked_scores(query_part, key_part, length):
    raw_scores = jnp.einsum(
        "qhe,khe->hqk", query_part, key_part, preferred_element_type=jnp.float32
    )
    live_keys = lax.iota(jnp.int32, key_part.shape[0]) < length
    return jnp.where(live_keys[None, None, :], raw_scores * 0.125, -1000000000.0)


def attend(packed_seq, length):
    query_part, key_part, value_part = split_packed(packed_seq)
    scores = masked_scores(query_part, key_part, length)
    row_max = jnp.max(scores, axis=-1, keepdims=True)
    exponent = jnp.exp(scores - row_max)
    row_total = jnp.sum(exponent, axis=-1, keepdims=True)
    low_probs = (exponent / row_total).astype(jnp.bfloat16)
    context = jnp.einsum("hqk,khe->qhe", low_probs, value_part, preferred_element_type=jnp.float32)
    logsum = row_max + jnp.log(row_total)
    return (context.astype(jnp.bfloat16), logsum[:, :, 0])


def attend_backward(packed_seq, length, logsum, d_context):
    query_part, key_part, value_part = split_packed(packed_seq)
    scores = masked_scores(query_part, key_part, length)
    attn_probs = jnp.exp(scores - logsum[:, :, None])
    low_probs = attn_probs.astype(jnp.bfloat16)
    d_values = jnp.einsum("hqk,qhe->khe", low_probs, d_context, preferred_element_type=jnp.float32)
    d_probs = jnp.einsum("qhe,khe->hqk", d_context, value_part, preferred_element_type=jnp.float32)
    row_dot = jnp.sum(attn_probs * d_probs, axis=-1, keepdims=True)
    d_raw = (attn_probs * (d_probs - row_dot) * 0.125).astype(jnp.bfloat16)
    d_query = jnp.einsum("hqk,khe->qhe", d_raw, key_part, preferred_element_type=jnp.float32)
    d_keys = jnp.einsum("hqk,qhe->khe", d_raw, query_part, preferred_element_type=jnp.float32)
    return jnp.concatenate([d_query, d_keys, d_values], axis=-1).astype(jnp.bfloat16)


def local(
    tokens,
    lengths,
    qkv_weight,
    qv_bias,
    out_weight,
    out_bias,
    norm1_gain,
    norm1_shift,
    up_weight,
    up_bias,
    down_weight,
    down_bias,
    norm2_gain,
    norm2_shift,
    cotangent,
):
    groups, quarter, model_width = tokens.shape
    row_count = groups * quarter
    token_rows = tokens.reshape(row_count, model_width)
    zero_bias = jnp.zeros((H, HD), jnp.float32)
    bias_cols = jnp.stack([qv_bias[0].reshape(H, HD), zero_bias, qv_bias[1].reshape(H, HD)], axis=1)
    packed = jnp.dot(token_rows, qkv_weight, preferred_element_type=jnp.float32)
    packed = (packed + bias_cols.reshape(3 * model_width)).astype(jnp.bfloat16)
    packed = packed.reshape(groups, quarter, H, 3 * HD)
    head_parts = lax.all_to_all(packed, "narrow", split_axis=2, concat_axis=1, tiled=True)
    context, logsum = lax.map(lambda member: attend(member[0], member[1]), (head_parts, lengths))
    context_rows = lax.all_to_all(
        context, "narrow", split_axis=1, concat_axis=2, tiled=True
    ).reshape(row_count, model_width)
    attended = jnp.dot(context_rows, out_weight, preferred_element_type=jnp.float32) + out_bias
    first_norm, normed1, scale1 = norm_forward(
        token_rows.astype(jnp.float32) + attended, norm1_gain, norm1_shift
    )
    first_low = first_norm.astype(jnp.bfloat16)
    pre_act = jnp.dot(first_low, up_weight, preferred_element_type=jnp.float32) + up_bias
    erf_part = lax.erf(pre_act * root_half)
    activated = (0.5 * pre_act * (1.0 + erf_part)).astype(jnp.bfloat16)
    ffn_out = jnp.dot(activated, down_weight, preferred_element_type=jnp.float32) + down_bias
    result, normed2, scale2 = norm_forward(first_norm + ffn_out, norm2_gain, norm2_shift)
    output = result.astype(jnp.bfloat16).reshape(groups, quarter, model_width)
    positions = lax.axis_index("narrow") * quarter + lax.iota(jnp.int32, quarter)
    row_live = positions[None, :] < lengths[:, None]
    d_out = jnp.where(row_live[:, :, None], cotangent.astype(jnp.float32), 0.0).reshape(
        row_count, model_width
    )
    d_second, norm2_gain_grad, norm2_shift_grad = norm_backward(d_out, normed2, scale2, norm2_gain)
    d_ffn = d_second.astype(jnp.bfloat16)
    down_weight_grad = jnp.einsum("rf,rd->fd", activated, d_ffn, preferred_element_type=jnp.float32)
    down_bias_grad = jnp.sum(d_ffn.astype(jnp.float32), axis=0)
    d_activated = jnp.einsum("rd,fd->rf", d_ffn, down_weight, preferred_element_type=jnp.float32)
    slope = 0.5 * (1.0 + erf_part) + pre_act * jnp.exp(-0.5 * pre_act * pre_act) * inv_root_two_pi
    d_pre = (d_activated * slope).astype(jnp.bfloat16)
    up_weight_grad = jnp.einsum("rd,rf->df", first_low, d_pre, preferred_element_type=jnp.float32)
    up_bias_grad = jnp.sum(d_pre.astype(jnp.float32), axis=0)
    d_first = d_second + jnp.einsum(
        "rf,df->rd", d_pre, up_weight, preferred_element_type=jnp.float32
    )
    d_sum1, norm1_gain_grad, norm1_shift_grad = norm_backward(d_first, normed1, scale1, norm1_gain)
    d_att = d_sum1.astype(jnp.bfloat16)
    out_weight_grad = jnp.einsum(
        "rd,re->de", context_rows, d_att, preferred_element_type=jnp.float32
    )
    out_bias_grad = jnp.sum(d_att.astype(jnp.float32), axis=0)
    d_context = jnp.einsum("re,de->rd", d_att, out_weight, preferred_element_type=jnp.float32)
    d_context = d_context.astype(jnp.bfloat16).reshape(groups, quarter, H, HD)
    d_heads = lax.all_to_all(d_context, "narrow", split_axis=2, concat_axis=1, tiled=True)
    d_packed = lax.map(
        lambda member: attend_backward(member[0], member[1], member[2], member[3]),
        (head_parts, lengths, logsum, d_heads),
    )
    d_packed = lax.all_to_all(d_packed, "narrow", split_axis=1, concat_axis=2, tiled=True).reshape(
        row_count, 3 * model_width
    )
    qkv_weight_grad = jnp.einsum(
        "rd,rc->dc", token_rows, d_packed, preferred_element_type=jnp.float32
    )
    column_sums = jnp.sum(d_packed.astype(jnp.float32), axis=0).reshape(H, 3, HD)
    qv_bias_grad = jnp.stack(
        [column_sums[:, 0].reshape(model_width), column_sums[:, 2].reshape(model_width)]
    )
    d_input = d_sum1 + jnp.einsum(
        "rc,dc->rd", d_packed, qkv_weight, preferred_element_type=jnp.float32
    )
    input_grad = d_input.astype(jnp.bfloat16).reshape(groups, quarter, model_width)
    every_share = (
        lax.psum_scatter(qkv_weight_grad, "narrow", scatter_dimension=0, tiled=True),
        lax.psum_scatter(qv_bias_grad, "narrow", scatter_dimension=1, tiled=True),
        lax.psum_scatter(out_weight_grad, "narrow", scatter_dimension=0, tiled=True),
        lax.psum_scatter(out_bias_grad, "narrow", scatter_dimension=0, tiled=True),
        lax.psum_scatter(norm1_gain_grad, "narrow", scatter_dimension=0, tiled=True),
        lax.psum_scatter(norm1_shift_grad, "narrow", scatter_dimension=0, tiled=True),
        lax.psum_scatter(up_weight_grad, "narrow", scatter_dimension=0, tiled=True),
        lax.psum_scatter(up_bias_grad, "narrow", scatter_dimension=0, tiled=True),
        lax.psum_scatter(down_weight_grad, "narrow", scatter_dimension=0, tiled=True),
        lax.psum_scatter(down_bias_grad, "narrow", scatter_dimension=0, tiled=True),
        lax.psum_scatter(norm2_gain_grad, "narrow", scatter_dimension=0, tiled=True),
        lax.psum_scatter(norm2_shift_grad, "narrow", scatter_dimension=0, tiled=True),
    )
    every_total = lax.psum(
        (
            every_share[0],
            every_share[1],
            every_share[2],
            every_share[3],
            every_share[4],
            every_share[5],
            every_share[6],
            every_share[7],
            every_share[8],
            every_share[9],
            every_share[10],
            every_share[11],
        ),
        "wide",
    )
    return (
        output,
        input_grad,
        every_total[0],
        every_total[1],
        every_total[2],
        every_total[3],
        every_total[4],
        every_total[5],
        every_total[6],
        every_total[7],
        every_total[8],
        every_total[9],
        every_total[10],
        every_total[11],
    )


def solution(mesh):
    return jax.shard_map(
        local,
        mesh=mesh,
        in_specs=(
            P("wide", "narrow", None),
            P("wide"),
            P(),
            P(),
            P(),
            P(),
            P(),
            P(),
            P(),
            P(),
            P(),
            P(),
            P(),
            P(),
            P("wide", "narrow", None),
        ),
        out_specs=(
            P("wide", "narrow", None),
            P("wide", "narrow", None),
            P("narrow", None),
            P(None, "narrow"),
            P("narrow", None),
            P("narrow"),
            P("narrow"),
            P("narrow"),
            P("narrow", None),
            P("narrow"),
            P("narrow", None),
            P("narrow"),
            P("narrow"),
            P("narrow"),
        ),
        check_vma=False,
    )
```

profile of v0, /device:TPU:0, one launch (start us, length us, event | category | flops | bytes accessed | tf_op | source)
XLA Modules:
  0.0 858.5 jit_solution(15880051272732677894)
XLA Ops:
  30.0 22.8 %all-to-all-done = bf16[3,128,12,192]{1,3,0,2:T(8,128)(2,1)} async-done(((bf16[3,128,12,192]{1,3,0,2:T(8,128)(2,1)}), bf16[3,128,12,192]{1,3,0,2:T(8,128)(2,1)}, u32[]{:S(2)}, u32[]{:S(2)}) %all-to-all-start) | async-done | bytes 1769504 | tf_op jit(solution)/shard_map/all_to_all | solution.py:99
  60.9 18.2 %while.22 = (s32[]{:T(128)}, bf16[3,512,3,64]{1,3,2,0:T(8,128)(2,1)}, f32[3,3,512]{2,1,0:T(4,128)}, bf16[3,512,3,192]{1,3,2,0:T(8,128)(2,1)}, s32[3]{0:T(128)S(1)}, /*index=5*/s32[]{:T(128)}) while((s32[]{:T(128)}, bf16[3,512,3,64]{1,3,2,0:T(8,128)(2,1)}, f32[3,3,512]{2,1,0:T(4,128)}, bf16[3,512,3,192]{1,3,2,0:T(8,128)(2,1)}, s32[3]{0:T(128)S(1)}, ...), condition=%wide.region_3.4_spmd, body=%wide.region_0.3_spmd.sunk | while | flops 210861056 | bytes 11460713 | solution.py:100
  142.4 9.3 %all-to-all-done.2 = bf16[3,128,12,64]{1,3,0,2:T(8,128)(2,1)} async-done(((bf16[3,128,12,64]{1,3,0,2:T(8,128)(2,1)}), bf16[3,128,12,64]{1,3,0,2:T(8,128)(2,1)}, u32[]{:S(2)}, u32[]{:S(2)}) %all-to-all-start.2) | async-done | bytes 589856 | tf_op jit(solution)/shard_map/all_to_all | solution.py:140
  156.4 71.6 %while.23 = (s32[]{:T(128)}, bf16[3,512,3,192]{1,3,2,0:T(8,128)(2,1)}, bf16[3,512,3,192]{1,3,2,0:T(8,128)(2,1)}, s32[3]{0:T(128)}, f32[3,3,512]{2,1,0:T(4,128)}, /*index=5*/bf16[3,512,3,64]{1,3,2,0:T(8,128)(2,1)}, s32[]{:T(128)}) while((s32[]{:T(128)}, bf16[3,512,3,192]{1,3,2,0:T(8,128)(2,1)}, bf16[3,512,3,192]{1,3,2,0:T(8,128)(2,1)}, ...), condition=%wide.region_14.15_spmd, body=%wide.region_12.14_spmd.sunk | while | flops 516395520 | bytes 56251596 | solution.py:141
  165.4 6.4 fusion.147
  171.9 6.4 fusion.146
  189.3 6.4 fusion.147
  195.7 6.4 fusion.146
  213.1 6.4 fusion.147
  219.6 6.4 fusion.146
  233.5 42.2 %all_to_all.66 = bf16[3,512,3,192]{3,2,0,1:T(4,128)(2,1)} all-to-all(bf16[3,512,3,192]{3,2,0,1:T(4,128)(2,1)} %copy.77), channel_id=1, replica_groups=mesh['wide'=8,'narrow'=4] {'narrow'}, dimensions={1} | all-to-all | bytes 3538944 | tf_op jit(solution)/shard_map/all_to_all | solution.py:145
  275.7 7.2 copy.78
  282.9 6.7 convolution_bitcast_fusion
  289.6 8.0 copy.90
  301.5 9.9 %fusion.93 = f32[768,3072]{1,0:T(8,128)} fusion(bf16[384,3072]{1,0:T(8,128)(2,1)} %copy-done.10, f32[384,768]{1,0:T(8,128)} %copy-done.5, f32[768]{0:T(1024)S(1)} %copy-done.13, f32[768]{0:T(1024)S(1)} %copy-done.12, f32[384]{0:T(512)S(1)} %add_rsqrt_fusion.1, f32[384]{0:T(512)S(1)} %broadcast_multiply_fusion.4), kind=kOutput, calls=%fused_computation.130 | convolution fusion | flops 1813413888 | bytes 12985344 | tf_op jit(solution)/shard_map/rd,rf->df/dot_general | solution.py:127
  311.7 8.5 fusion.90
  320.4 7.5 convert_reduce_fusion.1
  331.8 30.8 %reduce-scatter.16.cloned.1.call-done = f32[192,2304]{1,0:T(8,128)} async-done(((f32[768,2304]{1,0:T(8,128)}), f32[192,2304]{1,0:T(8,128)}) %reduce-scatter.16.cloned.1.call-update) | async-done | bytes 1769488
  365.6 32.9 %reduce-scatter.10.cloned.1.call-done = f32[192,768]{1,0:T(8,128)} async-done(((f32[768,768]{1,0:T(8,128)}), f32[192,768]{1,0:T(8,128)}) %reduce-scatter.10.cloned.1.call-update) | async-done | bytes 589840 | tf_op jit(solution)/shard_map/reduce_scatter | solution.py:162
  398.4 81.1 %reduce-scatter.12.cloned.1.call-done = f32[192,3072]{1,0:T(8,128)} async-done(((f32[768,3072]{1,0:T(8,128)}), f32[192,3072]{1,0:T(8,128)}) %reduce-scatter.12.cloned.1.call-update) | async-done | bytes 2359312 | tf_op jit(solution)/shard_map/reduce_scatter | solution.py:166
  479.5 80.9 %reduce-scatter.14.cloned.1.call-done = f32[768,768]{1,0:T(8,128)} async-done(((f32[3072,768]{1,0:T(8,128)}), f32[768,768]{1,0:T(8,128)}) %reduce-scatter.14.cloned.1.call-update) | async-done | bytes 2359312 | tf_op jit(solution)/shard_map/reduce_scatter | solution.py:168
  563.0 11.1 %all-reduce.9 = (f32[768]{0:T(1024)}, f32[768]{0:T(1024)}, f32[768]{0:T(1024)}, f32[3072]{0:T(1024)}, f32[768]{0:T(1024)}, /*index=5*/f32[768]{0:T(1024)}, f32[768]{0:T(1024)}) all-reduce(f32[768]{0:T(1024)S(1)} %copy-done.19, f32[768]{0:T(1024)} %get-tuple-element.135, ...), channel_id=5, replica_groups=mesh['wide'=8,'narrow'=4] {'narrow'}, use_global_device_ids=true, to_apply=%region_23.24.clone | all-reduce | flops 7680 | bytes 61440
  587.0 38.8 %all-reduce.7 = (f32[2,192]{1,0:T(2,128)}, f32[192]{0:T(256)}, f32[192]{0:T(256)}, f32[192]{0:T(256)}, f32[768]{0:T(1024)}, /*index=5*/f32[192]{0:T(256)}, f32[192]{0:T(256)}, f32[192]{0:T(256)}) all-reduce(f32[2,192]{1,0:T(2,128)S(1)} %copy.93, f32[192]{0:T(256)S(1)} %dynamic-slice.1, ...), channel_id=1, replica_groups=mesh['wide'=8,'narrow'=4] {'wide'}, use_global_device_ids=true, to_apply=%region_19.20 | all-reduce | flops 2304 | bytes 18432 | tf_op jit(solution)/shard_map/psum | solution.py:173
  625.8 215.7 %all-reduce.12.cloned.1.call-done = (f32[192,2304]{0,1:T(8,128)}, f32[192,768]{1,0:T(8,128)}, f32[192,3072]{1,0:T(8,128)}, f32[768,768]{1,0:T(8,128)}) async-done(((f32[192,2304]{0,1:T(8,128)}, f32[192,768]{1,0:T(8,128)}, f32[192,3072]{1,0:T(8,128)}, f32[768,768]{1,0:T(8,128)}), (f32[192,2304]{0,1:T(8,128)}, f32[192,768]{1,0:T(8,128)}, f32[192,3072]{1,0:T(8,128)}, ...) | async-done | bytes 7077904 | tf_op jit(solution)/shard_map/psum | solution.py:173
  (203 shorter events, 190.1 us)
Async XLA Ops:
  7.2 3.9 copy-start
  25.4 4.6 copy-start.25
  25.4 27.4 %all-to-all-start = ((bf16[3,128,12,192]{1,3,0,2:T(8,128)(2,1)}), bf16[3,128,12,192]{1,3,0,2:T(8,128)(2,1)}, u32[]{:S(2)}, u32[]{:S(2)}) async-start(bf16[3,128,12,192]{1,3,0,2:T(8,128)(2,1)} %copy.68), calls=%async_computation | async-start | bytes 3538944 | tf_op jit(solution)/shard_map/all_to_all | solution.py:99
  82.5 8.2 copy-start.14
  86.4 13.9 %all-to-all-start.1 = ((bf16[4,2,36864]{2,1,0:T(2,128)(2,1)}), bf16[4,2,36864]{2,1,0:T(2,128)(2,1)}, u32[]{:S(2)}, u32[]{:S(2)}) async-start(bf16[4,2,36864]{2,1,0:T(2,128)(2,1)} %reshape.255), calls=%async_computation.1 | async-start | bytes 1179648 | tf_op jit(solution)/shard_map/all_to_all | solution.py:101
  94.3 14.0 %copy-start.23 = (f32[768]{0:T(1024)S(1)}, f32[768]{0:T(1024)}, u32[]{:S(2)}) copy-start(f32[768]{0:T(1024)} %param.24) | copy-start | bytes 9220
  108.3 7.3 slice-start
  110.8 18.2 %copy-start.5 = (f32[384,768]{1,0:T(8,128)}, f32[384,768]{1,0:T(8,128)S(1)}, u32[]{:S(2)}) copy-start(f32[384,768]{1,0:T(8,128)S(1)} %get-tuple-element.195) | copy-start | bytes 3538948
  111.2 4.5 slice-start.1
  111.2 4.4 copy-start.24
  120.1 6.0 slice-start.2
  122.1 4.1 copy-start.7
  122.1 4.1 slice-start.3
  138.0 13.8 %all-to-all-start.2 = ((bf16[3,128,12,64]{1,3,0,2:T(8,128)(2,1)}), bf16[3,128,12,64]{1,3,0,2:T(8,128)(2,1)}, u32[]{:S(2)}, u32[]{:S(2)}) async-start(bf16[3,128,12,64]{1,3,0,2:T(8,128)(2,1)} %copy.74), calls=%async_computation.2 | async-start | bytes 1179648 | tf_op jit(solution)/shard_map/all_to_all | solution.py:140
  142.2 220.4 %reduce-scatter.16.cloned.1.call-start = ((), (), s32[]{:S(2)}) async-start(), calls=%async_computation.12 | async-start | bytes 8847360
  160.1 3.0 copy-start.2
  183.9 3.0 copy-start.2
  207.8 3.0 copy-start.2
  297.7 100.8 %reduce-scatter.10.cloned.1.call-start = ((), (), s32[]{:S(2)}) async-start(), calls=%async_computation.9 | async-start | bytes 2949120 | tf_op jit(solution)/shard_map/reduce_scatter | solution.py:162
  301.4 178.1 %reduce-scatter.12.cloned.1.call-start = ((), (), s32[]{:S(2)}) async-start(), calls=%async_computation.10 | async-start | bytes 11796480 | tf_op jit(solution)/shard_map/reduce_scatter | solution.py:166
  311.4 249.0 %reduce-scatter.14.cloned.1.call-start = ((), (), s32[]{:S(2)}) async-start(), calls=%async_computation.11 | async-start | bytes 11796480 | tf_op jit(solution)/shard_map/reduce_scatter | solution.py:168
  320.3 265.7 %reduce-scatter.18.cloned.1.call-start = ((), (), s32[]{:S(2)}) async-start(), calls=%async_computation.13 | async-start | bytes 491520
  331.8 509.7 %all-reduce.12.cloned.1.call-start = ((), (), s32[]{:S(2)}) async-start(), calls=%async_computation.14 | async-start | bytes 15335424 | tf_op jit(solution)/shard_map/psum | solution.py:173
  846.3 3.5 copy-start.9
  (21 other events, 44.8 us)
Sparse Core Ops, SparseCore 0:
  297.8 64.7 reduce-scatter.15
  365.3 33.0 reduce-scatter.9
  401.0 78.4 reduce-scatter.11
  482.0 78.3 reduce-scatter.13
  563.3 20.7 reduce-scatter.17
  589.1 252.3 all-reduce.11
where the time goes:
time: 867 us; the launch traced here: 858 us
  waiting for transfers between devices  480 us (55%)
  matrix products  115 us (13%)
  local copies, waits for them, and re-layouts  111 us (13%)
  blocking collectives  92.1 us (11%)
  other arithmetic  30 us (3%)
  between operations  16.2 us (2%)
  starting transfers between devices  13.7 us (2%)
    psum x1, waiting for transfers between devices, local(): lax.psum((every_share[0], every_share[1], every_share[2], every_share[3],...  216 us
    reduce_scatter x1, waiting for transfers between devices, local(): lax.psum_scatter(up_weight_grad, 'narrow', scatter_dimension=0, tiled=True)  81.1 us
    reduce_scatter x1, waiting for transfers between devices, local(): lax.psum_scatter(down_weight_grad, 'narrow', scatter_dimension=0, tiled=T...  80.9 us
    all_to_all x1, blocking collectives, local(): lax.all_to_all(d_packed, 'narrow', split_axis=1, concat_axis=2, tiled=True)  42.2 us
    unnamed x72, local copies, waits for them, and re-layouts  41.2 us
    psum x1, blocking collectives, local(): lax.psum((every_share[0], every_share[1], every_share[2], every_share[3],...  38.8 us
    reduce_scatter x1, waiting for transfers between devices, local(): lax.psum_scatter(out_weight_grad, 'narrow', scatter_dimension=0, tiled=True)  32.9 us
    unnamed x8, waiting for transfers between devices  30.9 us
  transfers between devices with their start and end apart: 9, of which 8 were waited for; matrix products, arithmetic and copies ran while one was open for 6% of the time, Pallas kernels for 0%

commit v1 on v0

v1 whole, which is shorter than its diff:
```python
import functools

import jax
import jax.numpy as jnp
from jax import lax
from jax.experimental import pallas as pl
from jax.experimental.pallas import tpu as pltpu
from jax.sharding import PartitionSpec as P

H = 12
HD = 64
PAIR = 2 * HD
epsilon = 1e-12
root_half = 0.7071067811865476
inv_root_two_pi = 0.3989422804014327
MESH = pl.DeviceIdType.MESH
F32 = jnp.float32
BF = jnp.bfloat16
V = pltpu.VMEM
DMA = pltpu.SemaphoreType.DMA
ANY = pl.ANY


def dg(a, b, ca, cb):
    return lax.dot_general(a, b, (((ca,), (cb,)), ((), ())), preferred_element_type=F32)


def copy_to(src, dst, ss, rs, dev):
    return pltpu.make_async_remote_copy(
        src_ref=src, dst_ref=dst, send_sem=ss, recv_sem=rs, device_id=dev, device_id_type=MESH)


def left_lanes(rows):
    return lax.broadcasted_iota(jnp.int32, (rows, PAIR), 1) < HD


def stack_heads(x):
    left = left_lanes(x.shape[0])
    zero = jnp.zeros_like(x)
    return jnp.concatenate([jnp.where(left, x, zero), jnp.where(left, zero, x)], axis=0)


def unstack_heads(x_t):
    q = x_t.shape[1] // 2
    top = lax.broadcasted_iota(jnp.int32, (PAIR, q), 0) < HD
    return jnp.where(top, x_t[:, :q], x_t[:, q:]).T


def forward_kernel(len_ref, tok_ref, w_hbm, b_ref,
                   ctx_ref, toks_hbm, q_hbm, k_hbm, v_hbm, p_hbm, wp_hbm,
                   w, wp, toks, q, k, v, pr,
                   w_sem, cs, cr, ys, yr, fs, fr, o_sem):
    seqs, quarter, d = tok_ref.shape
    pairs = d // PAIR
    wide, n = lax.axis_index("wide"), lax.axis_index("narrow")
    c, y = n % 2, n // 2
    core_n, y_n = n + 1 - 2 * c, n + 2 - 4 * y
    core_peer, y_peer = (wide, core_n), (wide, y_n)
    w_copy = pltpu.make_async_copy(w_hbm, w, w_sem)
    w_copy.start()
    bar = pltpu.get_barrier_semaphore()
    for peer in (core_peer, y_peer):
        pl.semaphore_signal(bar, inc=1, device_id=peer, device_id_type=MESH)
    pl.semaphore_wait(bar, 2)

    def send_y(s):
        return copy_to(tok_ref.at[s], toks.at[s, n], ys.at[s], yr.at[s], y_peer)

    def send_core(s):
        return copy_to(tok_ref.at[s], toks.at[s, n], cs.at[s], cr.at[s], core_peer)

    def forward_y(s):
        return copy_to(toks.at[s, y_n], toks.at[s, y_n], fs.at[s], fr.at[s], core_peer)

    for s in range(seqs):
        send_y(s).start()
        send_core(s).start()
    for s in range(seqs):
        toks[s, n] = tok_ref[s]
    w_copy.wait()
    left = left_lanes(d)
    for p in range(pairs):
        t0, t1, t2 = (w[:, pl.ds(p * 3 * PAIR + i * PAIR, PAIR)].astype(F32) for i in range(3))
        cols = pl.ds(p * PAIR, PAIR)
        wp[0, :, cols] = jnp.where(left, t0, t1).astype(BF)
        wp[1, :, cols] = pltpu.roll(jnp.where(left, t2, t0), HD, 1).astype(BF)
        wp[2, :, cols] = jnp.where(left, t1, t2).astype(BF)
    wp_out = pltpu.make_async_copy(wp, wp_hbm, o_sem.at[0])
    wp_out.start()
    own = tok_ref[...].reshape(seqs * quarter, d)
    q[...] = ((dg(own, wp[0], 1, 0) + b_ref[0:1, :]).astype(BF) * 0.125).reshape(seqs, quarter, d)
    q_out = pltpu.make_async_copy(q, q_hbm, o_sem.at[1])
    q_out.start()

    def project(s, half):
        blocks = pl.ds(2 * half, 2)
        rows = toks[s, blocks].reshape(2 * quarter, d)
        k[s, blocks] = dg(rows, wp[1], 1, 0).astype(BF).reshape(2, quarter, d)
        v[s, blocks] = (dg(rows, wp[2], 1, 0) + b_ref[1:2, :]).astype(BF).reshape(2, quarter, d)

    for s in range(seqs):
        send_core(s).wait_recv()
    for s in range(seqs):
        project(s, y)

    def fetch_far(s):
        copy_to(toks.at[s, y_n], toks.at[s, y_n], ys.at[s], yr.at[s], y_peer).wait_recv()
        forward_y(s).start()

    outs = []
    fetch_far(0)
    for s in range(seqs):
        far = core_n + 2 - 4 * y
        copy_to(toks.at[s, far], toks.at[s, far], fs.at[s], fr.at[s], core_peer).wait_recv()
        project(s, 1 - y)
        if s + 1 < seqs:
            fetch_far(s + 1)
        for i, (src, dst) in enumerate(((toks, toks_hbm), (k, k_hbm), (v, v_hbm))):
            cp = pltpu.make_async_copy(src.at[s], dst.at[s], o_sem.at[2 + 4 * s + i])
            cp.start()
            outs.append(cp)
        keys = 4 * quarter
        live = lax.broadcasted_iota(jnp.int32, (keys, 2 * quarter), 0) < len_ref[s]

        def unit(p, carry):
            cols = pl.ds(pl.multiple_of(p * PAIR, PAIR), PAIR)
            qs = stack_heads(q[s, :, cols])
            kp = k[s, :, :, cols].reshape(keys, PAIR)
            vp = v[s, :, :, cols].reshape(keys, PAIR)
            scores = jnp.where(live, dg(kp, qs, 1, 1), -1000000000.0)
            e = jnp.exp(scores - jnp.max(scores, axis=0, keepdims=True))
            probs = (e * (1.0 / jnp.sum(e, axis=0, keepdims=True))).astype(BF)
            pr[s, p] = probs
            ctx_ref[s, :, cols] = unstack_heads(dg(vp, probs, 0, 0)).astype(BF)
            return carry

        lax.fori_loop(0, pairs, unit, 0)
        cp = pltpu.make_async_copy(pr.at[s], p_hbm.at[s], o_sem.at[2 + 4 * s + 3])
        cp.start()
        outs.append(cp)
    for s in range(seqs):
        send_y(s).wait_send()
        send_core(s).wait_send()
        forward_y(s).wait_send()
    for cp in [wp_out, q_out] + outs:
        cp.wait()


def attention_forward(tokens, lengths, qkv_weight, qv_bias):
    seqs, quarter, d = tokens.shape
    S = jax.ShapeDtypeStruct
    keys = (seqs, 4, quarter, d)
    pairs = d // PAIR
    shapes = [S((seqs, quarter, d), BF), S(keys, BF), S((seqs, quarter, d), BF), S(keys, BF), S(keys, BF),
              S((seqs, pairs, 4 * quarter, 2 * quarter), BF), S((3, d, d), BF)]
    return pl.pallas_call(
        forward_kernel,
        out_shape=shapes,
        in_specs=[pl.BlockSpec(memory_space=pltpu.SMEM), pl.BlockSpec(memory_space=V),
                  pl.BlockSpec(memory_space=ANY), pl.BlockSpec(memory_space=V)],
        out_specs=[pl.BlockSpec(memory_space=V)] + [pl.BlockSpec(memory_space=ANY)] * 6,
        scratch_shapes=[V(qkv_weight.shape, BF), V((3, d, d), BF), V(keys, BF), V((seqs, quarter, d), BF),
                        V(keys, BF), V(keys, BF), V(shapes[5].shape, BF), DMA]
        + [DMA((seqs,))] * 6 + [DMA((2 + 4 * seqs,))],
        name="attention_forward",
        compiler_params=pltpu.CompilerParams(collective_id=1, has_side_effects=True, vmem_limit_bytes=40 << 20),
    )(lengths, tokens, qkv_weight, qv_bias)


def fold(x):
    return jnp.sum(x.reshape(x.shape[0] // 8, 8, x.shape[1]), axis=0)


def rows_kernel(len_ref, tok_ref, cot_ref, ctx_ref, wo_hbm, bo_ref, g1_ref, s1_ref, wu_hbm, bu_ref, wd_hbm, bd_ref,
                g2_ref, s2_ref,
                out_ref, dsum_ref, dctx_ref, first_ref, act_ref, dpre_ref, dffn_ref, datt_ref, sums_ref,
                wo, wu, wd, val, first, normed1, scale1, slope, dsec, part, part_up, sem):
    rows, d = tok_ref.shape
    ff = wu.shape[1]
    quarter = rows // len_ref.shape[0]
    base = lax.axis_index("narrow") * quarter
    loads = [pltpu.make_async_copy(s, t, sem.at[i])
             for i, (s, t) in enumerate(((wo_hbm, wo), (wu_hbm, wu), (wd_hbm, wd)))]
    for cp in loads:
        cp.start()
    part[...] = jnp.zeros_like(part)
    chunk = 64
    chunks = rows // chunk
    loads[0].wait()
    for b in range(d // 256):
        cols = pl.ds(b * 256, 256)
        val[:, cols] = dg(ctx_ref[...], wo[:, cols], 1, 0) + bo_ref[:, cols] + tok_ref[:, cols].astype(F32)

    def norm1(i, carry):
        r = pl.ds(pl.multiple_of(i * chunk, chunk), chunk)
        v = val[r]
        center = v - jnp.mean(v, axis=-1, keepdims=True)
        scale = lax.rsqrt(jnp.mean(center * center, axis=-1, keepdims=True) + epsilon)
        normed = center * scale
        x = normed * g1_ref[...] + s1_ref[...]
        normed1[r] = normed
        scale1[r] = jnp.broadcast_to(scale, (chunk, 128))
        first[r] = x
        first_ref[r] = x.astype(BF)
        return carry

    lax.fori_loop(0, chunks, norm1, 0)
    loads[1].wait()

    def up(j, carry):
        cols = pl.ds(pl.multiple_of(j * 256, 256), 256)
        pre = dg(first_ref[...], wu[:, cols], 1, 0) + bu_ref[:, cols]
        half = 0.5 + 0.5 * lax.erf(pre * root_half)
        act_ref[:, cols] = (pre * half).astype(BF)
        slope[:, cols] = half + pre * (jnp.exp(-0.5 * pre * pre) * inv_root_two_pi)
        return carry

    lax.fori_loop(0, ff // 256, up, 0)
    loads[2].wait()
    for b in range(d // 256):
        cols = pl.ds(b * 256, 256)
        val[:, cols] = dg(act_ref[...], wd[:, cols], 1, 0) + bd_ref[:, cols] + first[:, cols]

    def norm2(i, carry):
        r = pl.ds(pl.multiple_of(i * chunk, chunk), chunk)
        v = val[r]
        center = v - jnp.mean(v, axis=-1, keepdims=True)
        scale = lax.rsqrt(jnp.mean(center * center, axis=-1, keepdims=True) + epsilon)
        normed = center * scale
        out_ref[r] = (normed * g2_ref[...] + s2_ref[...]).astype(BF)
        s = i * chunk // quarter
        pos = base + i * chunk - s * quarter + lax.broadcasted_iota(jnp.int32, (chunk, d), 0)
        d_out = jnp.where(pos < len_ref[s], cot_ref[r].astype(F32), 0.0)
        part[1] += fold(d_out * normed)
        part[2] += fold(d_out)
        g = d_out * g2_ref[...]
        inner = g - jnp.mean(g, axis=-1, keepdims=True) - normed * jnp.mean(g * normed, axis=-1, keepdims=True)
        d_second = scale * inner
        dsec[r] = d_second
        low = d_second.astype(BF)
        dffn_ref[r] = low
        part[0] += fold(low.astype(F32))
        return carry

    lax.fori_loop(0, chunks, norm2, 0)

    def up_back(j, carry):
        cols = pl.ds(pl.multiple_of(j * 256, 256), 256)
        low = (dg(dffn_ref[...], wd[cols, :], 1, 1) * slope[:, cols]).astype(BF)
        dpre_ref[:, cols] = low
        part_up[:, cols] = fold(low.astype(F32))
        return carry

    lax.fori_loop(0, ff // 256, up_back, 0)
    for b in range(d // 256):
        cols = pl.ds(b * 256, 256)
        val[:, cols] = dsec[:, cols] + dg(dpre_ref[...], wu[cols, :], 1, 1)

    def norm1_back(i, carry):
        r = pl.ds(pl.multiple_of(i * chunk, chunk), chunk)
        d_first, normed = val[r], normed1[r]
        part[4] += fold(d_first * normed)
        part[5] += fold(d_first)
        g = d_first * g1_ref[...]
        inner = g - jnp.mean(g, axis=-1, keepdims=True) - normed * jnp.mean(g * normed, axis=-1, keepdims=True)
        d_sum = scale1[r, :1] * inner
        dsum_ref[r] = d_sum
        low = d_sum.astype(BF)
        datt_ref[r] = low
        part[3] += fold(low.astype(F32))
        return carry

    lax.fori_loop(0, chunks, norm1_back, 0)
    dctx_ref[...] = dg(datt_ref[...], wo[...], 1, 1).astype(BF)
    total = lambda x: jnp.sum(x, axis=0, keepdims=True)
    ups = ff // d
    sums_ref[0:1] = total(part[3])
    sums_ref[1:2] = total(part[4])
    sums_ref[2:3] = total(part[5])
    for i in range(ups):
        sums_ref[3 + i:4 + i] = total(part_up[:, i * d:(i + 1) * d])
    sums_ref[3 + ups:4 + ups] = total(part[0])
    sums_ref[4 + ups:5 + ups] = total(part[1])
    sums_ref[5 + ups:6 + ups] = total(part[2])


def rows_part(tok, cot, ctx, lengths, wo, bo, g1, s1, wu, bu, wd, bd, g2, s2):
    rows, d = tok.shape
    ff = wu.shape[1]
    S = jax.ShapeDtypeStruct
    row = lambda a: a.reshape(1, -1)
    vm, hbm = pl.BlockSpec(memory_space=V), pl.BlockSpec(memory_space=ANY)
    return pl.pallas_call(
        rows_kernel,
        out_shape=[S((rows, d), BF), S((rows, d), F32), S((rows, d), BF), S((rows, d), BF), S((rows, ff), BF),
                   S((rows, ff), BF), S((rows, d), BF), S((rows, d), BF), S((6 + ff // d, d), F32)],
        in_specs=[pl.BlockSpec(memory_space=pltpu.SMEM), vm, vm, vm, hbm, vm, vm, vm, hbm, vm, hbm, vm, vm, vm],
        out_specs=[vm] * 9,
        scratch_shapes=[V(wo.shape, BF), V(wu.shape, BF), V(wd.shape, BF), V((rows, d), F32), V((rows, d), F32),
                        V((rows, d), F32), V((rows, 128), F32), V((rows, ff), F32), V((rows, d), F32),
                        V((6, 8, d), F32), V((8, ff), F32), DMA((3,))],
        name="rows_part",
        compiler_params=pltpu.CompilerParams(vmem_limit_bytes=48 << 20),
    )(lengths, tok, cot, ctx, wo, row(bo), row(g1), row(s1), wu, row(bu), wd, row(bd), row(g2), row(s2))


def backward_kernel(dctx_ref, dsum_ref, toks_ref, q_ref, k_ref, v_ref, p_ref, wp_ref,
                    dtok_ref, dinp_ref, gq_ref, sums_ref, dq, dk, dv):
    seqs, quarter, d = q_ref.shape
    pairs = d // PAIR
    keys = 4 * quarter
    for s in range(seqs):
        def unit(p, carry):
            cols = pl.ds(pl.multiple_of(p * PAIR, PAIR), PAIR)
            qs = stack_heads(q_ref[s, :, cols])
            ds = stack_heads(dctx_ref[s, :, cols])
            kp = k_ref[s, :, :, cols].reshape(keys, PAIR)
            vp = v_ref[s, :, :, cols].reshape(keys, PAIR)
            low = p_ref[s, p]
            probs = low.astype(F32)
            d_probs = dg(vp, ds, 1, 1)
            t = probs * d_probs
            d_raw = (t - probs * jnp.sum(t, axis=0, keepdims=True)).astype(BF)
            dv[s, :, cols] = dg(low, ds, 1, 0).astype(BF)
            dk[s, :, cols] = dg(d_raw, qs, 1, 0).astype(BF)
            dq[s, :, cols] = (unstack_heads(dg(kp, d_raw, 0, 0)) * 0.125).astype(BF)
            return carry

        lax.fori_loop(0, pairs, unit, 0)
        dtok = dg(dk[s], wp_ref[1], 1, 1) + dg(dv[s], wp_ref[2], 1, 1)
        dtok_ref[:, s] = dtok.astype(BF).reshape(4, quarter, d)
    dq_all = dq[...].reshape(seqs * quarter, d)
    dinp_ref[...] = dsum_ref[...] + dg(dq_all, wp_ref[0], 1, 1)
    sums_ref[0:1] = jnp.sum(fold(dq_all.astype(F32)), axis=0, keepdims=True)
    total = jnp.zeros((8, d), F32)
    for s in range(seqs):
        total = total + fold(dv[s].astype(F32))
    sums_ref[1:2] = jnp.sum(total, axis=0, keepdims=True)


def qkv_grad_piece(i, tok_ref, toks_ref, dq, dk, dv, store):
    seqs, quarter, d = tok_ref.shape
    cols = pl.ds(i * 2 * PAIR, 2 * PAIR)
    rows = 4 * quarter
    a = dg(tok_ref[...].reshape(seqs * quarter, d), dq[:, :, cols].reshape(seqs * quarter, 2 * PAIR), 0, 0)
    allt = toks_ref[...].reshape(seqs * rows, d)
    b = dg(allt, dk[:, :, cols].reshape(seqs * rows, 2 * PAIR), 0, 0)
    cgrad = dg(allt, dv[:, :, cols].reshape(seqs * rows, 2 * PAIR), 0, 0)
    left = left_lanes(d)
    for j in range(2):
        sl = slice(j * PAIR, (j + 1) * PAIR)
        aj, bj, cj = a[:, sl], pltpu.roll(b[:, sl], HD, 1), cgrad[:, sl]
        store(3 * j, jnp.where(left, aj, bj))
        store(3 * j + 1, jnp.where(left, cj, aj))
        store(3 * j + 2, jnp.where(left, bj, cj))


def attention_backward(dctx, dsum, toks, q, k, v, probs, wp, tok):
    seqs, quarter, d = q.shape
    S = jax.ShapeDtypeStruct
    vm = pl.BlockSpec(memory_space=V)

    def kernel(dctx_ref, dsum_ref, toks_ref, q_ref, k_ref, v_ref, p_ref, wp_ref, tok_ref,
               dtok_ref, dinp_ref, gq_ref, sums_ref, dq, dk, dv):
        backward_kernel(dctx_ref, dsum_ref, toks_ref, q_ref, k_ref, v_ref, p_ref, wp_ref,
                        dtok_ref, dinp_ref, gq_ref, sums_ref, dq, dk, dv)
        for i in range(3):
            def store(t, x):
                gq_ref[i, :, t * PAIR:(t + 1) * PAIR] = x.astype(BF)
            qkv_grad_piece(i, tok_ref, toks_ref, dq, dk, dv, store)

    return pl.pallas_call(
        kernel,
        out_shape=[S((4, seqs, quarter, d), BF), S((seqs * quarter, d), F32), S((3, d, d), BF), S((2, d), F32)],
        in_specs=[vm] * 9,
        out_specs=[vm] * 4,
        scratch_shapes=[V((seqs, quarter, d), BF), V((seqs, 4 * quarter, d), BF), V((seqs, 4 * quarter, d), BF)],
        name="attention_backward",
        compiler_params=pltpu.CompilerParams(vmem_limit_bytes=56 << 20),
    )(dctx, dsum, toks, q, k, v, probs, wp, tok)


LAGS = (0, 1, 3, 4, 6, 7, 8)


def reduce_kernel(gd, gu, go, gq, dtok, dinp_ref, s_ref, out_hbm, din_ref, so_ref,
                  own, r1, r2, r3, r4, res, sbuf, srecv, xown, x1, x2,
                  s1, q1, s2, q2, s3, q3, s4, q4, s5, q5, s6, q6, ls, os_, ss, sq, xs):
    pieces, _, R, C = own.shape
    nd = gd.shape[2] // R
    nu = gu.shape[3] // C
    h = R // 2
    hr, hc = h // 2, C // 2
    w, n = lax.axis_index("wide"), lax.axis_index("narrow")
    c, y, x, z = n % 2, n // 2, w % 2, (w // 2) % 4
    core_peer, y_peer, x_peer = (w, n + 1 - 2 * c), (w, n + 2 - 4 * y), (w + 1 - 2 * x, n)
    zs = [z + 1 - 2 * (z % 2), z + 2 - 4 * (z // 2), 3 - z]
    z_peers = [(w + 2 * (q - z), n) for q in zs]
    bar = pltpu.get_barrier_semaphore()
    for dev in [core_peer, y_peer, x_peer] + z_peers:
        pl.semaphore_signal(bar, inc=1, device_id=dev, device_id_type=MESH)
    pl.semaphore_wait(bar, 6)

    def cut(j):
        return (pl.ds(pl.multiple_of(x * h + (j // 2) * hr, 16), hr), pl.ds(pl.multiple_of((j % 2) * hc, 128), hc))

    near = pl.ds(pl.multiple_of(x * h, 16), h)
    away = pl.ds(pl.multiple_of((1 - x) * h, 16), h)

    def c1(p, src):
        return copy_to(src, r1.at[p], s1.at[p], q1.at[p], core_peer)

    def c1_any(p):
        return c1(p, own.at[p])

    def load(p, src):
        return pltpu.make_async_copy(src, own.at[p], ls.at[p])

    def c2(p):
        return copy_to(own.at[p, 1 - y], r2.at[p], s2.at[p], q2.at[p], y_peer)

    def c3(p):
        return copy_to(own.at[p, y, away], r3.at[p], s3.at[p], q3.at[p], x_peer)

    def c4(p, d):
        rr, cc = cut(zs[d])
        return copy_to(own.at[p, y, rr, cc], r4.at[p, d], s4.at[p, d], q4.at[p, d], z_peers[d])

    def c5(p, d, j):
        rr, cc = cut(j)
        return copy_to(res.at[p, rr, cc], res.at[p, rr, cc], s5.at[p, d], q5.at[p, d], z_peers[d])

    def c6(p, rr):
        return copy_to(res.at[p, rr], res.at[p, rr], s6.at[p], q6.at[p], x_peer)

    def store(p):
        return pltpu.make_async_copy(res.at[p], out_hbm.at[p], os_.at[p])

    def st0(p):
        def go_from(view):
            c1(p, view(1 - c)).start()
            load(p, view(c)).start()

        @pl.when(p < nd)
        def down():
            go_from(lambda e: gd.at[:, e, pl.ds(p * R, R)])

        @pl.when(jnp.logical_and(p >= nd, p < nd + nu))
        def up():
            go_from(lambda e: gu.at[:, e, :, pl.ds(pl.multiple_of((p - nd) * C, C), C)])

        @pl.when(p == nd + nu)
        def out():
            go_from(lambda e: go.at[:, e])

        @pl.when(p > nd + nu)
        def qkv():
            go_from(lambda e: gq.at[p - (nd + nu + 1), :, e])

    def st1(p):
        load(p, own.at[p]).wait()
        c1_any(p).wait_recv()
        own[p] = (own[p].astype(F32) + r1[p].astype(F32)).astype(BF)
        c2(p).start()

    def st2(p):
        c2(p).wait_recv()
        own[p, y] = (own[p, y].astype(F32) + r2[p].astype(F32)).astype(BF)
        c3(p).start()

    def st3(p):
        c3(p).wait_recv()
        own[p, y, near] = (own[p, y, near].astype(F32) + r3[p].astype(F32)).astype(BF)
        for d in (1, 2, 0):
            c4(p, d).start()

    def st4(p):
        for d in range(3):
            c4(p, d).wait_recv()
        rr, cc = cut(z)
        t = own[p, y, rr, cc].astype(F32) + r4[p, 0].astype(F32) + r4[p, 1].astype(F32) + r4[p, 2].astype(F32)
        res[p, rr, cc] = t.astype(BF)
        for d in (1, 2, 0):
            c5(p, d, z).start()

    def st5(p):
        for d in range(3):
            c5(p, d, zs[d]).wait_recv()
        c6(p, near).start()

    def st6(p):
        c6(p, away).wait_recv()
        store(p).start()

    stages = [st0, st1, st2, st3, st4, st5, st6]

    cx1 = copy_to(dtok.at[:, 1 - c], x1, xs.at[0], xs.at[1], core_peer)
    cx2 = copy_to(xown.at[1 - y], x2, xs.at[2], xs.at[3], y_peer)
    cxl = pltpu.make_async_copy(dtok.at[:, c], xown, xs.at[4])
    cx1.start()
    cxl.start()

    def small(k, slot, dev):
        return copy_to(sbuf.at[k], srecv.at[slot], ss.at[slot], sq.at[slot], dev)

    sbuf[0] = s_ref[...]
    small(0, 0, core_peer).start()
    small(0, 0, core_peer).wait_recv()
    sbuf[1] = sbuf[0] + srecv[0]
    small(1, 1, y_peer).start()
    cxl.wait()
    cx1.wait_recv()

    def addx(i, carry):
        xown[i // 3, i % 3] = (xown[i // 3, i % 3].astype(F32) + x1[i // 3, i % 3].astype(F32)).astype(BF)
        return carry

    lax.fori_loop(0, 2 * xown.shape[1], addx, 0)
    cx2.start()

    def slot(t, carry):
        for k in (6, 5, 4, 3, 2, 1, 0):
            p = t - LAGS[k]

            @pl.when(jnp.logical_and(p >= 0, p < pieces))
            def run():
                stages[k](p)
        return carry

    lax.fori_loop(0, pieces + LAGS[6], slot, 0)
    cx2.wait_recv()

    def outx(i, carry):
        din_ref[i] = (dinp_ref[i] + xown[y, i].astype(F32) + x2[i].astype(F32)).astype(BF)
        return carry

    lax.fori_loop(0, xown.shape[1], outx, 0)
    small(1, 1, y_peer).wait_recv()
    sbuf[2] = sbuf[1] + srecv[1]
    small(2, 2, x_peer).start()
    small(2, 2, x_peer).wait_recv()
    sbuf[3] = sbuf[2] + srecv[2]
    for d in range(3):
        small(3, 3 + d, z_peers[d]).start()
    for d in range(3):
        small(3, 3 + d, z_peers[d]).wait_recv()
    so_ref[...] = sbuf[3] + srecv[3] + srecv[4] + srecv[5]
    small(0, 0, core_peer).wait_send()
    small(1, 1, y_peer).wait_send()
    small(2, 2, x_peer).wait_send()
    for d in range(3):
        small(3, 3 + d, z_peers[d]).wait_send()
    cx1.wait_send()
    cx2.wait_send()

    def drain(p, carry):
        c1_any(p).wait_send()
        c2(p).wait_send()
        c3(p).wait_send()
        c6(p, near).wait_send()
        store(p).wait()
        for d in range(3):
            c4(p, d).wait_send()
            c5(p, d, z).wait_send()
        return carry

    lax.fori_loop(0, pieces, drain, 0)


def reduce_all(gd, gu, go, gq, dtok, dinp, rows):
    d = go.shape[1]
    R = d // 4
    n = gd.shape[0] // d + gu.shape[1] // d + 4
    gd = gd.reshape(2, 2, -1, d)
    gu = gu.reshape(2, 2, R, -1)
    go = go.reshape(2, 2, R, d)
    gq = gq.reshape(3, 2, 2, R, d)
    xshape = (2,) + dtok.shape[1:]
    dtok = dtok.reshape((2,) + xshape)
    h = R // 2
    vm, hbm = pl.BlockSpec(memory_space=V), pl.BlockSpec(memory_space=ANY)
    S = jax.ShapeDtypeStruct
    return pl.pallas_call(
        reduce_kernel,
        out_shape=(S((n, R, d), BF), S(dinp.shape, BF), S(rows.shape, F32)),
        in_specs=[hbm] * 5 + [vm] * 2,
        out_specs=(hbm, vm, vm),
        scratch_shapes=[V((n, 2, R, d), BF), V((n, 2, R, d), BF), V((n, R, d), BF), V((n, h, d), BF),
                        V((n, 3, h // 2, d // 2), BF), V((n, R, d), BF), V((4,) + rows.shape, F32),
                        V((6,) + rows.shape, F32), V(xshape, BF), V(xshape, BF), V(xshape[1:], BF)]
        + [DMA((n,))] * 6 + [DMA((n, 3))] * 4 + [DMA((n,))] * 4 + [DMA((6,))] * 2 + [DMA((5,))],
        name="reduce_all",
        compiler_params=pltpu.CompilerParams(collective_id=2, has_side_effects=True, vmem_limit_bytes=48 << 20),
    )(gd, gu, go, gq, dtok, dinp, rows)


def local(tokens, lengths, qkv_weight, qv_bias, out_weight, out_bias, norm1_gain, norm1_shift, up_weight, up_bias,
          down_weight, down_bias, norm2_gain, norm2_shift, cotangent):
    seqs, quarter, d = tokens.shape
    rows = seqs * quarter
    ctx, toks, q, k, v, probs, wp = attention_forward(tokens, lengths, qkv_weight, qv_bias)
    ctx_rows = ctx.reshape(rows, d)
    output, dsum, dctx, first, act, dpre, dffn, datt, sums = rows_part(
        tokens.reshape(rows, d), cotangent.reshape(rows, d), ctx_rows, lengths, out_weight, out_bias,
        norm1_gain, norm1_shift, up_weight, up_bias, down_weight, down_bias, norm2_gain, norm2_shift)
    gd = dg(act, dffn, 0, 0).astype(BF)
    gu = dg(first, dpre, 0, 0).astype(BF)
    go = dg(ctx_rows, datt, 0, 0).astype(BF)
    dtok, dinp, gq, qv_sums = attention_backward(
        dctx.reshape(seqs, quarter, d), dsum, toks, q, k, v, probs, wp, tokens)
    total, input_grad, sums = reduce_all(
        gd, gu, go, gq, dtok, dinp.reshape(seqs, quarter, d), jnp.concatenate([qv_sums, sums]))
    return finish(output.reshape(seqs, quarter, d), input_grad, total, sums, down_weight.shape[0] // d)


def finish(output, input_grad, total, sums, nd):
    q, d = total.shape[1:]
    nu = nd
    wide = lax.axis_size("wide")
    total = total.astype(F32)
    if wide > 8:
        groups = [[g * 8 + i for g in range(wide // 8)] for i in range(8)]
        total = lax.psum(total, "wide", axis_index_groups=groups)
        sums = lax.psum(sums, "wide", axis_index_groups=groups)
    n = lax.axis_index("narrow")
    wide_cols = lambda a: a.transpose(1, 0, 2).reshape(q, -1)
    part = lambda r: lax.dynamic_slice_in_dim(sums[r], n * q, q, 0)
    k = 5 + nu
    return (
        output, input_grad,
        wide_cols(total[nd + nu + 1:]),
        lax.dynamic_slice_in_dim(sums[:2], n * q, q, 1),
        total[nd + nu],
        part(2), part(3), part(4),
        wide_cols(total[nd:nd + nu]),
        lax.dynamic_slice_in_dim(sums[5:k].reshape(-1), n * (nu * q), nu * q, 0),
        total[:nd].reshape(nd * q, d),
        part(k), part(k + 1), part(k + 2),
    )


def solution(mesh):
    return jax.shard_map(
        local,
        mesh=mesh,
        in_specs=(
            P("wide", "narrow", None),
            P("wide"),
            P(),
            P(),
            P(),
            P(),
            P(),
            P(),
            P(),
            P(),
            P(),
            P(),
            P(),
            P(),
            P("wide", "narrow", None),
        ),
        out_specs=(
            P("wide", "narrow", None),
            P("wide", "narrow", None),
            P("narrow", None),
            P(None, "narrow"),
            P("narrow", None),
            P("narrow"),
            P("narrow"),
            P("narrow"),
            P("narrow", None),
            P("narrow"),
            P("narrow", None),
            P("narrow"),
            P("narrow"),
            P("narrow"),
        ),
        check_vma=False,
    )
```

time: 867 us -> 250 us (0.29)
  waiting for transfers between devices: 480 us -> 0 us
  Pallas kernels: 0 us -> 213 us
  matrix products: 115 us -> 9.34 us
  blocking collectives: 92.1 us -> 0 us
  local copies, waits for them, and re-layouts: 111 us -> 22.4 us
  other arithmetic: 30 us -> 3.39 us
  between operations: 16.2 us -> 0.95 us
  starting transfers between devices: 13.7 us -> 0 us
    psum x1 -> x0, waiting for transfers between devices: 216 us -> none  [local(): lax.psum((every_share[0], every_share[1], every_share[2], every_share[3],...]
    pallas_call x0 -> x4, Pallas kernels: none -> 213 us  [the longest x1 132 us: reduce_all(): pl.pallas_call(reduce_kernel, out_shape=(S((n, R, d), BF), S(dinp.shape,...]
    reduce_scatter x3 -> x0, waiting for transfers between devices: 195 us -> none  [the longest x1 81.1 us: local(): lax.psum_scatter(up_weight_grad, 'narrow', scatter_dimension=0, tiled=True)]
    dot_general x33 -> x3, matrix products: 115 us -> 9.34 us  [dg(): lax.dot_general(a, b, (((ca,), (cb,)), ((), ())), preferred_element_type=...]
    all_to_all x1 -> x0, blocking collectives: 42.2 us -> none  [local(): lax.all_to_all(d_packed, 'narrow', split_axis=1, concat_axis=2, tiled=True)]
    psum x1 -> x0, blocking collectives: 38.8 us -> none  [local(): lax.psum((every_share[0], every_share[1], every_share[2], every_share[3],...]
    all_to_all x3 -> x0, waiting for transfers between devices: 38.2 us -> none  [the longest x1 22.8 us: local(): lax.all_to_all(packed, 'narrow', split_axis=2, concat_axis=1, tiled=True)]
    unnamed x8 -> x0, waiting for transfers between devices: 30.9 us -> none
  transfers between devices with their start and end apart: 9 -> 0, of which waited for: 8 -> 0; matrix products, arithmetic and copies ran while one was open for 6% -> 0% of each run, Pallas kernels for 0% -> 0%
where the time goes in v1:
time: 250 us; the launch traced here: 249 us
  Pallas kernels  213 us (85%)
  local copies, waits for them, and re-layouts  22.4 us (9%)
  matrix products  9.34 us (4%)
  other arithmetic  3.39 us (1%)
    pallas_call x1, Pallas kernels, reduce_all(): pl.pallas_call(reduce_kernel, out_shape=(S((n, R, d), BF), S(dinp.shape,...  132 us
    pallas_call x1, Pallas kernels, attention_forward(): pl.pallas_call(forward_kernel, out_shape=shapes, in_specs=[pl.BlockSpec(m...  29.3 us
    pallas_call x1, Pallas kernels, attention_backward(): pl.pallas_call(kernel, out_shape=[S((4, seqs, quarter, d), BF), S((seqs *...  28.5 us
    pallas_call x1, Pallas kernels, rows_part(): pl.pallas_call(rows_kernel, out_shape=[S((rows, d), BF), S((rows, d), F32...  23.2 us
    unnamed x53, local copies, waits for them, and re-layouts  13.7 us
    dot_general x3, matrix products, dg(): lax.dot_general(a, b, (((ca,), (cb,)), ((), ())), preferred_element_type=...  9.34 us

profile of v1, /device:TPU:0, one launch (start us, length us, event | category | flops | bytes accessed | tf_op | source)
XLA Modules:
  0.0 249.5 jit_solution(11747193225798435292)
XLA Ops:
  0.7 1.1 copy-done
  1.7 0.7 copy-done.13
  3.1 29.3 %attention_forward.1 = (bf16[3,128,768]{2,1,0:T(8,128)(2,1)S(1)}, bf16[3,4,128,768]{3,2,1,0:T(8,128)(2,1)S(1)}, bf16[3,128,768]{2,1,0:T(8,128)(2,1)S(1)}, bf16[3...) custom-call(s32[3]{0:T(128)S(1)} %copy-done.14, ...), custom_call_target="tpu_custom_call" | custom-call | tf_op jit(solution)/shard_map/attention_forward/pallas_call | solution.py:156
  32.5 1.8 copy-done.2
  34.3 1.4 copy-done.3
  35.7 1.4 copy-done.4
  37.0 1.4 copy-done.5
  38.5 0.8 copy-done.10
  39.4 23.2 %rows_part.1 = (bf16[384,768]{1,0:T(8,128)(2,1)}, f32[384,768]{1,0:T(8,128)S(1)}, bf16[384,768]{1,0:T(8,128)(2,1)S(1)}, bf16[384,768]{1,0:T(8,128)(2,1)S(1)}, bf...) custom-call(s32[3]{0:T(128)S(1)} %copy-done.15, ...), custom_call_target="tpu_custom_call" | custom-call | tf_op jit(solution)/shard_map/rows_part/pallas_call | solution.py:293
  62.6 1.0 copy-done.7
  63.7 0.8 copy-done.11
  64.5 28.5 %attention_backward.1 = (bf16[4,3,128,768]{3,2,1,0:T(8,128)(2,1)}, f32[384,768]{1,0:T(8,128)}, bf16[3,768,768]{2,1,0:T(8,128)(2,1)}, f32[2,768]{1,0:T(2,128)}) custom-call(bf16[3,128,768]{2,1,0:T(8,128)(2,1)} %bitcast.42, f32[384,768]{1,0:T(8,128)} %copy-done.7, bf16[3,4,128,768]{3,2,1,0:T(8,128)(2,1)} %copy-done.3, bf16[3,128,768]{2,1,0:T(8,128)(2,1)} %copy-done.10, ...), custom_call_target="tpu_custom_call" | custom-call | tf_op jit(solution)/shard_map/attention_backward/pallas_call | solution.py:372
  93.0 0.7 pad_maximum_fusion.s_ref
  93.7 4.3 %convolution_convert_fusion = bf16[768,3072]{1,0:T(8,128)(2,1)} fusion(bf16[384,768]{1,0:T(8,128)(2,1)S(1)} %get-tuple-element.41, bf16[384,3072]{1,0:T(8,128)(2,1)S(1)} %copy-done.24), kind=kOutput, calls=%fused_computation | convolution fusion | flops 1814298624 | bytes 7667712 | tf_op jit(solution)/shard_map/dot_general | solution.py:25
  98.0 4.3 %convolution_convert_fusion.1 = bf16[3072,768]{1,0:T(8,128)(2,1)} fusion(bf16[384,3072]{1,0:T(8,128)(2,1)S(1)} %copy-done.23, bf16[384,768]{1,0:T(8,128)(2,1)S(1)} %get-tuple-element.40), kind=kOutput, calls=%fused_computation.1 | convolution fusion | flops 1814298624 | bytes 7667712 | tf_op jit(solution)/shard_map/dot_general | solution.py:25
  102.2 0.8 convolution_convert_fusion.2
  103.1 0.8 copy-done.6
  103.9 132.4 %reduce_all.1 = (bf16[12,192,768]{2,1,0:T(8,128)(2,1)}, bf16[3,128,768]{2,1,0:T(8,128)(2,1)S(1)}, f32[12,768]{1,0:T(8,128)S(1)}) custom-call(bf16[2,2,768,768]{3,2,1,0:T(8,128)(2,1)} %bitcast.45, bf16[2,2,192,3072]{3,2,1,0:T(8,128)(2,1)} %bitcast.44, bf16[2,2,192,768]{3,2,1,0:T(8,128)(2,1)S(1)} %bitcast.38, bf16[3,2,2,192,768]{4,3,2,1,0:T(8,128)(2,1)} %bitcast.46, ...), custom_call_target="tpu_custom_call" | custom-call | tf_op jit(solution)/shard_map/reduce_all/pallas_call | solution.py:583
  238.2 2.7 %convert_element_type.15 = f32[12,192,768]{2,1,0:T(8,128)S(1)} convert(bf16[12,192,768]{2,1,0:T(8,128)(2,1)} %get-tuple-element.58) | non-fusion elementwise | flops 1769472 | bytes 10616832 | tf_op jit(solution)/shard_map/convert_element_type | solution.py:620
  241.1 1.7 copy.32
  242.9 1.3 copy.31
  244.2 0.9 slice_bitcast_fusion.2
  245.7 1.6 slice.51
  248.7 0.8 copy.34
  (57 shorter events, 5.0 us)
Async XLA Ops:
  0.6 1.1 copy-start
  1.7 0.7 copy-start.13
  3.1 36.2 %copy-start.17 = (f32[768]{0:T(1024)S(1)}, f32[768]{0:T(1024)}, u32[]{:S(2)}) copy-start(f32[768]{0:T(1024)} %param.20) | copy-start | bytes 9220
  3.1 36.2 %copy-start.18 = (f32[768]{0:T(1024)S(1)}, f32[768]{0:T(1024)}, u32[]{:S(2)}) copy-start(f32[768]{0:T(1024)} %param.21) | copy-start | bytes 9220
  3.1 36.2 %copy-start.19 = (f32[768]{0:T(1024)S(1)}, f32[768]{0:T(1024)}, u32[]{:S(2)}) copy-start(f32[768]{0:T(1024)} %param.22) | copy-start | bytes 9220
  3.1 36.2 %copy-start.20 = (f32[768]{0:T(1024)S(1)}, f32[768]{0:T(1024)}, u32[]{:S(2)}) copy-start(f32[768]{0:T(1024)} %param.26) | copy-start | bytes 9220
  3.1 36.3 %copy-start.21 = (f32[768]{0:T(1024)S(1)}, f32[768]{0:T(1024)}, u32[]{:S(2)}) copy-start(f32[768]{0:T(1024)} %param.27) | copy-start | bytes 9220
  3.1 36.3 %copy-start.22 = (f32[768]{0:T(1024)S(1)}, f32[768]{0:T(1024)}, u32[]{:S(2)}) copy-start(f32[768]{0:T(1024)} %param.28) | copy-start | bytes 9220
  3.1 36.3 %copy-start.1 = (bf16[3,128,768]{2,1,0:T(8,128)(2,1)S(1)}, bf16[3,128,768]{2,1,0:T(8,128)(2,1)}, u32[]{:S(2)}) copy-start(bf16[3,128,768]{2,1,0:T(8,128)(2,1)} %tok_ref.3) | copy-start | bytes 1769476
  3.1 36.3 %copy-start.9 = (bf16[3,128,768]{2,1,0:T(8,128)(2,1)S(1)}, bf16[3,128,768]{2,1,0:T(8,128)(2,1)}, u32[]{:S(2)}) copy-start(bf16[3,128,768]{2,1,0:T(8,128)(2,1)} %param.29) | copy-start | bytes 1769476
  3.1 36.3 %copy-start.12 = (f32[3072]{0:T(1024)S(1)}, f32[3072]{0:T(1024)}, u32[]{:S(2)}) copy-start(f32[3072]{0:T(1024)} %param.24) | copy-start | bytes 36868
  3.1 36.3 %copy-start.15 = (s32[3]{0:T(128)S(1)}, s32[3]{0:T(128)}, u32[]{:S(2)}) copy-start(s32[3]{0:T(128)} %len_ref.3) | copy-start | bytes 40
  32.5 1.8 copy-start.2
  34.3 1.4 copy-start.3
  35.7 1.4 copy-start.4
  37.0 1.4 copy-start.5
  38.5 0.8 copy-start.10
  62.6 1.0 copy-start.7
  63.7 0.8 copy-start.11
  64.5 29.2 %copy-start.24 = (bf16[384,3072]{1,0:T(8,128)(2,1)S(1)}, bf16[384,3072]{1,0:T(8,128)(2,1)}, u32[]{:S(2)}) copy-start(bf16[384,3072]{1,0:T(8,128)(2,1)} %get-tuple-element.42) | copy-start | bytes 7077892
  93.7 4.3 %copy-start.23 = (bf16[384,3072]{1,0:T(8,128)(2,1)S(1)}, bf16[384,3072]{1,0:T(8,128)(2,1)}, u32[]{:S(2)}) copy-start(bf16[384,3072]{1,0:T(8,128)(2,1)} %get-tuple-element.39) | copy-start | bytes 7077892
  98.0 5.1 %copy-start.8 = (f32[384,768]{1,0:T(8,128)S(1)}, f32[384,768]{1,0:T(8,128)}, u32[]{:S(2)}) copy-start(f32[384,768]{1,0:T(8,128)} %get-tuple-element.54) | copy-start | bytes 3538948
  102.2 1.7 copy-start.6
  242.9 2.9 %copy-start.16 = (bf16[12,192,768]{2,1,0:T(8,128)(2,1)S(1)}, bf16[12,192,768]{2,1,0:T(8,128)(2,1)}, u32[]{:S(2)}) copy-start(bf16[12,192,768]{2,1,0:T(8,128)(2,1)} %get-tuple-element.58) | copy-start | bytes 10616836
  (1 other events, 0.7 us)

commit v2 on v1

v2 whole, which is shorter than its diff:
```python
import functools

import jax
import jax.numpy as jnp
from jax import lax
from jax.experimental import pallas as pl
from jax.experimental.pallas import tpu as pltpu
from jax.sharding import PartitionSpec as P

H = 12
HD = 64
PAIR = 2 * HD
epsilon = 1e-12
root_half = 0.7071067811865476
inv_root_two_pi = 0.3989422804014327
MESH = pl.DeviceIdType.MESH
F32 = jnp.float32
BF = jnp.bfloat16
V = pltpu.VMEM
DMA = pltpu.SemaphoreType.DMA
ANY = pl.ANY


def dg(a, b, ca, cb):
    return lax.dot_general(a, b, (((ca,), (cb,)), ((), ())), preferred_element_type=F32)


def copy_to(src, dst, ss, rs, dev):
    return pltpu.make_async_remote_copy(
        src_ref=src, dst_ref=dst, send_sem=ss, recv_sem=rs, device_id=dev, device_id_type=MESH)


def left_lanes(rows):
    return lax.broadcasted_iota(jnp.int32, (rows, PAIR), 1) < HD


def stack_heads(x):
    left = left_lanes(x.shape[0])
    zero = jnp.zeros_like(x)
    return jnp.concatenate([jnp.where(left, x, zero), jnp.where(left, zero, x)], axis=0)


def unstack_heads(x_t):
    q = x_t.shape[1] // 2
    top = lax.broadcasted_iota(jnp.int32, (PAIR, q), 0) < HD
    return jnp.where(top, x_t[:, :q], x_t[:, q:]).T


def forward_kernel(len_ref, tok_ref, w_hbm, b_ref,
                   ctx_ref, toks_hbm, q_hbm, k_hbm, v_hbm, p_hbm, wp_hbm,
                   w, wp, toks, q, k, v, pr,
                   w_sem, cs, cr, ys, yr, fs, fr, o_sem):
    seqs, quarter, d = tok_ref.shape
    pairs = d // PAIR
    wide, n = lax.axis_index("wide"), lax.axis_index("narrow")
    c, y = n % 2, n // 2
    core_n, y_n = n + 1 - 2 * c, n + 2 - 4 * y
    core_peer, y_peer = (wide, core_n), (wide, y_n)
    w_copy = pltpu.make_async_copy(w_hbm, w, w_sem)
    w_copy.start()
    bar = pltpu.get_barrier_semaphore()
    for peer in (core_peer, y_peer):
        pl.semaphore_signal(bar, inc=1, device_id=peer, device_id_type=MESH)
    pl.semaphore_wait(bar, 2)

    def send_y(s):
        return copy_to(tok_ref.at[s], toks.at[s, n], ys.at[s], yr.at[s], y_peer)

    def send_core(s):
        return copy_to(tok_ref.at[s], toks.at[s, n], cs.at[s], cr.at[s], core_peer)

    def forward_y(s):
        return copy_to(toks.at[s, y_n], toks.at[s, y_n], fs.at[s], fr.at[s], core_peer)

    for s in range(seqs):
        send_y(s).start()
        send_core(s).start()
    for s in range(seqs):
        toks[s, n] = tok_ref[s]
    w_copy.wait()
    left = left_lanes(d)
    for p in range(pairs):
        t0, t1, t2 = (w[:, pl.ds(p * 3 * PAIR + i * PAIR, PAIR)].astype(F32) for i in range(3))
        cols = pl.ds(p * PAIR, PAIR)
        wp[0, :, cols] = jnp.where(left, t0, t1).astype(BF)
        wp[1, :, cols] = pltpu.roll(jnp.where(left, t2, t0), HD, 1).astype(BF)
        wp[2, :, cols] = jnp.where(left, t1, t2).astype(BF)
    wp_out = pltpu.make_async_copy(wp, wp_hbm, o_sem.at[0])
    wp_out.start()
    own = tok_ref[...].reshape(seqs * quarter, d)
    q[...] = ((dg(own, wp[0], 1, 0) + b_ref[0:1, :]).astype(BF) * 0.125).reshape(seqs, quarter, d)
    q_out = pltpu.make_async_copy(q, q_hbm, o_sem.at[1])
    q_out.start()

    def project(s, half):
        blocks = pl.ds(2 * half, 2)
        rows = toks[s, blocks].reshape(2 * quarter, d)
        k[s, blocks] = dg(rows, wp[1], 1, 0).astype(BF).reshape(2, quarter, d)
        v[s, blocks] = (dg(rows, wp[2], 1, 0) + b_ref[1:2, :]).astype(BF).reshape(2, quarter, d)

    for s in range(seqs):
        send_core(s).wait_recv()
    for s in range(seqs):
        project(s, y)

    def fetch_far(s):
        copy_to(toks.at[s, y_n], toks.at[s, y_n], ys.at[s], yr.at[s], y_peer).wait_recv()
        forward_y(s).start()

    outs = []
    fetch_far(0)
    for s in range(seqs):
        far = core_n + 2 - 4 * y
        copy_to(toks.at[s, far], toks.at[s, far], fs.at[s], fr.at[s], core_peer).wait_recv()
        project(s, 1 - y)
        if s + 1 < seqs:
            fetch_far(s + 1)
        for i, (src, dst) in enumerate(((toks, toks_hbm), (k, k_hbm), (v, v_hbm))):
            cp = pltpu.make_async_copy(src.at[s], dst.at[s], o_sem.at[2 + 4 * s + i])
            cp.start()
            outs.append(cp)
        keys = 4 * quarter
        live = lax.broadcasted_iota(jnp.int32, (keys, 2 * quarter), 0) < len_ref[s]

        def unit(p, carry):
            cols = pl.ds(pl.multiple_of(p * PAIR, PAIR), PAIR)
            qs = stack_heads(q[s, :, cols])
            kp = k[s, :, :, cols].reshape(keys, PAIR)
            vp = v[s, :, :, cols].reshape(keys, PAIR)
            scores = jnp.where(live, dg(kp, qs, 1, 1), -1000000000.0)
            e = jnp.exp(scores - jnp.max(scores, axis=0, keepdims=True))
            probs = (e * (1.0 / jnp.sum(e, axis=0, keepdims=True))).astype(BF)
            pr[s, p] = probs
            ctx_ref[s, :, cols] = unstack_heads(dg(vp, probs, 0, 0)).astype(BF)
            return carry

        lax.fori_loop(0, pairs, unit, 0)
        cp = pltpu.make_async_copy(pr.at[s], p_hbm.at[s], o_sem.at[2 + 4 * s + 3])
        cp.start()
        outs.append(cp)
    for s in range(seqs):
        send_y(s).wait_send()
        send_core(s).wait_send()
        forward_y(s).wait_send()
    for cp in [wp_out, q_out] + outs:
        cp.wait()


def attention_forward(tokens, lengths, qkv_weight, qv_bias):
    seqs, quarter, d = tokens.shape
    S = jax.ShapeDtypeStruct
    keys = (seqs, 4, quarter, d)
    pairs = d // PAIR
    shapes = [S((seqs, quarter, d), BF), S(keys, BF), S((seqs, quarter, d), BF), S(keys, BF), S(keys, BF),
              S((seqs, pairs, 4 * quarter, 2 * quarter), BF), S((3, d, d), BF)]
    return pl.pallas_call(
        forward_kernel,
        out_shape=shapes,
        in_specs=[pl.BlockSpec(memory_space=pltpu.SMEM), pl.BlockSpec(memory_space=V),
                  pl.BlockSpec(memory_space=ANY), pl.BlockSpec(memory_space=V)],
        out_specs=[pl.BlockSpec(memory_space=V)] + [pl.BlockSpec(memory_space=ANY)] * 6,
        scratch_shapes=[V(qkv_weight.shape, BF), V((3, d, d), BF), V(keys, BF), V((seqs, quarter, d), BF),
                        V(keys, BF), V(keys, BF), V(shapes[5].shape, BF), DMA]
        + [DMA((seqs,))] * 6 + [DMA((2 + 4 * seqs,))],
        name="attention_forward",
        compiler_params=pltpu.CompilerParams(collective_id=1, has_side_effects=True, vmem_limit_bytes=40 << 20),
    )(lengths, tokens, qkv_weight, qv_bias)


def fold(x):
    return jnp.sum(x.reshape(x.shape[0] // 8, 8, x.shape[1]), axis=0)


def rows_kernel(len_ref, tok_ref, cot_ref, ctx_ref, wo_hbm, bo_ref, g1_ref, s1_ref, wu_hbm, bu_ref, wd_hbm, bd_ref,
                g2_ref, s2_ref,
                out_ref, dsum_ref, dctx_ref, first_ref, act_ref, dpre_ref, dffn_ref, datt_ref, sums_ref,
                wo, wu, wd, val, first, normed1, scale1, slope, dsec, part, part_up, sem):
    rows, d = tok_ref.shape
    ff = wu.shape[1]
    quarter = rows // len_ref.shape[0]
    base = lax.axis_index("narrow") * quarter
    loads = [pltpu.make_async_copy(s, t, sem.at[i])
             for i, (s, t) in enumerate(((wo_hbm, wo), (wu_hbm, wu), (wd_hbm, wd)))]
    for cp in loads:
        cp.start()
    part[...] = jnp.zeros_like(part)
    chunk = 64
    chunks = rows // chunk
    loads[0].wait()
    for b in range(d // 256):
        cols = pl.ds(b * 256, 256)
        val[:, cols] = dg(ctx_ref[...], wo[:, cols], 1, 0) + bo_ref[:, cols] + tok_ref[:, cols].astype(F32)

    def norm1(i, carry):
        r = pl.ds(pl.multiple_of(i * chunk, chunk), chunk)
        v = val[r]
        center = v - jnp.mean(v, axis=-1, keepdims=True)
        scale = lax.rsqrt(jnp.mean(center * center, axis=-1, keepdims=True) + epsilon)
        normed = center * scale
        x = normed * g1_ref[...] + s1_ref[...]
        normed1[r] = normed
        scale1[r] = jnp.broadcast_to(scale, (chunk, 128))
        first[r] = x
        first_ref[r] = x.astype(BF)
        return carry

    lax.fori_loop(0, chunks, norm1, 0)
    loads[1].wait()

    def up(j, carry):
        cols = pl.ds(pl.multiple_of(j * 256, 256), 256)
        pre = dg(first_ref[...], wu[:, cols], 1, 0) + bu_ref[:, cols]
        half = 0.5 + 0.5 * lax.erf(pre * root_half)
        act_ref[j // 3, :, pl.ds(pl.multiple_of(j % 3 * 256, 256), 256)] = (pre * half).astype(BF)
        slope[:, cols] = half + pre * (jnp.exp(-0.5 * pre * pre) * inv_root_two_pi)
        return carry

    lax.fori_loop(0, ff // 256, up, 0)
    loads[2].wait()
    for b in range(d // 256):
        cols = pl.ds(b * 256, 256)
        val[:, cols] = bd_ref[:, cols] + first[:, cols] + sum(
            dg(act_ref[i], wd[i * d:(i + 1) * d, cols], 1, 0) for i in range(ff // d))

    def norm2(i, carry):
        r = pl.ds(pl.multiple_of(i * chunk, chunk), chunk)
        v = val[r]
        center = v - jnp.mean(v, axis=-1, keepdims=True)
        scale = lax.rsqrt(jnp.mean(center * center, axis=-1, keepdims=True) + epsilon)
        normed = center * scale
        out_ref[r] = (normed * g2_ref[...] + s2_ref[...]).astype(BF)
        s = i * chunk // quarter
        pos = base + i * chunk - s * quarter + lax.broadcasted_iota(jnp.int32, (chunk, d), 0)
        d_out = jnp.where(pos < len_ref[s], cot_ref[r].astype(F32), 0.0)
        part[1] += fold(d_out * normed)
        part[2] += fold(d_out)
        g = d_out * g2_ref[...]
        inner = g - jnp.mean(g, axis=-1, keepdims=True) - normed * jnp.mean(g * normed, axis=-1, keepdims=True)
        d_second = scale * inner
        dsec[r] = d_second
        low = d_second.astype(BF)
        dffn_ref[r] = low
        part[0] += fold(low.astype(F32))
        return carry

    lax.fori_loop(0, chunks, norm2, 0)

    def up_back(j, carry):
        cols = pl.ds(pl.multiple_of(j * 256, 256), 256)
        low = (dg(dffn_ref[...], wd[cols, :], 1, 1) * slope[:, cols]).astype(BF)
        dpre_ref[j // 3, :, pl.ds(pl.multiple_of(j % 3 * 256, 256), 256)] = low
        part_up[:, cols] = fold(low.astype(F32))
        return carry

    lax.fori_loop(0, ff // 256, up_back, 0)
    for b in range(d // 256):
        cols = pl.ds(b * 256, 256)
        val[:, cols] = dsec[:, cols] + sum(
            dg(dpre_ref[i], wu[cols, i * d:(i + 1) * d], 1, 1) for i in range(ff // d))

    def norm1_back(i, carry):
        r = pl.ds(pl.multiple_of(i * chunk, chunk), chunk)
        d_first, normed = val[r], normed1[r]
        part[4] += fold(d_first * normed)
        part[5] += fold(d_first)
        g = d_first * g1_ref[...]
        inner = g - jnp.mean(g, axis=-1, keepdims=True) - normed * jnp.mean(g * normed, axis=-1, keepdims=True)
        d_sum = scale1[r, :1] * inner
        dsum_ref[r] = d_sum
        low = d_sum.astype(BF)
        datt_ref[r] = low
        part[3] += fold(low.astype(F32))
        return carry

    lax.fori_loop(0, chunks, norm1_back, 0)
    dctx_ref[...] = dg(datt_ref[...], wo[...], 1, 1).astype(BF)
    total = lambda x: jnp.sum(x, axis=0, keepdims=True)
    ups = ff // d
    sums_ref[0:1] = total(part[3])
    sums_ref[1:2] = total(part[4])
    sums_ref[2:3] = total(part[5])
    for i in range(ups):
        sums_ref[3 + i:4 + i] = total(part_up[:, i * d:(i + 1) * d])
    sums_ref[3 + ups:4 + ups] = total(part[0])
    sums_ref[4 + ups:5 + ups] = total(part[1])
    sums_ref[5 + ups:6 + ups] = total(part[2])


def rows_part(tok, cot, ctx, lengths, wo, bo, g1, s1, wu, bu, wd, bd, g2, s2):
    rows, d = tok.shape
    ff = wu.shape[1]
    S = jax.ShapeDtypeStruct
    row = lambda a: a.reshape(1, -1)
    vm, hbm = pl.BlockSpec(memory_space=V), pl.BlockSpec(memory_space=ANY)
    return pl.pallas_call(
        rows_kernel,
        out_shape=[S((rows, d), BF), S((rows, d), F32), S((rows, d), BF), S((rows, d), BF), S((ff // d, rows, d), BF),
                   S((ff // d, rows, d), BF), S((rows, d), BF), S((rows, d), BF), S((6 + ff // d, d), F32)],
        in_specs=[pl.BlockSpec(memory_space=pltpu.SMEM), vm, vm, vm, hbm, vm, vm, vm, hbm, vm, hbm, vm, vm, vm],
        out_specs=[vm] * 9,
        scratch_shapes=[V(wo.shape, BF), V(wu.shape, BF), V(wd.shape, BF), V((rows, d), F32), V((rows, d), F32),
                        V((rows, d), F32), V((rows, 128), F32), V((rows, ff), F32), V((rows, d), F32),
                        V((6, 8, d), F32), V((8, ff), F32), DMA((3,))],
        name="rows_part",
        compiler_params=pltpu.CompilerParams(vmem_limit_bytes=48 << 20),
    )(lengths, tok, cot, ctx, wo, row(bo), row(g1), row(s1), wu, row(bu), wd, row(bd), row(g2), row(s2))


LAGS = (0, 1, 3, 4, 6, 7, 8)
UNITS = 5


def tail_kernel(act_h, dpre_h, dffn_h, first_h, ctx_h, datt_h, dctx_h, dsum_h, toks_h, tok_h, q_h, k_h, v_h, p_h, wp_h,
                sums_ref,
                od_hbm, ou_hbm, oo_hbm, oq_hbm, din_hbm, so_ref,
                a_buf, b_buf, dffn, first, ctx, datt, dctx, dsum, toks, tok, q, k, v, pr, wp, dq, dtok,
                g, r1, r2, r3, r4, sbuf, srecv, x1, x2, din,
                s1, q1, s2, q2, s3, q3, s4, q4, s5, q5, s6, q6, os_, ss, sq, xs, ls):
    pieces, _, _, R, C = g.shape
    seqs, quarter, d = dctx.shape
    rows, keys, pairs = seqs * quarter, 4 * quarter, d // PAIR
    nd = act_h.shape[0]
    nu = dpre_h.shape[0]
    h = R // 2
    hr, hc = h // 2, C // 2
    w, n = lax.axis_index("wide"), lax.axis_index("narrow")
    c, y, x, z = n % 2, n // 2, w % 2, (w // 2) % 4
    core_peer, y_peer, x_peer = (w, n + 1 - 2 * c), (w, n + 2 - 4 * y), (w + 1 - 2 * x, n)
    zs = [z + 1 - 2 * (z % 2), z + 2 - 4 * (z // 2), 3 - z]
    z_peers = [(w + 2 * (j - z), n) for j in zs]

    a_view, b_view = a_buf.reshape(nd, rows, d), b_buf.reshape(nu, rows, d)
    dk, dv = a_buf.reshape(seqs, keys, d), b_buf.reshape(seqs, keys, d)
    loads = [(act_h, a_view), (dffn_h, dffn), (dpre_h, b_view), (first_h, first), (ctx_h, ctx), (datt_h, datt),
             (v_h, v), (dctx_h, dctx), (p_h, pr), (q_h, q), (k_h, k), (toks_h, toks), (tok_h, tok), (wp_h, wp),
             (dsum_h, dsum)]
    loads = [pltpu.make_async_copy(s, t, ls.at[i]) for i, (s, t) in enumerate(loads)]
    for cp in loads:
        cp.start()
    bar = pltpu.get_barrier_semaphore()
    for dev in [core_peer, y_peer, x_peer] + z_peers:
        pl.semaphore_signal(bar, inc=1, device_id=dev, device_id_type=MESH)

    def cut(j):
        return (pl.ds(pl.multiple_of(x * h + (j // 2) * hr, 16), hr), pl.ds(pl.multiple_of((j % 2) * hc, 128), hc))

    near = pl.ds(pl.multiple_of(x * h, 16), h)
    away = pl.ds(pl.multiple_of((1 - x) * h, 16), h)

    def c1(p):
        return copy_to(g.at[p, 1 - c], r1.at[p], s1.at[p], q1.at[p], core_peer)

    def c2(p):
        return copy_to(g.at[p, c, 1 - y], r2.at[p], s2.at[p], q2.at[p], y_peer)

    def c3(p):
        return copy_to(g.at[p, c, y, away], r3.at[p], s3.at[p], q3.at[p], x_peer)

    def c4(p, e):
        rr, cc = cut(zs[e])
        return copy_to(g.at[p, c, y, rr, cc], r4.at[p, e], s4.at[p, e], q4.at[p, e], z_peers[e])

    def c5(p, e, j):
        rr, cc = cut(j)
        return copy_to(r1.at[p, 0, rr, cc], r1.at[p, 0, rr, cc], s5.at[p, e], q5.at[p, e], z_peers[e])

    def c6(p, rr):
        return copy_to(r1.at[p, 0, rr], r1.at[p, 0, rr], s6.at[p], q6.at[p], x_peer)

    def store(p, dst):
        return pltpu.make_async_copy(r1.at[p, 0], dst, os_.at[p])

    def st1(p):
        c1(p).wait_recv()
        g[p, c] = (g[p, c].astype(F32) + r1[p].astype(F32)).astype(BF)
        c2(p).start()

    def st2(p):
        c2(p).wait_recv()
        g[p, c, y] = (g[p, c, y].astype(F32) + r2[p].astype(F32)).astype(BF)
        c3(p).start()

    def st3(p):
        c3(p).wait_recv()
        g[p, c, y, near] = (g[p, c, y, near].astype(F32) + r3[p].astype(F32)).astype(BF)
        for e in (1, 2, 0):
            c4(p, e).start()

    def st4(p):
        for e in range(3):
            c4(p, e).wait_recv()
        rr, cc = cut(z)
        t = g[p, c, y, rr, cc].astype(F32) + r4[p, 0].astype(F32) + r4[p, 1].astype(F32) + r4[p, 2].astype(F32)
        r1[p, 0, rr, cc] = t.astype(BF)
        for e in (1, 2, 0):
            c5(p, e, z).start()

    def st5(p):
        for e in range(3):
            c5(p, e, zs[e]).wait_recv()
        c6(p, near).start()

    def st6(p):
        c6(p, away).wait_recv()

        @pl.when(p < nd)
        def down():
            store(p, od_hbm.at[pl.ds(p * R, R)]).start()

        @pl.when(jnp.logical_and(p >= nd, p < nd + nu))
        def up():
            store(p, ou_hbm.at[:, pl.ds(pl.multiple_of((p - nd) * C, C), C)]).start()

        @pl.when(p == nd + nu)
        def out():
            store(p, oo_hbm).start()

        @pl.when(p > nd + nu)
        def qkv():
            store(p, oq_hbm.at[:, pl.ds(pl.multiple_of((p - nd - nu - 1) * C, C), C)]).start()

    stages = [None, st1, st2, st3, st4, st5, st6]

    loads[0].wait()
    loads[1].wait()

    def down_block(i, carry):
        t = dg(a_view[i], dffn[...], 0, 0).astype(BF)
        for j in range(nd):
            g[j, i % 2, i // 2] = t[j * R:(j + 1) * R]
        return carry

    lax.fori_loop(0, nd, down_block, 0)
    pl.semaphore_wait(bar, 6)
    for p in range(nd):
        c1(p).start()
    loads[2].wait()
    loads[3].wait()

    def row_block(p, t):
        for j in range(4):
            g[p, j % 2, j // 2] = t[j * R:(j + 1) * R].astype(BF)

    def up_block(i, carry):
        row_block(nd + i, dg(first[...], b_view[i], 0, 0))
        c1(nd + i).start()
        return carry

    lax.fori_loop(0, 2, up_block, 0)
    st1(0)
    st1(1)
    lax.fori_loop(2, nu, up_block, 0)
    loads[4].wait()
    loads[5].wait()
    row_block(nd + nu, dg(ctx[...], datt[...], 0, 0))
    c1(nd + nu).start()
    for cp in loads[6:]:
        cp.wait()

    def unit(u, carry):
        s, p = u // pairs, u % pairs
        cols = pl.ds(pl.multiple_of(p * PAIR, PAIR), PAIR)
        qs = stack_heads(q[s, :, cols])
        ds = stack_heads(dctx[s, :, cols])
        low = pr[s, p]
        probs = low.astype(F32)
        t = probs * dg(v[s, :, cols], ds, 1, 1)
        d_raw = (t - probs * jnp.sum(t, axis=0, keepdims=True)).astype(BF)
        dv[s, :, cols] = dg(low, ds, 1, 0).astype(BF)
        dk[s, :, cols] = dg(d_raw, qs, 1, 0).astype(BF)
        dq[s, :, cols] = (unstack_heads(dg(k[s, :, cols], d_raw, 0, 0)) * 0.125).astype(BF)
        return carry

    def qkv_piece(i):
        cols = pl.ds(i * 2 * PAIR, 2 * PAIR)
        allt = toks[...].reshape(seqs * keys, d)
        ga = dg(tok[...].reshape(rows, d), dq[:, :, cols].reshape(rows, 2 * PAIR), 0, 0)
        gb = dg(allt, a_buf[:, cols], 0, 0)
        gc = dg(allt, b_buf[:, cols], 0, 0)
        left = left_lanes(R)
        p = nd + nu + 1 + i
        for e in range(4):
            rr = slice(e * R, (e + 1) * R)
            for j in range(2):
                sl = slice(j * PAIR, (j + 1) * PAIR)
                aj, bj, cj = ga[rr, sl], pltpu.roll(gb[rr, sl], HD, 1), gc[rr, sl]
                for t, val in enumerate((jnp.where(left, aj, bj), jnp.where(left, cj, aj), jnp.where(left, bj, cj))):
                    g[p, e % 2, e // 2, :, pl.ds((3 * j + t) * PAIR, PAIR)] = val.astype(BF)
        c1(p).start()

    cx1 = copy_to(dtok.at[:, 1 - c], x1, xs.at[0], xs.at[1], core_peer)
    cx2 = copy_to(dtok.at[1 - y, c], x2, xs.at[2], xs.at[3], y_peer)

    def input_part():
        def one(s, carry):
            t = dg(dk[s], wp[1], 1, 1) + dg(dv[s], wp[2], 1, 1)
            for e in range(4):
                dtok[e // 2, e % 2, s] = t[e * quarter:(e + 1) * quarter].astype(BF)
            return carry

        lax.fori_loop(0, seqs, one, 0)
        cx1.start()
        dsum[...] += dg(dq[...].reshape(rows, d), wp[0], 1, 1)

    def small(i, slot, dev):
        return copy_to(sbuf.at[i], srecv.at[slot], ss.at[slot], sq.at[slot], dev)

    def sums0():
        sbuf[0, 0:1] = jnp.sum(fold(dq[...].reshape(rows, d).astype(F32)), axis=0, keepdims=True)

        def add(s, acc):
            return acc + fold(dv[s].astype(F32))

        acc = lax.fori_loop(0, seqs, add, jnp.zeros((8, d), F32))
        sbuf[0, 1:2] = jnp.sum(acc, axis=0, keepdims=True)
        sbuf[0, 2:] = sums_ref[...]
        small(0, 0, core_peer).start()

    def sums1():
        small(0, 0, core_peer).wait_recv()
        sbuf[1] = sbuf[0] + srecv[0]
        small(1, 1, y_peer).start()

    def sums2():
        small(1, 1, y_peer).wait_recv()
        sbuf[2] = sbuf[1] + srecv[1]
        small(2, 2, x_peer).start()

    def sums3():
        small(2, 2, x_peer).wait_recv()
        sbuf[3] = sbuf[2] + srecv[2]
        for e in range(3):
            small(3, 3 + e, z_peers[e]).start()

    def add_x1():
        cx1.wait_recv()

        def add(i, carry):
            a, b = i // seqs, i % seqs
            dtok[a, c, b] = (dtok[a, c, b].astype(F32) + x1[a, b].astype(F32)).astype(BF)
            return carry

        lax.fori_loop(0, 2 * seqs, add, 0)

    units = seqs * pairs
    slots_of_units = -(-units // UNITS)
    extra = {7: [lambda: qkv_piece(0), lambda: qkv_piece(1)], 8: [lambda: qkv_piece(2), sums0, input_part],
             9: [add_x1, sums1], 12: [sums2], 13: [cx2.start, sums3]}

    def slot(t, carry):
        for i in (6, 5, 4, 3, 2, 1):
            p = t - LAGS[i]

            @pl.when(jnp.logical_and(p >= 0, p < pieces))
            def run():
                stages[i](p)

        @pl.when(t < 3 + slots_of_units)
        def attention():
            lo = (t - 3) * UNITS
            lax.fori_loop(lo, jnp.minimum(lo + UNITS, units), unit, 0)

        for at, todo in extra.items():
            @pl.when(t == at)
            def more():
                for f in todo:
                    f()
        return carry

    lax.fori_loop(3, pieces + LAGS[6], slot, 0)
    cx2.wait_recv()

    def out_x(i, carry):
        r = pl.ds(pl.multiple_of(i * quarter, quarter), quarter)
        din[i] = (dsum[r] + dtok[y, c, i].astype(F32) + x2[i].astype(F32)).astype(BF)
        return carry

    lax.fori_loop(0, seqs, out_x, 0)
    din_out = pltpu.make_async_copy(din, din_hbm, xs.at[4])
    din_out.start()
    for e in range(3):
        small(3, 3 + e, z_peers[e]).wait_recv()
    so_ref[...] = sbuf[3] + srecv[3] + srecv[4] + srecv[5]
    small(0, 0, core_peer).wait_send()
    small(1, 1, y_peer).wait_send()
    small(2, 2, x_peer).wait_send()
    for e in range(3):
        small(3, 3 + e, z_peers[e]).wait_send()
    cx1.wait_send()
    cx2.wait_send()

    def drain(p, carry):
        c1(p).wait_send()
        c2(p).wait_send()
        c3(p).wait_send()
        c6(p, near).wait_send()
        store(p, oo_hbm).wait()
        for e in range(3):
            c4(p, e).wait_send()
            c5(p, e, z).wait_send()
        return carry

    lax.fori_loop(0, pieces, drain, 0)
    din_out.wait()


def tail_part(act, dpre, dffn, first, ctx, datt, dctx, dsum, toks, tok, q, k, v, probs, wp, sums):
    seqs, quarter, d = tok.shape
    rows, keys = seqs * quarter, 4 * quarter
    R = d // 4
    nd, nu = act.shape[0], dpre.shape[0]
    n = nd + nu + 4
    h = R // 2
    all_rows = (sums.shape[0] + 2, d)
    vm, hbm = pl.BlockSpec(memory_space=V), pl.BlockSpec(memory_space=ANY)
    S = jax.ShapeDtypeStruct
    own, every = (seqs, quarter, d), (seqs, keys, d)
    return pl.pallas_call(
        tail_kernel,
        out_shape=(S((nd * R, d), BF), S((R, nu * d), BF), S((R, d), BF), S((R, 3 * d), BF), S(own, BF),
                   S(all_rows, F32)),
        in_specs=[hbm] * 15 + [vm],
        out_specs=(hbm, hbm, hbm, hbm, hbm, vm),
        scratch_shapes=[V((seqs * keys, d), BF), V((seqs * keys, d), BF), V((rows, d), BF), V((rows, d), BF),
                        V((rows, d), BF), V((rows, d), BF), V(own, BF), V((rows, d), F32), V(every, BF), V(own, BF),
                        V(own, BF), V(every, BF), V(every, BF), V(probs.shape, BF), V((3, d, d), BF), V(own, BF),
                        V((2, 2) + own, BF),
                        V((n, 2, 2, R, d), BF), V((n, 2, R, d), BF), V((n, R, d), BF), V((n, h, d), BF),
                        V((n, 3, h // 2, d // 2), BF), V((4,) + all_rows, F32), V((6,) + all_rows, F32),
                        V((2,) + own, BF), V(own, BF), V(own, BF)]
        + [DMA((n,))] * 6 + [DMA((n, 3))] * 4 + [DMA((n,))] * 3 + [DMA((6,))] * 2 + [DMA((5,)), DMA((15,))],
        name="tail_part",
        compiler_params=pltpu.CompilerParams(collective_id=2, has_side_effects=True, vmem_limit_bytes=62 << 20),
    )(act, dpre, dffn, first, ctx, datt, dctx, dsum, toks, tok, q, k, v, probs, wp, sums)


def local(tokens, lengths, qkv_weight, qv_bias, out_weight, out_bias, norm1_gain, norm1_shift, up_weight, up_bias,
          down_weight, down_bias, norm2_gain, norm2_shift, cotangent):
    seqs, quarter, d = tokens.shape
    rows = seqs * quarter
    own, every = (seqs, quarter, d), (seqs, 4 * quarter, d)
    ctx, toks, q, k, v, probs, wp = attention_forward(tokens, lengths, qkv_weight, qv_bias)
    ctx_rows = ctx.reshape(rows, d)
    output, dsum, dctx, first, act, dpre, dffn, datt, sums = rows_part(
        tokens.reshape(rows, d), cotangent.reshape(rows, d), ctx_rows, lengths, out_weight, out_bias,
        norm1_gain, norm1_shift, up_weight, up_bias, down_weight, down_bias, norm2_gain, norm2_shift)
    down, up, out, qkv, input_grad, sums = tail_part(
        act, dpre, dffn, first, ctx_rows, datt, dctx.reshape(own), dsum, toks.reshape(every), tokens, q,
        k.reshape(every), v.reshape(every), probs, wp, sums)
    grads = [a.astype(F32) for a in (down, up, out, qkv)]
    wide = lax.axis_size("wide")
    if wide > 8:
        groups = [[j * 8 + i for j in range(wide // 8)] for i in range(8)]
        grads = lax.psum(grads, "wide", axis_index_groups=groups)
        sums = lax.psum(sums, "wide", axis_index_groups=groups)
    down, up, out, qkv = grads
    n = lax.axis_index("narrow")
    R = d // 4
    nu = up.shape[1] // d
    part = lambda r: lax.dynamic_slice_in_dim(sums[r], n * R, R, 0)
    i = 5 + nu
    up_b = lax.dynamic_slice_in_dim(sums[5:i].reshape(-1), n * (nu * R), nu * R, 0)
    return (output.reshape(own), input_grad, qkv, lax.dynamic_slice_in_dim(sums[:2], n * R, R, 1), out,
            part(2), part(3), part(4), up, up_b, down, part(i), part(i + 1), part(i + 2))


def solution(mesh):
    return jax.shard_map(
        local,
        mesh=mesh,
        in_specs=(
            P("wide", "narrow", None),
            P("wide"),
            P(),
            P(),
            P(),
            P(),
            P(),
            P(),
            P(),
            P(),
            P(),
            P(),
            P(),
            P(),
            P("wide", "narrow", None),
        ),
        out_specs=(
            P("wide", "narrow", None),
            P("wide", "narrow", None),
            P("narrow", None),
            P(None, "narrow"),
            P("narrow", None),
            P("narrow"),
            P("narrow"),
            P("narrow"),
            P("narrow", None),
            P("narrow"),
            P("narrow", None),
            P("narrow"),
            P("narrow"),
            P("narrow"),
        ),
        check_vma=False,
    )
```

time: 250 us -> 206 us (0.82)
  Pallas kernels: 213 us -> 179 us
  matrix products: 9.34 us -> 0 us
  local copies, waits for them, and re-layouts: 22.4 us -> 18.5 us
  other arithmetic: 3.39 us -> 6.7 us
    pallas_call x2 -> x1, Pallas kernels: 161 us -> 127 us  [tail_part(): pl.pallas_call(tail_kernel, out_shape=(S((nd * R, d), BF), S((R, nu * d),...]
    dot_general x3 -> x0, matrix products: 9.34 us -> none  [dg(): lax.dot_general(a, b, (((ca,), (cb,)), ((), ())), preferred_element_type=...]
    convert_element_type x1 -> x4, other arithmetic: 2.69 us -> 6.7 us  [local(): grads = [a.astype(F32) for a in (down, up, out, qkv)]]
    reshape x3 -> x1, local copies, waits for them, and re-layouts: 3 us -> 0.01 us  [local(): sums[5:i].reshape(-1)]
    unnamed x53 -> x61, local copies, waits for them, and re-layouts: 13.7 us -> 15.2 us
where the time goes in v2:
time: 206 us; the launch traced here: 205 us
  Pallas kernels  179 us (87%)
  local copies, waits for them, and re-layouts  18.5 us (9%)
  other arithmetic  6.7 us (3%)
    pallas_call x1, Pallas kernels, tail_part(): pl.pallas_call(tail_kernel, out_shape=(S((nd * R, d), BF), S((R, nu * d),...  127 us
    pallas_call x1, Pallas kernels, attention_forward(): pl.pallas_call(forward_kernel, out_shape=shapes, in_specs=[pl.BlockSpec(m...  29.3 us
    pallas_call x1, Pallas kernels, rows_part(): pl.pallas_call(rows_kernel, out_shape=[S((rows, d), BF), S((rows, d), F32...  23.3 us
    unnamed x61, local copies, waits for them, and re-layouts  15.2 us
    convert_element_type x4, other arithmetic, local(): grads = [a.astype(F32) for a in (down, up, out, qkv)]  6.7 us

profile of v2, /device:TPU:0, one launch (start us, length us, event | category | flops | bytes accessed | tf_op | source)
XLA Modules:
  0.0 205.4 jit_solution(7932999589839503190)
XLA Ops:
  0.7 1.1 copy-done
  1.7 0.7 copy-done.16
  2.4 0.7 copy-done.17
  3.1 29.3 %attention_forward.1 = (bf16[3,128,768]{2,1,0:T(8,128)(2,1)S(1)}, bf16[3,4,128,768]{3,2,1,0:T(8,128)(2,1)S(1)}, bf16[3,128,768]{2,1,0:T(8,128)(2,1)S(1)}, bf16[3...) custom-call(s32[3]{0:T(128)S(1)} %copy-done.17, ...), custom_call_target="tpu_custom_call" | custom-call | tf_op jit(solution)/shard_map/attention_forward/pallas_call | solution.py:156
  32.5 1.8 copy-done.2
  34.3 1.5 copy-done.4
  35.8 1.5 copy-done.5
  37.3 1.4 copy-done.6
  38.7 0.8 copy-done.9
  39.7 23.3 %rows_part.1 = (bf16[384,768]{1,0:T(8,128)(2,1)}, f32[384,768]{1,0:T(8,128)S(1)}, bf16[384,768]{1,0:T(8,128)(2,1)S(1)}, bf16[384,768]{1,0:T(8,128)(2,1)S(1)}, bf...) custom-call(s32[3]{0:T(128)S(1)} %copy-done.18, ...), custom_call_target="tpu_custom_call" | custom-call | tf_op jit(solution)/shard_map/rows_part/pallas_call | solution.py:295
  63.0 1.0 copy-done.7
  64.0 0.8 copy-done.10
  64.9 0.8 copy-done.11
  65.7 0.8 copy-done.12
  66.5 0.8 copy-done.13
  67.9 126.6 %tail_part.1 = (bf16[768,768]{1,0:T(8,128)(2,1)}, bf16[192,3072]{1,0:T(8,128)(2,1)}, bf16[192,768]{1,0:T(8,128)(2,1)}, bf16[192,2304]{1,0:T(8,128)(2,1)}, bf16[3...) custom-call(bf16[4,384,768]{2,1,0:T(8,128)(2,1)} %get-tuple-element.38.act_h, bf16[4,384,768]{2,1,0:T(8,128)(2,1)} %get-tuple-element.39.dpre_h, ...), custom_call_target="tpu_custom_call" | custom-call | tf_op jit(solution)/shard_map/tail_part/pallas_call | solution.py:618
  194.6 2.6 %convert_element_type.12 = f32[192,2304]{1,0:T(8,128)} convert(bf16[192,2304]{1,0:T(8,128)(2,1)} %get-tuple-element.53) | non-fusion elementwise | flops 442368 | bytes 2654208 | tf_op jit(solution)/shard_map/convert_element_type | solution.py:650
  197.2 0.7 constant_dynamic-slice_fusion.6
  197.8 0.9 convert_element_type.13
  198.7 0.6 constant_dynamic-slice_fusion.4
  200.0 1.7 convert_element_type.14
  201.7 0.7 dynamic_slice.43
  202.4 1.6 convert_element_type.15
  204.6 0.8 copy.30
  (59 shorter events, 2.0 us)
Async XLA Ops:
  0.6 39.0 %copy-start.18 = (s32[3]{0:T(128)S(1)}, s32[3]{0:T(128)}, u32[]{:S(2)}) copy-start(s32[3]{0:T(128)} %len_ref.3) | copy-start | bytes 40
  0.7 1.1 copy-start
  3.1 36.4 %copy-start.24 = (f32[768]{0:T(1024)S(1)}, f32[768]{0:T(1024)}, u32[]{:S(2)}) copy-start(f32[768]{0:T(1024)} %param.20) | copy-start | bytes 9220
  3.1 36.4 %copy-start.25 = (f32[768]{0:T(1024)S(1)}, f32[768]{0:T(1024)}, u32[]{:S(2)}) copy-start(f32[768]{0:T(1024)} %param.21) | copy-start | bytes 9220
  3.1 36.5 %copy-start.26 = (f32[768]{0:T(1024)S(1)}, f32[768]{0:T(1024)}, u32[]{:S(2)}) copy-start(f32[768]{0:T(1024)} %param.22) | copy-start | bytes 9220
  3.1 36.5 %copy-start.27 = (f32[768]{0:T(1024)S(1)}, f32[768]{0:T(1024)}, u32[]{:S(2)}) copy-start(f32[768]{0:T(1024)} %param.26) | copy-start | bytes 9220
  3.1 36.5 %copy-start.28 = (f32[768]{0:T(1024)S(1)}, f32[768]{0:T(1024)}, u32[]{:S(2)}) copy-start(f32[768]{0:T(1024)} %param.27) | copy-start | bytes 9220
  3.1 36.5 %copy-start.29 = (f32[768]{0:T(1024)S(1)}, f32[768]{0:T(1024)}, u32[]{:S(2)}) copy-start(f32[768]{0:T(1024)} %param.28) | copy-start | bytes 9220
  3.1 36.5 %copy-start.1 = (bf16[3,128,768]{2,1,0:T(8,128)(2,1)S(1)}, bf16[3,128,768]{2,1,0:T(8,128)(2,1)}, u32[]{:S(2)}) copy-start(bf16[3,128,768]{2,1,0:T(8,128)(2,1)} %tok_h.1) | copy-start | bytes 1769476
  3.1 36.5 %copy-start.8 = (bf16[3,128,768]{2,1,0:T(8,128)(2,1)S(1)}, bf16[3,128,768]{2,1,0:T(8,128)(2,1)}, u32[]{:S(2)}) copy-start(bf16[3,128,768]{2,1,0:T(8,128)(2,1)} %param.29) | copy-start | bytes 1769476
  3.1 36.5 %copy-start.15 = (f32[3072]{0:T(1024)S(1)}, f32[3072]{0:T(1024)}, u32[]{:S(2)}) copy-start(f32[3072]{0:T(1024)} %param.24) | copy-start | bytes 36868
  32.5 1.8 copy-start.2
  34.3 1.5 copy-start.4
  35.8 1.5 copy-start.5
  37.3 1.4 copy-start.6
  39.5 23.5 %copy-start.3 = (bf16[3,128,768]{2,1,0:T(8,128)(2,1)}, bf16[3,128,768]{2,1,0:T(8,128)(2,1)S(1)}, u32[]{:S(2)}) copy-start(bf16[3,128,768]{2,1,0:T(8,128)(2,1)S(1)} %get-tuple-element.36) | copy-start | bytes 1769476
  63.0 1.0 copy-start.7
  64.0 0.8 copy-start.10
  66.5 0.8 copy-start.13
  194.5 2.6 %copy-start.23 = (f32[12,768]{1,0:T(8,128)S(1)}, f32[12,768]{1,0:T(8,128)}, u32[]{:S(2)}) copy-start(f32[12,768]{1,0:T(8,128)} %get-tuple-element.54) | copy-start | bytes 110596
  194.5 3.3 %copy-start.22 = (bf16[192,768]{1,0:T(8,128)(2,1)S(1)}, bf16[192,768]{1,0:T(8,128)(2,1)}, u32[]{:S(2)}) copy-start(bf16[192,768]{1,0:T(8,128)(2,1)} %get-tuple-element.55) | copy-start | bytes 884740
  194.5 5.4 %copy-start.20 = (bf16[192,3072]{1,0:T(8,128)(2,1)S(1)}, bf16[192,3072]{1,0:T(8,128)(2,1)}, u32[]{:S(2)}) copy-start(bf16[192,3072]{1,0:T(8,128)(2,1)} %get-tuple-element.56) | copy-start | bytes 3538948
  197.2 5.2 %copy-start.19 = (bf16[768,768]{1,0:T(8,128)(2,1)S(1)}, bf16[768,768]{1,0:T(8,128)(2,1)}, u32[]{:S(2)}) copy-start(bf16[768,768]{1,0:T(8,128)(2,1)} %get-tuple-element.57) | copy-start | bytes 3538948
  201.7 2.9 %copy-start.21 = (bf16[3,128,768]{2,1,0:T(8,128)(2,1)S(1)}, bf16[3,128,768]{2,1,0:T(8,128)(2,1)}, u32[]{:S(2)}) copy-start(bf16[3,128,768]{2,1,0:T(8,128)(2,1)} %get-tuple-element.85) | copy-start | bytes 1769476
  (6 other events, 4.4 us)

commit v3 on v2

v3 whole, which is shorter than its diff:
```python
import functools

import jax
import jax.numpy as jnp
from jax import lax
from jax.experimental import pallas as pl
from jax.experimental.pallas import tpu as pltpu
from jax.sharding import PartitionSpec as P

H = 12
HD = 64
PAIR = 2 * HD
epsilon = 1e-12
root_half = 0.7071067811865476
inv_root_two_pi = 0.3989422804014327
MESH = pl.DeviceIdType.MESH
F32 = jnp.float32
BF = jnp.bfloat16
V = pltpu.VMEM
DMA = pltpu.SemaphoreType.DMA
ANY = pl.ANY
UNROLL_ATT = 1
UNROLL_UP = 1


def dg(a, b, ca, cb):
    return lax.dot_general(a, b, (((ca,), (cb,)), ((), ())), preferred_element_type=F32)


def copy_to(src, dst, ss, rs, dev):
    return pltpu.make_async_remote_copy(
        src_ref=src, dst_ref=dst, send_sem=ss, recv_sem=rs, device_id=dev, device_id_type=MESH)


def left_lanes(rows):
    return lax.broadcasted_iota(jnp.int32, (rows, PAIR), 1) < HD


def stack_heads(x):
    left = left_lanes(x.shape[0])
    zero = jnp.zeros_like(x)
    return jnp.concatenate([jnp.where(left, x, zero), jnp.where(left, zero, x)], axis=0)


def unstack_heads(x_t):
    q = x_t.shape[1] // 2
    top = lax.broadcasted_iota(jnp.int32, (PAIR, q), 0) < HD
    return jnp.where(top, x_t[:, :q], x_t[:, q:]).T


def fold(x):
    return jnp.sum(x.reshape(x.shape[0] // 8, 8, x.shape[1]), axis=0)


def total(x):
    return jnp.sum(x, axis=0, keepdims=True)


def center_scale(v):
    center = v - jnp.mean(v, axis=-1, keepdims=True)
    scale = lax.rsqrt(jnp.mean(center * center, axis=-1, keepdims=True) + epsilon)
    return center * scale, scale


def norm_grad(g, normed):
    return g - jnp.mean(g, axis=-1, keepdims=True) - normed * jnp.mean(g * normed, axis=-1, keepdims=True)


def front_kernel(len_ref, tok_h, cot_h, w_h, wo_h, wu_h, wd_h, qvb_h, bo_h, g1_h, s1_h, bu_h, bd_h, g2_h, s2_h,
                 toks_h, q_h, k_h, v_h, p_h, wp_h, ctx_h, first_h, act_h, slope_h, out_h, dffn_h, dsec_h, normed_h,
                 scale_h, sums_ref,
                 w, wp, toks, q, k, v, pr, tok, cot, wo, wu, wd, ctx, low1, act, slope, out, dffn, dsec, normed1,
                 scale1, val, first, part, qvb_ref, bo_v, g1_v, s1_v, bu_v, bd_v, g2_v, s2_v,
                 ls, cs, cr, ys, yr, fs, fr, os_):
    seqs, quarter, d = tok.shape
    rows, keys, pairs = seqs * quarter, 4 * quarter, d // PAIR
    ff = wu.shape[1]
    wide, n = lax.axis_index("wide"), lax.axis_index("narrow")
    c, y = n % 2, n // 2
    core_n, y_n = n + 1 - 2 * c, n + 2 - 4 * y
    far_n = core_n + 2 - 4 * y
    core_peer, y_peer = (wide, core_n), (wide, y_n)
    loads = [pltpu.make_async_copy(s, t, ls.at[i]) for i, (s, t) in enumerate(
        ((tok_h, tok), (w_h, w), (wo_h, wo), (wu_h, wu), (cot_h, cot), (wd_h, wd), (qvb_h, qvb_ref), (bo_h, bo_v),
         (g1_h, g1_v), (s1_h, s1_v), (bu_h, bu_v), (bd_h, bd_v), (g2_h, g2_v), (s2_h, s2_v)))]
    outs = []

    def emit(src, dst):
        cp = pltpu.make_async_copy(src, dst, os_.at[len(outs)])
        cp.start()
        outs.append(cp)

    for cp in loads[:2]:
        cp.start()
    bar = pltpu.get_barrier_semaphore()
    for peer in (core_peer, y_peer):
        pl.semaphore_signal(bar, inc=1, device_id=peer, device_id_type=MESH)
    pl.semaphore_wait(bar, 2)

    def send_y(s):
        return copy_to(tok_h.at[s], toks.at[s, n], ys.at[s], yr.at[s], y_peer)

    def send_core(s):
        return copy_to(tok_h.at[s], toks.at[s, n], cs.at[s], cr.at[s], core_peer)

    def forward_y(s):
        return copy_to(toks.at[s, y_n], toks.at[s, y_n], fs.at[s], fr.at[s], core_peer)

    for s in range(seqs):
        send_y(s).start()
        send_core(s).start()
    for cp in loads[2:]:
        cp.start()
    loads[0].wait()
    for s in range(seqs):
        toks[s, n] = tok[s]
    loads[1].wait()
    left = left_lanes(d)
    for p in range(pairs):
        t0, t1, t2 = (w[:, pl.ds(p * 3 * PAIR + i * PAIR, PAIR)].astype(F32) for i in range(3))
        cols = pl.ds(p * PAIR, PAIR)
        wp[0, :, cols] = jnp.where(left, t0, t1).astype(BF)
        wp[1, :, cols] = pltpu.roll(jnp.where(left, t2, t0), HD, 1).astype(BF)
        wp[2, :, cols] = jnp.where(left, t1, t2).astype(BF)
    emit(wp, wp_h)
    for cp in loads[6:]:
        cp.wait()
    bo_ref, g1_ref, s1_ref, bd_ref, g2_ref, s2_ref = (
        r[...].reshape(1, d) for r in (bo_v, g1_v, s1_v, bd_v, g2_v, s2_v))
    own = tok[...].reshape(rows, d)
    q[...] = ((dg(own, wp[0], 1, 0) + qvb_ref[0:1, :]).astype(BF) * 0.125).reshape(seqs, quarter, d)
    emit(q, q_h)

    def project(s, half):
        blocks = pl.ds(2 * half, 2)
        x = toks[s, blocks].reshape(2 * quarter, d)
        k[s, blocks] = dg(x, wp[1], 1, 0).astype(BF).reshape(2, quarter, d)
        v[s, blocks] = (dg(x, wp[2], 1, 0) + qvb_ref[1:2, :]).astype(BF).reshape(2, quarter, d)

    for s in range(seqs):
        send_core(s).wait_recv()
    for s in range(seqs):
        project(s, y)

    def fetch_far(s):
        copy_to(toks.at[s, y_n], toks.at[s, y_n], ys.at[s], yr.at[s], y_peer).wait_recv()
        forward_y(s).start()

    fetch_far(0)
    for s in range(seqs):
        copy_to(toks.at[s, far_n], toks.at[s, far_n], fs.at[s], fr.at[s], core_peer).wait_recv()
        project(s, 1 - y)
        if s + 1 < seqs:
            fetch_far(s + 1)
        emit(toks.at[s], toks_h.at[s])
        emit(k.at[s], k_h.at[s])
        emit(v.at[s], v_h.at[s])
        live = lax.broadcasted_iota(jnp.int32, (keys, 2 * quarter), 0) < len_ref[s]

        def unit(p, carry):
            cols = pl.ds(pl.multiple_of(p * PAIR, PAIR), PAIR)
            qs = stack_heads(q[s, :, cols])
            kp = k[s, :, :, cols].reshape(keys, PAIR)
            vp = v[s, :, :, cols].reshape(keys, PAIR)
            scores = jnp.where(live, dg(kp, qs, 1, 1), -1000000000.0)
            e = jnp.exp(scores - jnp.max(scores, axis=0, keepdims=True))
            probs = (e * (1.0 / jnp.sum(e, axis=0, keepdims=True))).astype(BF)
            pr[s, p] = probs
            ctx[s * quarter:(s + 1) * quarter, cols] = unstack_heads(dg(vp, probs, 0, 0)).astype(BF)
            return carry

        lax.fori_loop(0, pairs, unit, 0, unroll=UNROLL_ATT)
        emit(pr.at[s], p_h.at[s])
    emit(ctx, ctx_h)

    part[...] = jnp.zeros_like(part)
    chunk = 64
    chunks = rows // chunk
    loads[2].wait()
    for b in range(d // 256):
        cols = pl.ds(b * 256, 256)
        val[:, cols] = (dg(ctx[...], wo[:, cols], 1, 0) + bo_ref[:, b * 256:(b + 1) * 256]
                        + tok[:, :, cols].reshape(rows, 256).astype(F32))

    def norm1(i, carry):
        r = pl.ds(pl.multiple_of(i * chunk, chunk), chunk)
        normed, scale = center_scale(val[r])
        x = normed * g1_ref + s1_ref
        normed1[r] = normed
        scale1[r] = jnp.broadcast_to(scale, (chunk, 128))
        first[r] = x
        low1[r] = x.astype(BF)
        return carry

    lax.fori_loop(0, chunks, norm1, 0)
    emit(low1, first_h)
    emit(normed1, normed_h)
    emit(scale1, scale_h)
    loads[3].wait()

    def up(j, carry):
        cols = pl.ds(pl.multiple_of(j * 256, 256), 256)
        at = (j // 3, slice(None), pl.ds(pl.multiple_of(j % 3 * 256, 256), 256))
        pre = dg(low1[...], wu[:, cols], 1, 0) + bu_v[cols].reshape(1, 256)
        half = 0.5 + 0.5 * lax.erf(pre * root_half)
        act[at] = (pre * half).astype(BF)
        slope[at] = (half + pre * (jnp.exp(-0.5 * pre * pre) * inv_root_two_pi)).astype(BF)
        return carry

    lax.fori_loop(0, ff // 256, up, 0, unroll=UNROLL_UP)
    emit(act, act_h)
    emit(slope, slope_h)
    loads[4].wait()
    loads[5].wait()
    for b in range(d // 256):
        cols = pl.ds(b * 256, 256)
        val[:, cols] = bd_ref[:, b * 256:(b + 1) * 256] + first[:, cols] + sum(
            dg(act[i], wd[i * d:(i + 1) * d, cols], 1, 0) for i in range(ff // d))

    def norm2(i, carry):
        r = pl.ds(pl.multiple_of(i * chunk, chunk), chunk)
        normed, scale = center_scale(val[r])
        out[r] = (normed * g2_ref + s2_ref).astype(BF)
        s = i * chunk // quarter
        off = pl.multiple_of(i * chunk - s * quarter, chunk)
        pos = n * quarter + off + lax.broadcasted_iota(jnp.int32, (chunk, d), 0)
        d_out = jnp.where(pos < len_ref[s], cot[s, pl.ds(off, chunk)].astype(F32), 0.0)
        part[1] += fold(d_out * normed)
        part[2] += fold(d_out)
        d_second = scale * norm_grad(d_out * g2_ref, normed)
        dsec[r] = d_second
        low = d_second.astype(BF)
        dffn[r] = low
        part[0] += fold(low.astype(F32))
        return carry

    lax.fori_loop(0, chunks, norm2, 0)
    emit(out, out_h)
    emit(dffn, dffn_h)
    emit(dsec, dsec_h)
    for i in range(3):
        sums_ref[i:i + 1] = total(part[i])
    for s in range(seqs):
        send_y(s).wait_send()
        send_core(s).wait_send()
        forward_y(s).wait_send()
    for cp in outs:
        cp.wait()


def front_part(tokens, lengths, w, qvb, wo, bo, g1, s1, wu, bu, wd, bd, g2, s2, cot):
    seqs, quarter, d = tokens.shape
    rows, pairs, ff = seqs * quarter, d // PAIR, wu.shape[1]
    S = jax.ShapeDtypeStruct
    vm, hbm = pl.BlockSpec(memory_space=V), pl.BlockSpec(memory_space=ANY)
    own, keys, flat = (seqs, quarter, d), (seqs, 4, quarter, d), (rows, d)
    probs, hidden = (seqs, pairs, 4 * quarter, 2 * quarter), (ff // d, rows, d)
    return pl.pallas_call(
        front_kernel,
        out_shape=[S(keys, BF), S(own, BF), S(keys, BF), S(keys, BF), S(probs, BF), S((3, d, d), BF), S(flat, BF),
                   S(flat, BF), S(hidden, BF), S(hidden, BF), S(flat, BF), S(flat, BF), S(flat, F32), S(flat, F32),
                   S((rows, 128), F32), S((3, d), F32)],
        in_specs=[pl.BlockSpec(memory_space=pltpu.SMEM)] + [hbm] * 14,
        out_specs=[hbm] * 15 + [vm],
        scratch_shapes=[V(w.shape, BF), V((3, d, d), BF), V(keys, BF), V(own, BF), V(keys, BF), V(keys, BF),
                        V(probs, BF), V(own, BF), V(own, BF), V(wo.shape, BF), V(wu.shape, BF), V(wd.shape, BF),
                        V(flat, BF), V(flat, BF), V(hidden, BF), V(hidden, BF), V(flat, BF), V(flat, BF),
                        V(flat, F32), V(flat, F32), V((rows, 128), F32), V(flat, F32), V(flat, F32),
                        V((3, 8, d), F32), V((2, d), F32), V((d,), F32), V((d,), F32), V((d,), F32), V((ff,), F32),
                        V((d,), F32), V((d,), F32), V((d,), F32), DMA((14,))] + [DMA((seqs,))] * 6 + [DMA((11 + 4 * seqs,))],
        name="front_part",
        compiler_params=pltpu.CompilerParams(collective_id=1, has_side_effects=True, vmem_limit_bytes=56 << 20),
    )(lengths, tokens, cot, w, wo, wu, wd, qvb, bo, g1, s1, bu, bd, g2, s2)


LAGS = (0, 1, 3, 4, 6, 7, 8)
UNITS = 5
UNROLL_BACK = 1


def tail_kernel(act_h, dffn_h, wd_h, slope_h, first_h, wu_h, dsec_h, normed_h, scale_h, wo_h, ctx_h, q_h, toks_h,
                wp_h, k_h, v_h, p_h, g1_h, sums_h,
                od_hbm, ou_hbm, oo_hbm, oq_hbm, din_hbm, so_ref,
                a_buf, b_buf, dffn, first, ctx, datt, dsum, toks, q, kv, pr, wp, dq, dtok, wo, dsec, normed1,
                scale1, part, part_up, g1_v, sums_ref, g, r1, r2, r3, r4, sbuf, srecv, x1, x2,
                s1, q1, s2, q2, s3, q3, s4, q4, s5, q5, s6, q6, os_, ss, sq, xs, ls):
    pieces, _, _, R, C = g.shape
    seqs, quarter, d = q.shape
    rows, keys, pairs = seqs * quarter, 4 * quarter, d // PAIR
    nd = nu = act_h.shape[0]
    ff = nd * d
    h = R // 2
    hr, hc = h // 2, C // 2
    w, n = lax.axis_index("wide"), lax.axis_index("narrow")
    c, y, x, z = n % 2, n // 2, w % 2, (w // 2) % 4
    core_peer, y_peer, x_peer = (w, n + 1 - 2 * c), (w, n + 2 - 4 * y), (w + 1 - 2 * x, n)
    zs = [z + 1 - 2 * (z % 2), z + 2 - 4 * (z // 2), 3 - z]
    z_peers = [(w + 2 * (j - z), n) for j in zs]

    a_view, b_view = a_buf.reshape(nd, rows, d), b_buf.reshape(nu, rows, d)
    dk, dv = a_buf.reshape(seqs, keys, d), b_buf.reshape(seqs, keys, d)
    wd, kvs = kv.reshape(ff, d), kv.reshape(2, seqs, keys, d)
    k, v = kvs.at[0], kvs.at[1]
    wu = pr.reshape(ff // 256, d, 2 * quarter)
    prs = pr.reshape(seqs, pairs, keys, 2 * quarter)
    slope = dtok.reshape(nd, rows, d)
    dctx = first.reshape(seqs, quarter, d)
    early = [(act_h, a_view), (dffn_h, dffn), (wd_h, wd), (slope_h, slope), (first_h, first), (dsec_h, dsec),
             (normed_h, normed1), (scale_h, scale1), (wo_h, wo), (ctx_h, ctx), (q_h, q), (toks_h, toks),
             (wp_h, wp), (g1_h, g1_v), (sums_h, sums_ref)]
    loads = [pltpu.make_async_copy(s, t, ls.at[i]) for i, (s, t) in enumerate(early)]
    wu_loads = [pltpu.make_async_copy(wu_h.at[:, j * 256:(j + 1) * 256], wu.at[j], ls.at[len(early) + j])
                for j in range(ff // 256)]
    after = len(early) + ff // 256
    k_load, v_load, p_load = (pltpu.make_async_copy(s, t, ls.at[after + i]) for i, (s, t) in enumerate(
        ((k_h, k), (v_h, v), (p_h, prs))))
    loads[4:4] = wu_loads
    for cp in loads:
        cp.start()
    bar = pltpu.get_barrier_semaphore()
    for dev in [core_peer, y_peer, x_peer] + z_peers:
        pl.semaphore_signal(bar, inc=1, device_id=dev, device_id_type=MESH)

    def cut(j):
        return (pl.ds(pl.multiple_of(x * h + (j // 2) * hr, 16), hr), pl.ds(pl.multiple_of((j % 2) * hc, 128), hc))

    near = pl.ds(pl.multiple_of(x * h, 16), h)
    away = pl.ds(pl.multiple_of((1 - x) * h, 16), h)

    def c1(p):
        return copy_to(g.at[p, 1 - c], r1.at[p], s1.at[p], q1.at[p], core_peer)

    def c2(p):
        return copy_to(g.at[p, c, 1 - y], r2.at[p], s2.at[p], q2.at[p], y_peer)

    def c3(p):
        return copy_to(g.at[p, c, y, away], r3.at[p], s3.at[p], q3.at[p], x_peer)

    def c4(p, e):
        rr, cc = cut(zs[e])
        return copy_to(g.at[p, c, y, rr, cc], r4.at[p, e], s4.at[p, e], q4.at[p, e], z_peers[e])

    def c5(p, e, j):
        rr, cc = cut(j)
        return copy_to(r1.at[p, 0, rr, cc], r1.at[p, 0, rr, cc], s5.at[p, e], q5.at[p, e], z_peers[e])

    def c6(p, rr):
        return copy_to(r1.at[p, 0, rr], r1.at[p, 0, rr], s6.at[p], q6.at[p], x_peer)

    def store(p, dst):
        return pltpu.make_async_copy(r1.at[p, 0], dst, os_.at[p])

    def st1(p):
        c1(p).wait_recv()
        g[p, c] = (g[p, c].astype(F32) + r1[p].astype(F32)).astype(BF)
        c2(p).start()

    def st2(p):
        c2(p).wait_recv()
        g[p, c, y] = (g[p, c, y].astype(F32) + r2[p].astype(F32)).astype(BF)
        c3(p).start()

    def st3(p):
        c3(p).wait_recv()
        g[p, c, y, near] = (g[p, c, y, near].astype(F32) + r3[p].astype(F32)).astype(BF)
        for e in (1, 2, 0):
            c4(p, e).start()

    def st4(p):
        for e in range(3):
            c4(p, e).wait_recv()
        rr, cc = cut(z)
        t = g[p, c, y, rr, cc].astype(F32) + r4[p, 0].astype(F32) + r4[p, 1].astype(F32) + r4[p, 2].astype(F32)
        r1[p, 0, rr, cc] = t.astype(BF)
        for e in (1, 2, 0):
            c5(p, e, z).start()

    def st5(p):
        for e in range(3):
            c5(p, e, zs[e]).wait_recv()
        c6(p, near).start()

    def st6(p):
        c6(p, away).wait_recv()

        @pl.when(p < nd)
        def down():
            store(p, od_hbm.at[pl.ds(p * R, R)]).start()

        @pl.when(jnp.logical_and(p >= nd, p < nd + nu))
        def up():
            store(p, ou_hbm.at[:, pl.ds(pl.multiple_of((p - nd) * C, C), C)]).start()

        @pl.when(p == nd + nu)
        def out():
            store(p, oo_hbm).start()

        @pl.when(p > nd + nu)
        def qkv():
            store(p, oq_hbm.at[:, pl.ds(pl.multiple_of((p - nd - nu - 1) * C, C), C)]).start()

    stages = [None, st1, st2, st3, st4, st5, st6]

    loads[0].wait()
    loads[1].wait()

    def down_block(i, carry):
        t = dg(a_view[i], dffn[...], 0, 0).astype(BF)
        for j in range(nd):
            g[j, i % 2, i // 2] = t[j * R:(j + 1) * R]
        return carry

    lax.fori_loop(0, nd, down_block, 0)
    pl.semaphore_wait(bar, 6)
    for p in range(nd):
        c1(p).start()
    loads[2].wait()
    loads[3].wait()

    def up_back(j, carry):
        at = (j // 3, slice(None), pl.ds(pl.multiple_of(j % 3 * 256, 256), 256))
        low = (dg(dffn[...], wd[pl.ds(pl.multiple_of(j * 256, 256), 256)], 1, 1) * slope[at].astype(F32)).astype(BF)
        b_view[at] = low
        part_up[:, pl.ds(pl.multiple_of(j * 256, 256), 256)] = fold(low.astype(F32))
        return carry

    lax.fori_loop(0, ff // 512, up_back, 0, unroll=UNROLL_BACK)
    st1(0)
    st1(1)
    lax.fori_loop(ff // 512, ff // 256, up_back, 0, unroll=UNROLL_BACK)
    k_load.start()
    v_load.start()
    for cp in loads[4:]:
        cp.wait()

    def row_block(p, t):
        for j in range(4):
            g[p, j % 2, j // 2] = t[j * R:(j + 1) * R].astype(BF)

    def up_block(i, carry):
        row_block(nd + i, dg(first[...], b_view[i], 0, 0))
        c1(nd + i).start()
        return carry

    lax.fori_loop(0, nu, up_block, 0)

    def rows_back():
        for b in range(d // 256):
            cols = pl.ds(b * 256, 256)
            dsum[:, cols] = dsec[:, cols] + sum(
                dg(b_view[j // 3, :, j % 3 * 256:(j % 3 + 1) * 256], wu[j, cols, :], 1, 1) for j in range(ff // 256))
        p_load.start()
        part[...] = jnp.zeros_like(part)
        chunk = 64
        gain = g1_v[...].reshape(1, d)

        def norm1_back(i, carry):
            r = pl.ds(pl.multiple_of(i * chunk, chunk), chunk)
            d_first, normed = dsum[r], normed1[r]
            part[1] += fold(d_first * normed)
            part[2] += fold(d_first)
            d_sum = scale1[r, :1] * norm_grad(d_first * gain, normed)
            dsum[r] = d_sum
            low = d_sum.astype(BF)
            datt[r] = low
            part[0] += fold(low.astype(F32))
            return carry

        lax.fori_loop(0, rows // chunk, norm1_back, 0)
        row_block(nd + nu, dg(ctx[...], datt[...], 0, 0))
        c1(nd + nu).start()
        dctx[...] = dg(datt[...], wo[...], 1, 1).astype(BF).reshape(seqs, quarter, d)
        k_load.wait()
        v_load.wait()
        p_load.wait()

    def unit(u, carry):
        s, p = u // pairs, u % pairs
        cols = pl.ds(pl.multiple_of(p * PAIR, PAIR), PAIR)
        qs = stack_heads(q[s, :, cols])
        ds = stack_heads(dctx[s, :, cols])
        low = prs[s, p]
        probs = low.astype(F32)
        t = probs * dg(v[s, :, cols], ds, 1, 1)
        d_raw = (t - probs * jnp.sum(t, axis=0, keepdims=True)).astype(BF)
        dv[s, :, cols] = dg(low, ds, 1, 0).astype(BF)
        dk[s, :, cols] = dg(d_raw, qs, 1, 0).astype(BF)
        dq[s, :, cols] = (unstack_heads(dg(k[s, :, cols], d_raw, 0, 0)) * 0.125).astype(BF)
        return carry

    def qkv_piece(i):
        cols = pl.ds(i * 2 * PAIR, 2 * PAIR)
        allt = toks[...].reshape(seqs * keys, d)
        ga = dg(toks[:, pl.ds(pl.multiple_of(n * quarter, quarter), quarter)].reshape(rows, d), dq[:, :, cols].reshape(rows, 2 * PAIR), 0, 0)
        gb = dg(allt, a_buf[:, cols], 0, 0)
        gc = dg(allt, b_buf[:, cols], 0, 0)
        left = left_lanes(R)
        p = nd + nu + 1 + i
        for e in range(4):
            rr = slice(e * R, (e + 1) * R)
            for j in range(2):
                sl = slice(j * PAIR, (j + 1) * PAIR)
                aj, bj, cj = ga[rr, sl], pltpu.roll(gb[rr, sl], HD, 1), gc[rr, sl]
                for t, val in enumerate((jnp.where(left, aj, bj), jnp.where(left, cj, aj), jnp.where(left, bj, cj))):
                    g[p, e % 2, e // 2, :, pl.ds((3 * j + t) * PAIR, PAIR)] = val.astype(BF)
        c1(p).start()

    cx1 = copy_to(dtok.at[:, 1 - c], x1, xs.at[0], xs.at[1], core_peer)
    cx2 = copy_to(dtok.at[1 - y, c], x2, xs.at[2], xs.at[3], y_peer)

    def input_part():
        def one(s, carry):
            t = dg(dk[s], wp[1], 1, 1) + dg(dv[s], wp[2], 1, 1)
            for e in range(4):
                dtok[e // 2, e % 2, s] = t[e * quarter:(e + 1) * quarter].astype(BF)
            return carry

        lax.fori_loop(0, seqs, one, 0)
        cx1.start()
        dsum[...] += dg(dq[...].reshape(rows, d), wp[0], 1, 1)

    def small(i, slot, dev):
        return copy_to(sbuf.at[i], srecv.at[slot], ss.at[slot], sq.at[slot], dev)

    def sums0():
        sbuf[0, 0:1] = jnp.sum(fold(dq[...].reshape(rows, d).astype(F32)), axis=0, keepdims=True)

        def add(s, acc):
            return acc + fold(dv[s].astype(F32))

        acc = lax.fori_loop(0, seqs, add, jnp.zeros((8, d), F32))
        sbuf[0, 1:2] = jnp.sum(acc, axis=0, keepdims=True)
        for i in range(3):
            sbuf[0, 2 + i:3 + i] = total(part[i])
        for i in range(nu):
            sbuf[0, 5 + i:6 + i] = total(part_up[:, i * d:(i + 1) * d])
        sbuf[0, 5 + nu:] = sums_ref[...]
        small(0, 0, core_peer).start()

    def sums1():
        small(0, 0, core_peer).wait_recv()
        sbuf[1] = sbuf[0] + srecv[0]
        small(1, 1, y_peer).start()

    def sums2():
        small(1, 1, y_peer).wait_recv()
        sbuf[2] = sbuf[1] + srecv[1]
        small(2, 2, x_peer).start()

    def sums3():
        small(2, 2, x_peer).wait_recv()
        sbuf[3] = sbuf[2] + srecv[2]
        for e in range(3):
            small(3, 3 + e, z_peers[e]).start()

    def add_x1():
        cx1.wait_recv()

        def add(i, carry):
            a, b = i // seqs, i % seqs
            dtok[a, c, b] = (dtok[a, c, b].astype(F32) + x1[a, b].astype(F32)).astype(BF)
            return carry

        lax.fori_loop(0, 2 * seqs, add, 0)

    units = seqs * pairs
    slots_of_units = -(-units // UNITS)
    extra = {3: [rows_back], 8: [lambda: qkv_piece(0), lambda: qkv_piece(1)],
             9: [lambda: qkv_piece(2), sums0, input_part], 10: [add_x1, sums1], 12: [sums2], 13: [cx2.start, sums3]}

    def slot(t, carry):
        for i in (6, 5, 4, 3, 2, 1):
            p = t - LAGS[i]

            @pl.when(jnp.logical_and(p >= 0, p < pieces))
            def run():
                stages[i](p)

        @pl.when(jnp.logical_and(t > 3, t <= 3 + slots_of_units))
        def attention():
            lo = (t - 4) * UNITS
            lax.fori_loop(lo, jnp.minimum(lo + UNITS, units), unit, 0)

        for at, todo in extra.items():
            @pl.when(t == at)
            def more():
                for f in todo:
                    f()
        return carry

    lax.fori_loop(3, pieces + LAGS[6], slot, 0)
    cx2.wait_recv()

    def out_x(i, carry):
        r = pl.ds(pl.multiple_of(i * quarter, quarter), quarter)
        x1[0, i] = (dsum[r] + dtok[y, c, i].astype(F32) + x2[i].astype(F32)).astype(BF)
        return carry

    lax.fori_loop(0, seqs, out_x, 0)
    din_out = pltpu.make_async_copy(x1.at[0], din_hbm, xs.at[4])
    din_out.start()
    for e in range(3):
        small(3, 3 + e, z_peers[e]).wait_recv()
    so_ref[...] = sbuf[3] + srecv[3] + srecv[4] + srecv[5]
    small(0, 0, core_peer).wait_send()
    small(1, 1, y_peer).wait_send()
    small(2, 2, x_peer).wait_send()
    for e in range(3):
        small(3, 3 + e, z_peers[e]).wait_send()
    cx1.wait_send()
    cx2.wait_send()

    def drain(p, carry):
        c1(p).wait_send()
        c2(p).wait_send()
        c3(p).wait_send()
        c6(p, near).wait_send()
        store(p, oo_hbm).wait()
        for e in range(3):
            c4(p, e).wait_send()
            c5(p, e, z).wait_send()
        return carry

    lax.fori_loop(0, pieces, drain, 0)
    din_out.wait()


def tail_part(act, dffn, wd, slope, first, wu, dsec, normed, scale, wo, ctx, q, toks, wp, k, v, probs, g1, sums):
    seqs, quarter, d = q.shape
    rows, keys = seqs * quarter, 4 * quarter
    R = d // 4
    nd = nu = act.shape[0]
    ff = nd * d
    n = nd + nu + 4
    h = R // 2
    all_rows = (6 + nu + sums.shape[0] - 1, d)
    vm, hbm = pl.BlockSpec(memory_space=V), pl.BlockSpec(memory_space=ANY)
    S = jax.ShapeDtypeStruct
    own, every, flat = (seqs, quarter, d), (seqs, keys, d), (rows, d)
    return pl.pallas_call(
        tail_kernel,
        out_shape=(S((nd * R, d), BF), S((R, nu * d), BF), S((R, d), BF), S((R, 3 * d), BF), S(own, BF),
                   S(all_rows, F32)),
        in_specs=[hbm] * 19,
        out_specs=(hbm, hbm, hbm, hbm, hbm, vm),
        scratch_shapes=[V((seqs * keys, d), BF), V((seqs * keys, d), BF), V(flat, BF), V(flat, BF), V(flat, BF),
                        V(flat, BF), V(flat, F32), V(every, BF), V(own, BF),
                        V((2 * seqs * keys, d), BF), V((seqs * (d // PAIR) * keys, 2 * quarter), BF), V((3, d, d), BF),
                        V(own, BF), V((2, 2) + own, BF), V(wo.shape, BF), V(flat, F32), V(flat, F32),
                        V((rows, 128), F32), V((3, 8, d), F32), V((8, ff), F32), V((d,), F32), V(sums.shape, F32),
                        V((n, 2, 2, R, d), BF), V((n, 2, R, d), BF), V((n, R, d), BF), V((n, h, d), BF),
                        V((n, 3, h // 2, d // 2), BF), V((4,) + all_rows, F32), V((6,) + all_rows, F32),
                        V((2,) + own, BF), V(own, BF)]
        + [DMA((n,))] * 6 + [DMA((n, 3))] * 4 + [DMA((n,))] * 3
        + [DMA((6,))] * 2 + [DMA((5,)), DMA((18 + ff // 256,))],
        name="tail_part",
        compiler_params=pltpu.CompilerParams(collective_id=2, has_side_effects=True, vmem_limit_bytes=63 << 20),
    )(act, dffn, wd, slope, first, wu, dsec, normed, scale, wo, ctx, q, toks, wp, k, v, probs,
      g1, sums)


def finish_kernel(d_h, u_h, o_h, q_h, sums_ref, fd, fu, fo, fq, qvb, outb, n1g, n1s, upb, downb, n2g, n2s,
                  low, full, ls, os_):
    R, C = low.shape[1:]
    nd, nu = d_h.shape[0] // R, u_h.shape[1] // C
    cut = lambda ref, i: ref.at[:, pl.ds(i * C, C)]
    ends = ([(d_h.at[pl.ds(i * R, R)], fd.at[pl.ds(i * R, R)]) for i in range(nd)]
            + [(cut(u_h, i), cut(fu, i)) for i in range(nu)] + [(o_h, fo)]
            + [(cut(q_h, i), cut(fq, i)) for i in range(3)])
    loads = [pltpu.make_async_copy(s, low.at[i], ls.at[i]) for i, (s, _) in enumerate(ends)]
    stores = [pltpu.make_async_copy(full.at[i], t, os_.at[i]) for i, (_, t) in enumerate(ends)]
    for cp in loads:
        cp.start()
    n = lax.axis_index("narrow")
    for i in range(4):
        @pl.when(n == i)
        def pick():
            at = slice(i * R, (i + 1) * R)
            qvb[...] = sums_ref[0:2, at]
            for j, ref in ((2, outb), (3, n1g), (4, n1s), (5 + nu, downb), (6 + nu, n2g), (7 + nu, n2s)):
                ref[...] = sums_ref[j:j + 1, at]
            upb[...] = sums_ref[5 + i:6 + i]
    for i, (a, b) in enumerate(zip(loads, stores)):
        a.wait()
        full[i] = low[i].astype(F32)
        b.start()
    for cp in stores:
        cp.wait()


def finish_part(down, up, out, qkv, sums):
    R, d = out.shape
    n = down.shape[0] // R + up.shape[1] // d + 4
    vm, hbm = pl.BlockSpec(memory_space=V), pl.BlockSpec(memory_space=ANY)
    S = jax.ShapeDtypeStruct
    shapes = [S(a.shape, F32) for a in (down, up, out, qkv)] + [S((2, R), F32)] + [S((1, R), F32)] * 3
    shapes += [S((1, d), F32)] + [S((1, R), F32)] * 3
    return pl.pallas_call(
        finish_kernel,
        out_shape=shapes,
        in_specs=[hbm] * 4 + [vm],
        out_specs=[hbm] * 4 + [vm] * 8,
        scratch_shapes=[V((n, R, d), BF), V((n, R, d), F32), DMA((n,)), DMA((n,))],
        name="finish_part",
        compiler_params=pltpu.CompilerParams(vmem_limit_bytes=60 << 20),
    )(down, up, out, qkv, sums)


def local(tokens, lengths, qkv_weight, qv_bias, out_weight, out_bias, norm1_gain, norm1_shift, up_weight, up_bias,
          down_weight, down_bias, norm2_gain, norm2_shift, cotangent):
    seqs, quarter, d = tokens.shape
    own, every = (seqs, quarter, d), (seqs, 4 * quarter, d)
    (toks, q, k, v, probs, wp, ctx, first, act, slope, output, dffn, dsec, normed, scale, sums) = front_part(
        tokens, lengths, qkv_weight, qv_bias, out_weight, out_bias, norm1_gain, norm1_shift, up_weight, up_bias,
        down_weight, down_bias, norm2_gain, norm2_shift, cotangent)
    down, up, out, qkv, input_grad, sums = tail_part(
        act, dffn, down_weight, slope, first, up_weight, dsec, normed, scale, out_weight, ctx, q, toks.reshape(every),
        wp, k.reshape(every), v.reshape(every), probs, norm1_gain, sums)
    wide = lax.axis_size("wide")
    if wide > 8:
        groups = [[j * 8 + i for j in range(wide // 8)] for i in range(8)]
        down, up, out, qkv = (
            lax.psum(a.astype(F32), "wide", axis_index_groups=groups).astype(BF) for a in (down, up, out, qkv))
        sums = lax.psum(sums, "wide", axis_index_groups=groups)
    down, up, out, qkv, qvb, outb, n1g, n1s, upb, downb, n2g, n2s = finish_part(down, up, out, qkv, sums)
    flat = lambda a: a.reshape(-1)
    return (output.reshape(own), input_grad, qkv, qvb, out, flat(outb), flat(n1g), flat(n1s), up, flat(upb), down,
            flat(downb), flat(n2g), flat(n2s))


def solution(mesh):
    return jax.shard_map(
        local,
        mesh=mesh,
        in_specs=(
            P("wide", "narrow", None),
            P("wide"),
            P(),
            P(),
            P(),
            P(),
            P(),
            P(),
            P(),
            P(),
            P(),
            P(),
            P(),
            P(),
            P("wide", "narrow", None),
        ),
        out_specs=(
            P("wide", "narrow", None),
            P("wide", "narrow", None),
            P("narrow", None),
            P(None, "narrow"),
            P("narrow", None),
            P("narrow"),
            P("narrow"),
            P("narrow"),
            P("narrow", None),
            P("narrow"),
            P("narrow", None),
            P("narrow"),
            P("narrow"),
            P("narrow"),
        ),
        check_vma=False,
    )
```

time: 206 us -> 177 us (0.86)
  local copies, waits for them, and re-layouts: 18.5 us -> 1.64 us
  Pallas kernels: 179 us -> 173 us
  other arithmetic: 6.7 us -> 1.29 us
    unnamed x61 -> x6, local copies, waits for them, and re-layouts: 15.2 us -> 1.64 us
    convert_element_type x4 -> x0, other arithmetic: 6.7 us -> none  [local(): grads = [a.astype(F32) for a in (down, up, out, qkv)]]
    pallas_call x2, Pallas kernels: 52.7 us -> 47.2 us  [the longest x1 41.5 us: front_part(): pl.pallas_call(front_kernel, out_shape=[S(keys, BF), S(own, BF), S(keys,...]
    dynamic_slice x5 -> x0, local copies, waits for them, and re-layouts: 3.25 us -> none  [the longest x3 1.92 us: local(): part = lambda r: lax.dynamic_slice_in_dim(sums[r], n * R, R, 0)]
where the time goes in v3:
time: 177 us; the launch traced here: 176 us
  Pallas kernels  173 us (98%)
    pallas_call x1, Pallas kernels, tail_part(): pl.pallas_call(tail_kernel, out_shape=(S((nd * R, d), BF), S((R, nu * d),...  126 us
    pallas_call x1, Pallas kernels, front_part(): pl.pallas_call(front_kernel, out_shape=[S(keys, BF), S(own, BF), S(keys,...  41.5 us
    pallas_call x1, Pallas kernels, finish_part(): pl.pallas_call(finish_kernel, out_shape=shapes, in_specs=[hbm] * 4 + [vm]...  5.61 us

profile of v3, /device:TPU:0, one launch (start us, length us, event | category | flops | bytes accessed | tf_op | source)
XLA Modules:
  0.0 176.3 jit_solution(2426244913891585512)
XLA Ops:
  0.6 41.5 %front_part.1 = (bf16[3,4,128,768]{3,2,1,0:T(8,128)(2,1)}, bf16[3,128,768]{2,1,0:T(8,128)(2,1)}, bf16[3,4,128,768]{3,2,1,0:T(8,128)(2,1)}, bf16[3,4,128,768]{3,2...) custom-call(s32[3]{0:T(128)} %len_ref.1, ...), custom_call_target="tpu_custom_call" | custom-call | tf_op jit(solution)/shard_map/front_part/pallas_call | solution.py:258
  42.2 125.5 %tail_part.1 = (bf16[768,768]{1,0:T(8,128)(2,1)}, bf16[192,3072]{1,0:T(8,128)(2,1)}, bf16[192,768]{1,0:T(8,128)(2,1)}, bf16[192,2304]{1,0:T(8,128)(2,1)}, bf16[3...) custom-call(bf16[4,384,768]{2,1,0:T(8,128)(2,1)} %get-tuple-element.49.act_h, bf16[384,768]{1,0:T(8,128)(2,1)} %get-tuple-element.50.dffn_h, ...), custom_call_target="tpu_custom_call" | custom-call | tf_op jit(solution)/shard_map/tail_part/pallas_call | solution.py:640
  167.7 0.0 copy-start
  167.8 0.0 copy-start.1
  167.8 5.6 %finish_part.1 = (f32[768,768]{1,0:T(8,128)}, f32[192,3072]{1,0:T(8,128)}, f32[192,768]{1,0:T(8,128)}, f32[192,2304]{1,0:T(8,128)}, f32[2,192]{1,0:T(2,128)}, /*...) custom-call(bf16[768,768]{1,0:T(8,128)(2,1)} %get-tuple-element.65.d, ...), custom_call_target="tpu_custom_call" | custom-call | tf_op jit(solution)/shard_map/finish_part/pallas_call | solution.py:698
  173.4 1.3 reduce
  174.7 0.0 copy-done
  174.7 0.8 copy.31
  175.5 0.0 copy-done.1
  175.5 0.8 copy.32
Async XLA Ops:
  167.7 6.9 %copy-start = (bf16[384,768]{1,0:T(8,128)(2,1)S(1)}, bf16[384,768]{1,0:T(8,128)(2,1)}, u32[]{:S(2)}) copy-start(bf16[384,768]{1,0:T(8,128)(2,1)} %get-tuple-element.48) | copy-start | bytes 1769476
  167.8 7.7 %copy-start.1 = (bf16[3,128,768]{2,1,0:T(8,128)(2,1)S(1)}, bf16[3,128,768]{2,1,0:T(8,128)(2,1)}, u32[]{:S(2)}) copy-start(bf16[3,128,768]{2,1,0:T(8,128)(2,1)} %get-tuple-element.97) | copy-start | bytes 1769476

commit v4 on v3

--- a/solution.py
+++ b/solution.py
@@ -19,8 +19,8 @@
 V = pltpu.VMEM
 DMA = pltpu.SemaphoreType.DMA
 ANY = pl.ANY
-UNROLL_ATT = 1
-UNROLL_UP = 1
+UNROLL_ATT = 6
+UNROLL_UP = 3
 
 
 def dg(a, b, ca, cb):
@@ -273,8 +273,9 @@
     )(lengths, tokens, cot, w, wo, wu, wd, qvb, bo, g1, s1, bu, bd, g2, s2)
 
 
-LAGS = (0, 1, 3, 4, 6, 7, 8)
-UNITS = 5
+LAGS = (0, 1, 3, 4, 5, 7, 11)
+UNITS = 4
+ORDER = (3, 1, 6, 4, 2, 5)
 UNROLL_BACK = 1
 
 
@@ -404,16 +405,23 @@
     loads[0].wait()
     loads[1].wait()
 
-    def down_block(i, carry):
-        t = dg(a_view[i], dffn[...], 0, 0).astype(BF)
-        for j in range(nd):
-            g[j, i % 2, i // 2] = t[j * R:(j + 1) * R]
-        return carry
-
-    lax.fori_loop(0, nd, down_block, 0)
-    pl.semaphore_wait(bar, 6)
-    for p in range(nd):
-        c1(p).start()
+    block = 256
+    for a in range(d // block):
+        def down_block(i, carry):
+            t = dg(a_view[i, :, a * block:(a + 1) * block], dffn[...], 0, 0).astype(BF)
+            for j in range(nd):
+                lo, hi = max(j * R, a * block), min((j + 1) * R, (a + 1) * block)
+                if lo < hi:
+                    g[j, i % 2, i // 2, lo - j * R:hi - j * R] = t[lo - a * block:hi - a * block]
+            return carry
+
+        lax.fori_loop(0, nd, down_block, 0)
+        if a == 0:
+            pl.semaphore_wait(bar, 6)
+        for p in range(a * block // R, nd if a == d // block - 1 else (a + 1) * block // R):
+            c1(p).start()
+    st1(0)
+    st1(1)
     loads[2].wait()
     loads[3].wait()
 
@@ -424,10 +432,7 @@
         part_up[:, pl.ds(pl.multiple_of(j * 256, 256), 256)] = fold(low.astype(F32))
         return carry
 
-    lax.fori_loop(0, ff // 512, up_back, 0, unroll=UNROLL_BACK)
-    st1(0)
-    st1(1)
-    lax.fori_loop(ff // 512, ff // 256, up_back, 0, unroll=UNROLL_BACK)
+    lax.fori_loop(0, ff // 256, up_back, 0, unroll=UNROLL_BACK)
     k_load.start()
     v_load.start()
     for cp in loads[4:]:
@@ -565,11 +570,11 @@
 
     units = seqs * pairs
     slots_of_units = -(-units // UNITS)
-    extra = {3: [rows_back], 8: [lambda: qkv_piece(0), lambda: qkv_piece(1)],
-             9: [lambda: qkv_piece(2), sums0, input_part], 10: [add_x1, sums1], 12: [sums2], 13: [cx2.start, sums3]}
+    extra = {3: [rows_back], 9: [lambda: qkv_piece(0), sums0], 10: [lambda: qkv_piece(1), sums1],
+             11: [lambda: qkv_piece(2), sums2], 12: [sums3], 13: [input_part], 14: [add_x1, cx2.start]}
 
     def slot(t, carry):
-        for i in (6, 5, 4, 3, 2, 1):
+        for i in ORDER:
             p = t - LAGS[i]
 
             @pl.when(jnp.logical_and(p >= 0, p < pieces))
@@ -678,8 +683,8 @@
             at = slice(i * R, (i + 1) * R)
             qvb[...] = sums_ref[0:2, at]
             for j, ref in ((2, outb), (3, n1g), (4, n1s), (5 + nu, downb), (6 + nu, n2g), (7 + nu, n2s)):
-                ref[...] = sums_ref[j:j + 1, at]
-            upb[...] = sums_ref[5 + i:6 + i]
+                ref[...] = sums_ref[j, at]
+            upb[...] = sums_ref[5 + i]
     for i, (a, b) in enumerate(zip(loads, stores)):
         a.wait()
         full[i] = low[i].astype(F32)
@@ -693,8 +698,8 @@
     n = down.shape[0] // R + up.shape[1] // d + 4
     vm, hbm = pl.BlockSpec(memory_space=V), pl.BlockSpec(memory_space=ANY)
     S = jax.ShapeDtypeStruct
-    shapes = [S(a.shape, F32) for a in (down, up, out, qkv)] + [S((2, R), F32)] + [S((1, R), F32)] * 3
-    shapes += [S((1, d), F32)] + [S((1, R), F32)] * 3
+    shapes = [S(a.shape, F32) for a in (down, up, out, qkv)] + [S((2, R), F32)] + [S((R,), F32)] * 3
+    shapes += [S((d,), F32)] + [S((R,), F32)] * 3
     return pl.pallas_call(
         finish_kernel,
         out_shape=shapes,
@@ -723,9 +728,8 @@
             lax.psum(a.astype(F32), "wide", axis_index_groups=groups).astype(BF) for a in (down, up, out, qkv))
         sums = lax.psum(sums, "wide", axis_index_groups=groups)
     down, up, out, qkv, qvb, outb, n1g, n1s, upb, downb, n2g, n2s = finish_part(down, up, out, qkv, sums)
-    flat = lambda a: a.reshape(-1)
-    return (output.reshape(own), input_grad, qkv, qvb, out, flat(outb), flat(n1g), flat(n1s), up, flat(upb), down,
-            flat(downb), flat(n2g), flat(n2s))
+    return (output.reshape(own), input_grad, qkv, qvb, out, outb, n1g, n1s, up, upb, down,
+            downb, n2g, n2s)
 
 
 def solution(mesh):

time: 177 us -> 164 us (0.927)
  Pallas kernels: 173 us -> 161 us
    pallas_call x1, Pallas kernels: 126 us -> 118 us  [tail_part(): pl.pallas_call(tail_kernel, out_shape=(S((nd * R, d), BF), S((R, nu * d),...]
    pallas_call x1, Pallas kernels: 41.5 us -> 37.7 us  [front_part(): pl.pallas_call(front_kernel, out_shape=[S(keys, BF), S(own, BF), S(keys,...]
where the time goes in v4:
time: 164 us; the launch traced here: 163 us
  Pallas kernels  161 us (98%)
    pallas_call x1, Pallas kernels, tail_part(): pl.pallas_call(tail_kernel, out_shape=(S((nd * R, d), BF), S((R, nu * d),...  118 us
    pallas_call x1, Pallas kernels, front_part(): pl.pallas_call(front_kernel, out_shape=[S(keys, BF), S(own, BF), S(keys,...  37.7 us
    pallas_call x1, Pallas kernels, finish_part(): pl.pallas_call(finish_kernel, out_shape=shapes, in_specs=[hbm] * 4 + [vm]...  5.61 us

profile of v4, /device:TPU:0, one launch (start us, length us, event | category | flops | bytes accessed | tf_op | source)
XLA Modules:
  0.0 163.4 jit_solution(16611722219970456157)
XLA Ops:
  0.6 37.7 %front_part.1 = (bf16[3,4,128,768]{3,2,1,0:T(8,128)(2,1)}, bf16[3,128,768]{2,1,0:T(8,128)(2,1)}, bf16[3,4,128,768]{3,2,1,0:T(8,128)(2,1)}, bf16[3,4,128,768]{3,2...) custom-call(s32[3]{0:T(128)} %len_ref.1, ...), custom_call_target="tpu_custom_call" | custom-call | tf_op jit(solution)/shard_map/front_part/pallas_call | solution.py:258
  38.3 117.8 %tail_part.1 = (bf16[768,768]{1,0:T(8,128)(2,1)}, bf16[192,3072]{1,0:T(8,128)(2,1)}, bf16[192,768]{1,0:T(8,128)(2,1)}, bf16[192,2304]{1,0:T(8,128)(2,1)}, bf16[3...) custom-call(bf16[4,384,768]{2,1,0:T(8,128)(2,1)} %get-tuple-element.49.act_h, bf16[384,768]{1,0:T(8,128)(2,1)} %get-tuple-element.50.dffn_h, ...), custom_call_target="tpu_custom_call" | custom-call | tf_op jit(solution)/shard_map/tail_part/pallas_call | solution.py:645
  156.1 0.0 copy-start
  156.2 0.0 copy-start.1
  156.2 5.6 %finish_part.1 = (f32[768,768]{1,0:T(8,128)}, f32[192,3072]{1,0:T(8,128)}, f32[192,768]{1,0:T(8,128)}, f32[192,2304]{1,0:T(8,128)}, f32[2,192]{1,0:T(2,128)}, /*...) custom-call(bf16[768,768]{1,0:T(8,128)(2,1)} %get-tuple-element.65.d, ...), custom_call_target="tpu_custom_call" | custom-call | tf_op jit(solution)/shard_map/finish_part/pallas_call | solution.py:703
  161.8 0.0 copy-done
  161.8 0.8 copy.31
  162.6 0.0 copy-done.1
  162.6 0.8 copy.32
Async XLA Ops:
  156.1 5.6 %copy-start = (bf16[384,768]{1,0:T(8,128)(2,1)S(1)}, bf16[384,768]{1,0:T(8,128)(2,1)}, u32[]{:S(2)}) copy-start(bf16[384,768]{1,0:T(8,128)(2,1)} %get-tuple-element.48) | copy-start | bytes 1769476
  156.2 6.5 %copy-start.1 = (bf16[3,128,768]{2,1,0:T(8,128)(2,1)S(1)}, bf16[3,128,768]{2,1,0:T(8,128)(2,1)}, u32[]{:S(2)}) copy-start(bf16[3,128,768]{2,1,0:T(8,128)(2,1)} %get-tuple-element.97) | copy-start | bytes 1769476

commit v5 on v4

v5 whole, which is shorter than its diff:
```python
import functools

import jax
import jax.numpy as jnp
from jax import lax
from jax.experimental import pallas as pl
from jax.experimental.pallas import tpu as pltpu
from jax.sharding import PartitionSpec as P

H = 12
HD = 64
PAIR = 2 * HD
epsilon = 1e-12
root_half = 0.7071067811865476
inv_root_two_pi = 0.3989422804014327
MESH = pl.DeviceIdType.MESH
F32 = jnp.float32
BF = jnp.bfloat16
V = pltpu.VMEM
DMA = pltpu.SemaphoreType.DMA
ANY = pl.ANY
UNROLL_ATT = 6
UNROLL_UP = 3


def dg(a, b, ca, cb):
    return lax.dot_general(a, b, (((ca,), (cb,)), ((), ())), preferred_element_type=F32)


def copy_to(src, dst, ss, rs, dev):
    return pltpu.make_async_remote_copy(
        src_ref=src, dst_ref=dst, send_sem=ss, recv_sem=rs, device_id=dev, device_id_type=MESH)


def left_lanes(rows):
    return lax.broadcasted_iota(jnp.int32, (rows, PAIR), 1) < HD


def stack_heads(x):
    left = left_lanes(x.shape[0])
    zero = jnp.zeros_like(x)
    return jnp.concatenate([jnp.where(left, x, zero), jnp.where(left, zero, x)], axis=0)


def unstack_heads(x_t):
    q = x_t.shape[1] // 2
    top = lax.broadcasted_iota(jnp.int32, (PAIR, q), 0) < HD
    return jnp.where(top, x_t[:, :q], x_t[:, q:]).T


def fold(x):
    return jnp.sum(x.reshape(x.shape[0] // 8, 8, x.shape[1]), axis=0)


def total(x):
    return jnp.sum(x, axis=0, keepdims=True)


def center_scale(v):
    center = v - jnp.mean(v, axis=-1, keepdims=True)
    scale = lax.rsqrt(jnp.mean(center * center, axis=-1, keepdims=True) + epsilon)
    return center * scale, scale


def norm_grad(g, normed):
    return g - jnp.mean(g, axis=-1, keepdims=True) - normed * jnp.mean(g * normed, axis=-1, keepdims=True)


LAGS = (0, 1, 3, 4, 5, 7, 11)
UNITS = 4
ORDER = (3, 1, 6, 4, 2, 5)
UNROLL_BACK = 1


def layer_kernel(len_ref, tok_h, cot_h, w_h, wo_h, wu_h, wd_h, qvb_h, bo_h, g1_h, s1_h, bu_h, bd_h, g2_h, s2_h,
                 out_h, od_hbm, ou_hbm, oo_hbm, oq_hbm, din_hbm, so_ref,
                 a_buf, b_buf, dtok, toks, k, v, q, pr, wp, ctx, low1, dffn, datt, dq, wo, dsum, first, normed1,
                 scale1, part, part2, part_up, qvb_ref, bo_v, g1_v, s1_v, bu_v, bd_v, g2_v, s2_v,
                 g, r1, r2, r3, r4, sbuf, srecv, x1, x2,
                 ls, cs, cr, ys, yr, fs, fr,
                 s1, q1, s2, q2, s3, q3, s4, q4, s5, q5, s6, q6, os_, ss, sq, xs):
    pieces, _, _, R, C = g.shape
    seqs, quarter, d = q.shape
    rows, keys, pairs = seqs * quarter, 4 * quarter, d // PAIR
    ff = wu_h.shape[1]
    nd = nu = ff // d
    h = R // 2
    hr, hc = h // 2, C // 2
    w, n = lax.axis_index("wide"), lax.axis_index("narrow")
    c, y, x, z = n % 2, n // 2, w % 2, (w // 2) % 4
    core_n, y_n = n + 1 - 2 * c, n + 2 - 4 * y
    far_n = core_n + 2 - 4 * y
    core_peer, y_peer, x_peer = (w, core_n), (w, y_n), (w + 1 - 2 * x, n)
    zs = [z + 1 - 2 * (z % 2), z + 2 - 4 * (z // 2), 3 - z]
    z_peers = [(w + 2 * (j - z), n) for j in zs]
    gp = g.reshape(pieces, d, d)
    a_view, b_view = a_buf.reshape(nd, rows, d), b_buf.reshape(nu, rows, d)
    dk, dv = a_buf.reshape(seqs, keys, d), b_buf.reshape(seqs, keys, d)
    slope = dtok.reshape(nd, rows, d)
    tok = datt.reshape(seqs, quarter, d)
    dctx = low1.reshape(seqs, quarter, d)
    out = dq.reshape(rows, d)
    cot = dffn.reshape(seqs, quarter, d)
    toks3, k3, v3 = (r.reshape(seqs, keys, d) for r in (toks, k, v))
    blocks = lambda ref, i: ref.at[:, i * d:(i + 1) * d]
    moves = [(tok_h, tok)] + [(blocks(w_h, i), gp.at[i]) for i in range(3)] + [
        (qvb_h, qvb_ref), (bo_h, bo_v), (g1_h, g1_v), (s1_h, s1_v), (bu_h, bu_v), (bd_h, bd_v), (g2_h, g2_v),
        (s2_h, s2_v), (wo_h, wo)] + [(blocks(wu_h, i), gp.at[nd + i]) for i in range(nu)] + [(cot_h, cot)] + [
        (wd_h.at[pl.ds(i * d, d)], gp.at[nd + nu + i]) for i in range(nd)]
    loads = [pltpu.make_async_copy(s, t, ls.at[i]) for i, (s, t) in enumerate(moves)]
    for cp in loads[:4]:
        cp.start()
    bar = pltpu.get_barrier_semaphore()
    for dev in [core_peer, y_peer, x_peer] + z_peers:
        pl.semaphore_signal(bar, inc=1, device_id=dev, device_id_type=MESH)
    pl.semaphore_wait(bar, 6)

    def send_y(s):
        return copy_to(tok_h.at[s], toks.at[s, n], ys.at[s], yr.at[s], y_peer)

    def send_core(s):
        return copy_to(tok_h.at[s], toks.at[s, n], cs.at[s], cr.at[s], core_peer)

    def forward_y(s):
        return copy_to(toks.at[s, y_n], toks.at[s, y_n], fs.at[s], fr.at[s], core_peer)

    for s in range(seqs):
        send_y(s).start()
        send_core(s).start()
    for cp in loads[4:]:
        cp.start()
    loads[0].wait()
    for s in range(seqs):
        toks[s, n] = tok[s]
    for cp in loads[1:4]:
        cp.wait()
    left = left_lanes(d)
    for p in range(pairs):
        t0, t1, t2 = (gp[p // 2, :, pl.ds((p % 2 * 3 + i) * PAIR, PAIR)].astype(F32) for i in range(3))
        cols = pl.ds(p * PAIR, PAIR)
        wp[0, :, cols] = jnp.where(left, t0, t1).astype(BF)
        wp[1, :, cols] = pltpu.roll(jnp.where(left, t2, t0), HD, 1).astype(BF)
        wp[2, :, cols] = jnp.where(left, t1, t2).astype(BF)
    for cp in loads[4:12]:
        cp.wait()
    bo_ref, g1_ref, s1_ref, bd_ref, g2_ref, s2_ref = (
        r[...].reshape(1, d) for r in (bo_v, g1_v, s1_v, bd_v, g2_v, s2_v))
    own = tok[...].reshape(rows, d)
    q[...] = ((dg(own, wp[0], 1, 0) + qvb_ref[0:1, :]).astype(BF) * 0.125).reshape(seqs, quarter, d)

    def project(s, half):
        blocks = pl.ds(2 * half, 2)
        x = toks[s, blocks].reshape(2 * quarter, d)
        k[s, blocks] = dg(x, wp[1], 1, 0).astype(BF).reshape(2, quarter, d)
        v[s, blocks] = (dg(x, wp[2], 1, 0) + qvb_ref[1:2, :]).astype(BF).reshape(2, quarter, d)

    for s in range(seqs):
        send_core(s).wait_recv()
    for s in range(seqs):
        project(s, y)

    def fetch_far(s):
        copy_to(toks.at[s, y_n], toks.at[s, y_n], ys.at[s], yr.at[s], y_peer).wait_recv()
        forward_y(s).start()

    fetch_far(0)
    for s in range(seqs):
        copy_to(toks.at[s, far_n], toks.at[s, far_n], fs.at[s], fr.at[s], core_peer).wait_recv()
        project(s, 1 - y)
        if s + 1 < seqs:
            fetch_far(s + 1)
        live = lax.broadcasted_iota(jnp.int32, (keys, 2 * quarter), 0) < len_ref[s]

        def unit(p, carry):
            cols = pl.ds(pl.multiple_of(p * PAIR, PAIR), PAIR)
            qs = stack_heads(q[s, :, cols])
            kp = k[s, :, :, cols].reshape(keys, PAIR)
            vp = v[s, :, :, cols].reshape(keys, PAIR)
            scores = jnp.where(live, dg(kp, qs, 1, 1), -1000000000.0)
            e = jnp.exp(scores - jnp.max(scores, axis=0, keepdims=True))
            probs = (e * (1.0 / jnp.sum(e, axis=0, keepdims=True))).astype(BF)
            pr[s, p] = probs
            ctx[s * quarter:(s + 1) * quarter, cols] = unstack_heads(dg(vp, probs, 0, 0)).astype(BF)
            return carry

        lax.fori_loop(0, pairs, unit, 0, unroll=UNROLL_ATT)

    part2[...] = jnp.zeros_like(part2)
    chunk = 64
    chunks = rows // chunk
    loads[12].wait()
    for b in range(d // 256):
        cols = pl.ds(b * 256, 256)
        dsum[:, cols] = (dg(ctx[...], wo[:, cols], 1, 0) + bo_ref[:, b * 256:(b + 1) * 256]
                        + tok[:, :, cols].reshape(rows, 256).astype(F32))

    def norm1(i, carry):
        r = pl.ds(pl.multiple_of(i * chunk, chunk), chunk)
        normed, scale = center_scale(dsum[r])
        x = normed * g1_ref + s1_ref
        normed1[r] = normed
        scale1[r] = jnp.broadcast_to(scale, (chunk, 128))
        first[r] = x
        low1[r] = x.astype(BF)
        return carry

    lax.fori_loop(0, chunks, norm1, 0)
    for cp in loads[13:13 + nu]:
        cp.wait()

    def up(j, carry):
        cols = pl.ds(pl.multiple_of(j * 256, 256), 256)
        at = (j // 3, slice(None), pl.ds(pl.multiple_of(j % 3 * 256, 256), 256))
        pre = dg(low1[...], gp[(nd + at[0],) + at[1:]], 1, 0) + bu_v[cols].reshape(1, 256)
        half = 0.5 + 0.5 * lax.erf(pre * root_half)
        a_view[at] = (pre * half).astype(BF)
        slope[at] = (half + pre * (jnp.exp(-0.5 * pre * pre) * inv_root_two_pi)).astype(BF)
        return carry

    lax.fori_loop(0, ff // 256, up, 0, unroll=UNROLL_UP)
    for cp in loads[13 + nu:]:
        cp.wait()
    for b in range(d // 256):
        cols = pl.ds(b * 256, 256)
        dsum[:, cols] = bd_ref[:, b * 256:(b + 1) * 256] + first[:, cols] + sum(
            dg(a_view[i], gp[nd + nu + i, :, cols], 1, 0) for i in range(ff // d))

    def norm2(i, carry):
        r = pl.ds(pl.multiple_of(i * chunk, chunk), chunk)
        normed, scale = center_scale(dsum[r])
        out[r] = (normed * g2_ref + s2_ref).astype(BF)
        s = i * chunk // quarter
        off = pl.multiple_of(i * chunk - s * quarter, chunk)
        pos = n * quarter + off + lax.broadcasted_iota(jnp.int32, (chunk, d), 0)
        d_out = jnp.where(pos < len_ref[s], cot[s, pl.ds(off, chunk)].astype(F32), 0.0)
        part2[1] += fold(d_out * normed)
        part2[2] += fold(d_out)
        d_second = scale * norm_grad(d_out * g2_ref, normed)
        dsum[r] = d_second
        low = d_second.astype(BF)
        dffn[r] = low
        part2[0] += fold(low.astype(F32))
        return carry

    lax.fori_loop(0, chunks, norm2, 0)
    out_store = pltpu.make_async_copy(out, out_h, xs.at[5])
    out_store.start()

    def cut(j):
        return (pl.ds(pl.multiple_of(x * h + (j // 2) * hr, 16), hr), pl.ds(pl.multiple_of((j % 2) * hc, 128), hc))

    near = pl.ds(pl.multiple_of(x * h, 16), h)
    away = pl.ds(pl.multiple_of((1 - x) * h, 16), h)

    def c1(p):
        return copy_to(g.at[p, 1 - c], r1.at[p], s1.at[p], q1.at[p], core_peer)

    def c2(p):
        return copy_to(g.at[p, c, 1 - y], r2.at[p], s2.at[p], q2.at[p], y_peer)

    def c3(p):
        return copy_to(g.at[p, c, y, away], r3.at[p], s3.at[p], q3.at[p], x_peer)

    def c4(p, e):
        rr, cc = cut(zs[e])
        return copy_to(g.at[p, c, y, rr, cc], r4.at[p, e], s4.at[p, e], q4.at[p, e], z_peers[e])

    def c5(p, e, j):
        rr, cc = cut(j)
        return copy_to(r1.at[p, 0, rr, cc], r1.at[p, 0, rr, cc], s5.at[p, e], q5.at[p, e], z_peers[e])

    def c6(p, rr):
        return copy_to(r1.at[p, 0, rr], r1.at[p, 0, rr], s6.at[p], q6.at[p], x_peer)

    def store(p, dst):
        return pltpu.make_async_copy(r1.at[p, 0], dst, os_.at[p])

    def st1(p):
        c1(p).wait_recv()
        g[p, c] = (g[p, c].astype(F32) + r1[p].astype(F32)).astype(BF)
        c2(p).start()

    def st2(p):
        c2(p).wait_recv()
        g[p, c, y] = (g[p, c, y].astype(F32) + r2[p].astype(F32)).astype(BF)
        c3(p).start()

    def st3(p):
        c3(p).wait_recv()
        g[p, c, y, near] = (g[p, c, y, near].astype(F32) + r3[p].astype(F32)).astype(BF)
        for e in (1, 2, 0):
            c4(p, e).start()

    def st4(p):
        for e in range(3):
            c4(p, e).wait_recv()
        rr, cc = cut(z)
        t = g[p, c, y, rr, cc].astype(F32) + r4[p, 0].astype(F32) + r4[p, 1].astype(F32) + r4[p, 2].astype(F32)
        r1[p, 0, rr, cc] = t.astype(BF)
        for e in (1, 2, 0):
            c5(p, e, z).start()

    def st5(p):
        for e in range(3):
            c5(p, e, zs[e]).wait_recv()
        c6(p, near).start()

    def st6(p):
        c6(p, away).wait_recv()

        @pl.when(p < nd)
        def down():
            store(p, od_hbm.at[pl.ds(p * R, R)]).start()

        @pl.when(jnp.logical_and(p >= nd, p < nd + nu))
        def up():
            store(p, ou_hbm.at[:, pl.ds(pl.multiple_of((p - nd) * C, C), C)]).start()

        @pl.when(p == nd + nu)
        def out():
            store(p, oo_hbm).start()

        @pl.when(p > nd + nu)
        def qkv():
            store(p, oq_hbm.at[:, pl.ds(pl.multiple_of((p - nd - nu - 1) * C, C), C)]).start()

    stages = [None, st1, st2, st3, st4, st5, st6]

    block = 256
    for a in range(d // block):
        def down_block(i, carry):
            t = dg(a_view[i, :, a * block:(a + 1) * block], dffn[...], 0, 0).astype(BF)
            for j in range(nd):
                lo, hi = max(j * R, a * block), min((j + 1) * R, (a + 1) * block)
                if lo < hi:
                    g[j, i % 2, i // 2, lo - j * R:hi - j * R] = t[lo - a * block:hi - a * block]
            return carry

        lax.fori_loop(0, nd, down_block, 0)
        for p in range(a * block // R, nd if a == d // block - 1 else (a + 1) * block // R):
            c1(p).start()
    st1(0)
    st1(1)

    def up_back(j, carry):
        at = (j // 3, slice(None), pl.ds(pl.multiple_of(j % 3 * 256, 256), 256))
        low = (dg(dffn[...], gp[nd + nu + j // 3, pl.ds(pl.multiple_of(j % 3 * 256, 256), 256)], 1, 1) * slope[at].astype(F32)).astype(BF)
        b_view[at] = low
        part_up[:, pl.ds(pl.multiple_of(j * 256, 256), 256)] = fold(low.astype(F32))
        return carry

    lax.fori_loop(0, ff // 256, up_back, 0, unroll=UNROLL_BACK)
    for b in range(d // 256):
        cols = pl.ds(b * 256, 256)
        dsum[:, cols] += sum(dg(b_view[i], gp[nd + i, cols, :], 1, 1) for i in range(nu))

    def row_block(p, t):
        for j in range(4):
            g[p, j % 2, j // 2] = t[j * R:(j + 1) * R].astype(BF)

    def up_block(i, carry):
        row_block(nd + i, dg(low1[...], b_view[i], 0, 0))
        c1(nd + i).start()
        return carry

    lax.fori_loop(0, nu, up_block, 0)

    def rows_back():
        part[...] = jnp.zeros_like(part)
        chunk = 64
        gain = g1_v[...].reshape(1, d)

        def norm1_back(i, carry):
            r = pl.ds(pl.multiple_of(i * chunk, chunk), chunk)
            d_first, normed = dsum[r], normed1[r]
            part[1] += fold(d_first * normed)
            part[2] += fold(d_first)
            d_sum = scale1[r, :1] * norm_grad(d_first * gain, normed)
            dsum[r] = d_sum
            low = d_sum.astype(BF)
            datt[r] = low
            part[0] += fold(low.astype(F32))
            return carry

        lax.fori_loop(0, rows // chunk, norm1_back, 0)
        row_block(nd + nu, dg(ctx[...], datt[...], 0, 0))
        c1(nd + nu).start()
        dctx[...] = dg(datt[...], wo[...], 1, 1).astype(BF).reshape(seqs, quarter, d)
        out_store.wait()

    def unit(u, carry):
        s, p = u // pairs, u % pairs
        cols = pl.ds(pl.multiple_of(p * PAIR, PAIR), PAIR)
        qs = stack_heads(q[s, :, cols])
        ds = stack_heads(dctx[s, :, cols])
        low = pr[s, p]
        probs = low.astype(F32)
        t = probs * dg(v3[s, :, cols], ds, 1, 1)
        d_raw = (t - probs * jnp.sum(t, axis=0, keepdims=True)).astype(BF)
        dv[s, :, cols] = dg(low, ds, 1, 0).astype(BF)
        dk[s, :, cols] = dg(d_raw, qs, 1, 0).astype(BF)
        dq[s, :, cols] = (unstack_heads(dg(k3[s, :, cols], d_raw, 0, 0)) * 0.125).astype(BF)
        return carry

    def qkv_piece(i):
        cols = pl.ds(i * 2 * PAIR, 2 * PAIR)
        allt = toks3[...].reshape(seqs * keys, d)
        ga = dg(toks3[:, pl.ds(pl.multiple_of(n * quarter, quarter), quarter)].reshape(rows, d), dq[:, :, cols].reshape(rows, 2 * PAIR), 0, 0)
        gb = dg(allt, a_buf[:, cols], 0, 0)
        gc = dg(allt, b_buf[:, cols], 0, 0)
        left = left_lanes(R)
        p = nd + nu + 1 + i
        for e in range(4):
            rr = slice(e * R, (e + 1) * R)
            for j in range(2):
                sl = slice(j * PAIR, (j + 1) * PAIR)
                aj, bj, cj = ga[rr, sl], pltpu.roll(gb[rr, sl], HD, 1), gc[rr, sl]
                for t, val in enumerate((jnp.where(left, aj, bj), jnp.where(left, cj, aj), jnp.where(left, bj, cj))):
                    g[p, e % 2, e // 2, :, pl.ds((3 * j + t) * PAIR, PAIR)] = val.astype(BF)
        c1(p).start()

    cx1 = copy_to(dtok.at[:, 1 - c], x1, xs.at[0], xs.at[1], core_peer)
    cx2 = copy_to(dtok.at[1 - y, c], x2, xs.at[2], xs.at[3], y_peer)

    def input_part():
        def one(s, carry):
            t = dg(dk[s], wp[1], 1, 1) + dg(dv[s], wp[2], 1, 1)
            for e in range(4):
                dtok[e // 2, e % 2, s] = t[e * quarter:(e + 1) * quarter].astype(BF)
            return carry

        lax.fori_loop(0, seqs, one, 0)
        cx1.start()
        dsum[...] += dg(dq[...].reshape(rows, d), wp[0], 1, 1)

    def small(i, slot, dev):
        return copy_to(sbuf.at[i], srecv.at[slot], ss.at[slot], sq.at[slot], dev)

    def sums0():
        sbuf[0, 0:1] = jnp.sum(fold(dq[...].reshape(rows, d).astype(F32)), axis=0, keepdims=True)

        def add(s, acc):
            return acc + fold(dv[s].astype(F32))

        acc = lax.fori_loop(0, seqs, add, jnp.zeros((8, d), F32))
        sbuf[0, 1:2] = jnp.sum(acc, axis=0, keepdims=True)
        for i in range(3):
            sbuf[0, 2 + i:3 + i] = total(part[i])
        for i in range(nu):
            sbuf[0, 5 + i:6 + i] = total(part_up[:, i * d:(i + 1) * d])
        for i in range(3):
            sbuf[0, 5 + nu + i:6 + nu + i] = total(part2[i])
        small(0, 0, core_peer).start()

    def sums1():
        small(0, 0, core_peer).wait_recv()
        sbuf[1] = sbuf[0] + srecv[0]
        small(1, 1, y_peer).start()

    def sums2():
        small(1, 1, y_peer).wait_recv()
        sbuf[2] = sbuf[1] + srecv[1]
        small(2, 2, x_peer).start()

    def sums3():
        small(2, 2, x_peer).wait_recv()
        sbuf[3] = sbuf[2] + srecv[2]
        for e in range(3):
            small(3, 3 + e, z_peers[e]).start()

    def add_x1():
        cx1.wait_recv()

        def add(i, carry):
            a, b = i // seqs, i % seqs
            dtok[a, c, b] = (dtok[a, c, b].astype(F32) + x1[a, b].astype(F32)).astype(BF)
            return carry

        lax.fori_loop(0, 2 * seqs, add, 0)

    units = seqs * pairs
    slots_of_units = -(-units // UNITS)
    extra = {3: [rows_back], 9: [lambda: qkv_piece(0), sums0], 10: [lambda: qkv_piece(1), sums1],
             11: [lambda: qkv_piece(2), sums2], 12: [sums3], 13: [input_part], 14: [add_x1, cx2.start]}

    def slot(t, carry):
        for i in ORDER:
            p = t - LAGS[i]

            @pl.when(jnp.logical_and(p >= 0, p < pieces))
            def run():
                stages[i](p)

        @pl.when(jnp.logical_and(t > 3, t <= 3 + slots_of_units))
        def attention():
            lo = (t - 4) * UNITS
            lax.fori_loop(lo, jnp.minimum(lo + UNITS, units), unit, 0)

        for at, todo in extra.items():
            @pl.when(t == at)
            def more():
                for f in todo:
                    f()
        return carry

    lax.fori_loop(3, pieces + LAGS[6], slot, 0)
    cx2.wait_recv()

    def out_x(i, carry):
        r = pl.ds(pl.multiple_of(i * quarter, quarter), quarter)
        x1[0, i] = (dsum[r] + dtok[y, c, i].astype(F32) + x2[i].astype(F32)).astype(BF)
        return carry

    lax.fori_loop(0, seqs, out_x, 0)
    din_out = pltpu.make_async_copy(x1.at[0], din_hbm, xs.at[4])
    din_out.start()
    for e in range(3):
        small(3, 3 + e, z_peers[e]).wait_recv()
    so_ref[...] = sbuf[3] + srecv[3] + srecv[4] + srecv[5]
    small(0, 0, core_peer).wait_send()
    small(1, 1, y_peer).wait_send()
    small(2, 2, x_peer).wait_send()
    for e in range(3):
        small(3, 3 + e, z_peers[e]).wait_send()
    cx1.wait_send()
    cx2.wait_send()

    def drain(p, carry):
        c1(p).wait_send()
        c2(p).wait_send()
        c3(p).wait_send()
        c6(p, near).wait_send()
        store(p, oo_hbm).wait()
        for e in range(3):
            c4(p, e).wait_send()
            c5(p, e, z).wait_send()
        return carry

    lax.fori_loop(0, pieces, drain, 0)
    for s in range(seqs):
        send_y(s).wait_send()
        send_core(s).wait_send()
        forward_y(s).wait_send()
    din_out.wait()


def layer_part(tokens, lengths, w, qvb, wo, bo, g1, s1, wu, bu, wd, bd, g2, s2, cot):
    seqs, quarter, d = tokens.shape
    rows, keys, pairs, ff = seqs * quarter, 4 * quarter, d // PAIR, wu.shape[1]
    R = d // 4
    nd = nu = ff // d
    n = nd + nu + 4
    h = R // 2
    all_rows = (8 + nu, d)
    vm, hbm = pl.BlockSpec(memory_space=V), pl.BlockSpec(memory_space=ANY)
    S = jax.ShapeDtypeStruct
    own, every, flat = (seqs, quarter, d), (seqs, 4, quarter, d), (rows, d)
    row = V((d,), F32)
    return pl.pallas_call(
        layer_kernel,
        out_shape=(S(flat, BF), S((nd * R, d), BF), S((R, nu * d), BF), S((R, d), BF), S((R, 3 * d), BF), S(own, BF),
                   S(all_rows, F32)),
        in_specs=[pl.BlockSpec(memory_space=pltpu.SMEM)] + [hbm] * 14,
        out_specs=[hbm] * 6 + [vm],
        scratch_shapes=[V((seqs * keys, d), BF), V((seqs * keys, d), BF), V((2, 2) + own, BF), V(every, BF), V(every, BF),
                        V(every, BF), V(own, BF), V((seqs, pairs, keys, 2 * quarter), BF), V((3, d, d), BF),
                        V(flat, BF), V(flat, BF), V(flat, BF), V(flat, BF), V(own, BF), V(wo.shape, BF),
                        V(flat, F32), V(flat, F32), V(flat, F32), V((rows, 128), F32), V((3, 8, d), F32),
                        V((3, 8, d), F32), V((8, ff), F32), V((2, d), F32), row, row, row, V((ff,), F32), row, row, row,
                        V((n, 2, 2, R, d), BF), V((n, 2, R, d), BF), V((n, R, d), BF), V((n, h, d), BF),
                        V((n, 3, h // 2, d // 2), BF), V((4,) + all_rows, F32), V((6,) + all_rows, F32),
                        V((2,) + own, BF), V(own, BF), DMA((14 + nd + nu,))]
        + [DMA((seqs,))] * 6 + [DMA((n,))] * 6 + [DMA((n, 3))] * 4 + [DMA((n,))] * 3
        + [DMA((6,))] * 2 + [DMA((6,))],
        name="layer_part",
        compiler_params=pltpu.CompilerParams(collective_id=1, has_side_effects=True, vmem_limit_bytes=63 << 20),
    )(lengths, tokens, cot, w, wo, wu, wd, qvb, bo, g1, s1, bu, bd, g2, s2)


def finish_kernel(d_h, u_h, o_h, q_h, out_h, din_h, sums_ref, fd, fu, fo, fq, fout, fdin, qvb, outb, n1g, n1s, upb, downb, n2g, n2s,
                  low, full, rows, ls, os_):
    R, C = low.shape[1:]
    nd, nu = d_h.shape[0] // R, u_h.shape[1] // C
    cut = lambda ref, i: ref.at[:, pl.ds(i * C, C)]
    ends = ([(d_h.at[pl.ds(i * R, R)], fd.at[pl.ds(i * R, R)]) for i in range(nd)]
            + [(cut(u_h, i), cut(fu, i)) for i in range(nu)] + [(o_h, fo)]
            + [(cut(q_h, i), cut(fq, i)) for i in range(3)])
    loads = [pltpu.make_async_copy(s, low.at[i], ls.at[i]) for i, (s, _) in enumerate(ends)]
    stores = [pltpu.make_async_copy(full.at[i], t, os_.at[i]) for i, (_, t) in enumerate(ends)]
    pieces = len(ends)
    loads += [pltpu.make_async_copy(s, rows.at[i], ls.at[pieces + i]) for i, s in enumerate((out_h, din_h))]
    stores += [pltpu.make_async_copy(rows.at[i], t, os_.at[pieces + i]) for i, t in enumerate((fout, fdin))]
    for cp in loads:
        cp.start()
    n = lax.axis_index("narrow")
    for i in range(4):
        @pl.when(n == i)
        def pick():
            at = slice(i * R, (i + 1) * R)
            qvb[...] = sums_ref[0:2, at]
            for j, ref in ((2, outb), (3, n1g), (4, n1s), (5 + nu, downb), (6 + nu, n2g), (7 + nu, n2s)):
                ref[...] = sums_ref[j, at]
            upb[...] = sums_ref[5 + i]
    for i, (a, b) in enumerate(zip(loads, stores)):
        a.wait()
        if i < pieces:
            full[i] = low[i].astype(F32)
        b.start()
    for cp in stores:
        cp.wait()


def finish_part(down, up, out, qkv, output, input_grad, sums):
    R, d = out.shape
    n = down.shape[0] // R + up.shape[1] // d + 4
    vm, hbm = pl.BlockSpec(memory_space=V), pl.BlockSpec(memory_space=ANY)
    S = jax.ShapeDtypeStruct
    shapes = [S(a.shape, F32) for a in (down, up, out, qkv)] + [S(output.shape, BF)] * 2 + [S((2, R), F32)] + [S((R,), F32)] * 3
    shapes += [S((d,), F32)] + [S((R,), F32)] * 3
    return pl.pallas_call(
        finish_kernel,
        out_shape=shapes,
        in_specs=[hbm] * 6 + [vm],
        out_specs=[hbm] * 6 + [vm] * 8,
        scratch_shapes=[V((n, R, d), BF), V((n, R, d), F32), V((2,) + output.shape, BF), DMA((n + 2,)), DMA((n + 2,))],
        name="finish_part",
        compiler_params=pltpu.CompilerParams(vmem_limit_bytes=60 << 20),
    )(down, up, out, qkv, output, input_grad, sums)


def local(tokens, lengths, qkv_weight, qv_bias, out_weight, out_bias, norm1_gain, norm1_shift, up_weight, up_bias,
          down_weight, down_bias, norm2_gain, norm2_shift, cotangent):
    own = tokens.shape
    output, down, up, out, qkv, input_grad, sums = layer_part(
        tokens, lengths, qkv_weight, qv_bias, out_weight, out_bias, norm1_gain, norm1_shift, up_weight, up_bias,
        down_weight, down_bias, norm2_gain, norm2_shift, cotangent)
    wide = lax.axis_size("wide")
    if wide > 8:
        groups = [[j * 8 + i for j in range(wide // 8)] for i in range(8)]
        down, up, out, qkv = (
            lax.psum(a.astype(F32), "wide", axis_index_groups=groups).astype(BF) for a in (down, up, out, qkv))
        sums = lax.psum(sums, "wide", axis_index_groups=groups)
    down, up, out, qkv, output, input_grad, qvb, outb, n1g, n1s, upb, downb, n2g, n2s = finish_part(
        down, up, out, qkv, output, input_grad.reshape(output.shape), sums)
    return (output.reshape(own), input_grad.reshape(own), qkv, qvb, out, outb, n1g, n1s, up, upb, down, downb, n2g, n2s)


def solution(mesh):
    return jax.shard_map(
        local,
        mesh=mesh,
        in_specs=(
            P("wide", "narrow", None),
            P("wide"),
            P(),
            P(),
            P(),
            P(),
            P(),
            P(),
            P(),
            P(),
            P(),
            P(),
            P(),
            P(),
            P("wide", "narrow", None),
        ),
        out_specs=(
            P("wide", "narrow", None),
            P("wide", "narrow", None),
            P("narrow", None),
            P(None, "narrow"),
            P("narrow", None),
            P("narrow"),
            P("narrow"),
            P("narrow"),
            P("narrow", None),
            P("narrow"),
            P("narrow", None),
            P("narrow"),
            P("narrow"),
            P("narrow"),
        ),
        check_vma=False,
    )
```

time: 164 us -> 159 us (0.970)
  Pallas kernels: 161 us -> 158 us
    pallas_call x3 -> x2, Pallas kernels: 161 us -> 158 us  [the longest x1 152 us: layer_part(): pl.pallas_call(layer_kernel, out_shape=(S(flat, BF), S((nd * R, d), BF),...]
    unnamed x6 -> x0, local copies, waits for them, and re-layouts: 1.64 us -> none
where the time goes in v5:
time: 159 us
  Pallas kernels  158 us (99%)
    pallas_call x1, Pallas kernels, layer_part(): pl.pallas_call(layer_kernel, out_shape=(S(flat, BF), S((nd * R, d), BF),...  152 us
    pallas_call x1, Pallas kernels, finish_part(): pl.pallas_call(finish_kernel, out_shape=shapes, in_specs=[hbm] * 6 + [vm]...  5.91 us

profile of v5, /device:TPU:0, one launch (start us, length us, event | category | flops | bytes accessed | tf_op | source)
XLA Modules:
  0.0 158.5 jit_solution(9012999758301269605)
XLA Ops:
  0.7 151.8 %layer_part.1 = (bf16[384,768]{1,0:T(8,128)(2,1)}, bf16[768,768]{1,0:T(8,128)(2,1)}, bf16[192,3072]{1,0:T(8,128)(2,1)}, bf16[192,768]{1,0:T(8,128)(2,1)}, bf16[1...) custom-call(s32[3]{0:T(128)} %len_ref.1, bf16[3,128,768]{2,1,0:T(8,128)(2,1)} %tok_h.1, ...), custom_call_target="tpu_custom_call" | custom-call | tf_op jit(solution)/shard_map/layer_part/pallas_call | solution.py:559
  152.5 5.9 %finish_part.1 = (f32[768,768]{1,0:T(8,128)}, f32[192,3072]{1,0:T(8,128)}, f32[192,768]{1,0:T(8,128)}, f32[192,2304]{1,0:T(8,128)}, bf16[384,768]{1,0:T(8,128)(2...) custom-call(bf16[768,768]{1,0:T(8,128)(2,1)} %get-tuple-element.35.d, ...), custom_call_target="tpu_custom_call" | custom-call | tf_op jit(solution)/shard_map/finish_part/pallas_call | solution.py:620

commit v6 on v5

--- a/solution.py
+++ b/solution.py
@@ -68,15 +68,15 @@
 
 LAGS = (0, 1, 3, 4, 5, 7, 11)
 UNITS = 4
-ORDER = (3, 1, 6, 4, 2, 5)
+ORDER = (3, 2, 5, 4, 6, 1)
 UNROLL_BACK = 1
 
 
 def layer_kernel(len_ref, tok_h, cot_h, w_h, wo_h, wu_h, wd_h, qvb_h, bo_h, g1_h, s1_h, bu_h, bd_h, g2_h, s2_h,
-                 out_h, od_hbm, ou_hbm, oo_hbm, oq_hbm, din_hbm, so_ref,
+                 out_h, od_hbm, ou_hbm, oo_hbm, oq_hbm, din_hbm, so_hbm,
                  a_buf, b_buf, dtok, toks, k, v, q, pr, wp, ctx, low1, dffn, datt, dq, wo, dsum, first, normed1,
                  scale1, part, part2, part_up, qvb_ref, bo_v, g1_v, s1_v, bu_v, bd_v, g2_v, s2_v,
-                 g, r1, r2, r3, r4, sbuf, srecv, x1, x2,
+                 g, r1, r2, r3, r4, sbuf, srecv, so_v, x1, x2,
                  ls, cs, cr, ys, yr, fs, fr,
                  s1, q1, s2, q2, s3, q3, s4, q4, s5, q5, s6, q6, os_, ss, sq, xs):
     pieces, _, _, R, C = g.shape
@@ -339,7 +339,8 @@
         lax.fori_loop(0, nd, down_block, 0)
         for p in range(a * block // R, nd if a == d // block - 1 else (a + 1) * block // R):
             c1(p).start()
-    st1(0)
+        if a == 1:
+            st1(0)
     st1(1)
 
     def up_back(j, carry):
@@ -468,6 +469,14 @@
         for e in range(3):
             small(3, 3 + e, z_peers[e]).start()
 
+    so_store = pltpu.make_async_copy(so_v, so_hbm, xs.at[6])
+
+    def sums4():
+        for e in range(3):
+            small(3, 3 + e, z_peers[e]).wait_recv()
+        so_v[...] = sbuf[3] + srecv[3] + srecv[4] + srecv[5]
+        so_store.start()
+
     def add_x1():
         cx1.wait_recv()
 
@@ -480,8 +489,17 @@
 
     units = seqs * pairs
     slots_of_units = -(-units // UNITS)
-    extra = {3: [rows_back], 9: [lambda: qkv_piece(0), sums0], 10: [lambda: qkv_piece(1), sums1],
-             11: [lambda: qkv_piece(2), sums2], 12: [sums3], 13: [input_part], 14: [add_x1, cx2.start]}
+    extra = {3: [rows_back], 9: [lambda: qkv_piece(0)], 10: [lambda: qkv_piece(1), lambda: qkv_piece(2), sums0],
+             11: [input_part, sums1], 12: [add_x1, sums2], 13: [cx2.start, sums3], 16: [sums4]}
+
+    def drain(p):
+        c1(p).wait_send()
+        c2(p).wait_send()
+        c3(p).wait_send()
+        c6(p, near).wait_send()
+        for e in range(3):
+            c4(p, e).wait_send()
+            c5(p, e, z).wait_send()
 
     def slot(t, carry):
         for i in ORDER:
@@ -501,6 +519,12 @@
             def more():
                 for f in todo:
                     f()
+
+        old = t - LAGS[5] - 3
+
+        @pl.when(jnp.logical_and(old >= 0, old < pieces))
+        def finished():
+            drain(old)
         return carry
 
     lax.fori_loop(3, pieces + LAGS[6], slot, 0)
@@ -514,9 +538,6 @@
     lax.fori_loop(0, seqs, out_x, 0)
     din_out = pltpu.make_async_copy(x1.at[0], din_hbm, xs.at[4])
     din_out.start()
-    for e in range(3):
-        small(3, 3 + e, z_peers[e]).wait_recv()
-    so_ref[...] = sbuf[3] + srecv[3] + srecv[4] + srecv[5]
     small(0, 0, core_peer).wait_send()
     small(1, 1, y_peer).wait_send()
     small(2, 2, x_peer).wait_send()
@@ -525,23 +546,17 @@
     cx1.wait_send()
     cx2.wait_send()
 
-    def drain(p, carry):
-        c1(p).wait_send()
-        c2(p).wait_send()
-        c3(p).wait_send()
-        c6(p, near).wait_send()
+    def stored(p, carry):
         store(p, oo_hbm).wait()
-        for e in range(3):
-            c4(p, e).wait_send()
-            c5(p, e, z).wait_send()
-        return carry
-
-    lax.fori_loop(0, pieces, drain, 0)
+        return carry
+
+    lax.fori_loop(0, pieces, stored, 0)
     for s in range(seqs):
         send_y(s).wait_send()
         send_core(s).wait_send()
         forward_y(s).wait_send()
     din_out.wait()
+    so_store.wait()
 
 
 def layer_part(tokens, lengths, w, qvb, wo, bo, g1, s1, wu, bu, wd, bd, g2, s2, cot):
@@ -561,7 +576,7 @@
         out_shape=(S(flat, BF), S((nd * R, d), BF), S((R, nu * d), BF), S((R, d), BF), S((R, 3 * d), BF), S(own, BF),
                    S(all_rows, F32)),
         in_specs=[pl.BlockSpec(memory_space=pltpu.SMEM)] + [hbm] * 14,
-        out_specs=[hbm] * 6 + [vm],
+        out_specs=[hbm] * 7,
         scratch_shapes=[V((seqs * keys, d), BF), V((seqs * keys, d), BF), V((2, 2) + own, BF), V(every, BF), V(every, BF),
                         V(every, BF), V(own, BF), V((seqs, pairs, keys, 2 * quarter), BF), V((3, d, d), BF),
                         V(flat, BF), V(flat, BF), V(flat, BF), V(flat, BF), V(own, BF), V(wo.shape, BF),
@@ -569,16 +584,17 @@
                         V((3, 8, d), F32), V((8, ff), F32), V((2, d), F32), row, row, row, V((ff,), F32), row, row, row,
                         V((n, 2, 2, R, d), BF), V((n, 2, R, d), BF), V((n, R, d), BF), V((n, h, d), BF),
                         V((n, 3, h // 2, d // 2), BF), V((4,) + all_rows, F32), V((6,) + all_rows, F32),
-                        V((2,) + own, BF), V(own, BF), DMA((14 + nd + nu,))]
+                        V(all_rows, F32), V((2,) + own, BF), V(own, BF), DMA((14 + nd + nu,))]
         + [DMA((seqs,))] * 6 + [DMA((n,))] * 6 + [DMA((n, 3))] * 4 + [DMA((n,))] * 3
-        + [DMA((6,))] * 2 + [DMA((6,))],
+        + [DMA((6,))] * 2 + [DMA((7,))],
         name="layer_part",
         compiler_params=pltpu.CompilerParams(collective_id=1, has_side_effects=True, vmem_limit_bytes=63 << 20),
     )(lengths, tokens, cot, w, wo, wu, wd, qvb, bo, g1, s1, bu, bd, g2, s2)
 
 
-def finish_kernel(d_h, u_h, o_h, q_h, out_h, din_h, sums_ref, fd, fu, fo, fq, fout, fdin, qvb, outb, n1g, n1s, upb, downb, n2g, n2s,
-                  low, full, rows, ls, os_):
+def finish_kernel(d_h, u_h, o_h, q_h, out_h, din_h, sums_h, fd, fu, fo, fq, fout, fdin,
+                  qvb_h, outb_h, n1g_h, n1s_h, upb_h, downb_h, n2g_h, n2s_h,
+                  low, full, rows, sums_ref, qvb, outb, n1g, n1s, upb, downb, n2g, n2s, ls, os_, ms):
     R, C = low.shape[1:]
     nd, nu = d_h.shape[0] // R, u_h.shape[1] // C
     cut = lambda ref, i: ref.at[:, pl.ds(i * C, C)]
@@ -590,8 +606,14 @@
     pieces = len(ends)
     loads += [pltpu.make_async_copy(s, rows.at[i], ls.at[pieces + i]) for i, s in enumerate((out_h, din_h))]
     stores += [pltpu.make_async_copy(rows.at[i], t, os_.at[pieces + i]) for i, t in enumerate((fout, fdin))]
+    sums_load = pltpu.make_async_copy(sums_h, sums_ref, ms.at[8])
+    sums_load.start()
     for cp in loads:
         cp.start()
+    small = [pltpu.make_async_copy(s, t, ms.at[i]) for i, (s, t) in enumerate(
+        ((qvb, qvb_h), (outb, outb_h), (n1g, n1g_h), (n1s, n1s_h), (upb, upb_h), (downb, downb_h), (n2g, n2g_h),
+         (n2s, n2s_h)))]
+    sums_load.wait()
     n = lax.axis_index("narrow")
     for i in range(4):
         @pl.when(n == i)
@@ -601,12 +623,14 @@
             for j, ref in ((2, outb), (3, n1g), (4, n1s), (5 + nu, downb), (6 + nu, n2g), (7 + nu, n2s)):
                 ref[...] = sums_ref[j, at]
             upb[...] = sums_ref[5 + i]
+    for cp in small:
+        cp.start()
     for i, (a, b) in enumerate(zip(loads, stores)):
         a.wait()
         if i < pieces:
             full[i] = low[i].astype(F32)
         b.start()
-    for cp in stores:
+    for cp in stores + small:
         cp.wait()
 
 
@@ -620,9 +644,10 @@
     return pl.pallas_call(
         finish_kernel,
         out_shape=shapes,
-        in_specs=[hbm] * 6 + [vm],
-        out_specs=[hbm] * 6 + [vm] * 8,
-        scratch_shapes=[V((n, R, d), BF), V((n, R, d), F32), V((2,) + output.shape, BF), DMA((n + 2,)), DMA((n + 2,))],
+        in_specs=[hbm] * 7,
+        out_specs=[hbm] * 14,
+        scratch_shapes=[V((n, R, d), BF), V((n, R, d), F32), V((2,) + output.shape, BF), V(sums.shape, F32)]
+        + [V(a.shape, F32) for a in shapes[6:]] + [DMA((n + 2,)), DMA((n + 2,)), DMA((9,))],
         name="finish_part",
         compiler_params=pltpu.CompilerParams(vmem_limit_bytes=60 << 20),
     )(down, up, out, qkv, output, input_grad, sums)

time: 159 us -> 158 us (level)
  no operation moved by 1% of the time
where the time goes in v6:
time: 158 us
  Pallas kernels  157 us (99%)
    pallas_call x1, Pallas kernels, layer_part(): pl.pallas_call(layer_kernel, out_shape=(S(flat, BF), S((nd * R, d), BF),...  151 us
    pallas_call x1, Pallas kernels, finish_part(): pl.pallas_call(finish_kernel, out_shape=shapes, in_specs=[hbm] * 7, out_s...  5.7 us

profile of v6, /device:TPU:0, one launch (start us, length us, event | category | flops | bytes accessed | tf_op | source)
XLA Modules:
  0.0 157.5 jit_solution(15623214858445400758)
XLA Ops:
  0.7 151.0 %layer_part.1 = (bf16[384,768]{1,0:T(8,128)(2,1)}, bf16[768,768]{1,0:T(8,128)(2,1)}, bf16[192,3072]{1,0:T(8,128)(2,1)}, bf16[192,768]{1,0:T(8,128)(2,1)}, bf16[1...) custom-call(s32[3]{0:T(128)} %len_ref.1, bf16[3,128,768]{2,1,0:T(8,128)(2,1)} %tok_h.1, ...), custom_call_target="tpu_custom_call" | custom-call | tf_op jit(solution)/shard_map/layer_part/pallas_call | solution.py:574
  151.6 5.7 %finish_part.1 = (f32[768,768]{1,0:T(8,128)}, f32[192,3072]{1,0:T(8,128)}, f32[192,768]{1,0:T(8,128)}, f32[192,2304]{1,0:T(8,128)}, bf16[384,768]{1,0:T(8,128)(2...) custom-call(bf16[768,768]{1,0:T(8,128)(2,1)} %get-tuple-element.35.d, ...), custom_call_target="tpu_custom_call" | custom-call | tf_op jit(solution)/shard_map/finish_part/pallas_call | solution.py:644

commit v7 on v6

--- a/solution.py
+++ b/solution.py
@@ -20,7 +20,7 @@
 DMA = pltpu.SemaphoreType.DMA
 ANY = pl.ANY
 UNROLL_ATT = 6
-UNROLL_UP = 3
+UNROLL_UP = 6
 
 
 def dg(a, b, ca, cb):
@@ -69,7 +69,7 @@
 LAGS = (0, 1, 3, 4, 5, 7, 11)
 UNITS = 4
 ORDER = (3, 2, 5, 4, 6, 1)
-UNROLL_BACK = 1
+UNROLL_BACK = 3
 
 
 def layer_kernel(len_ref, tok_h, cot_h, w_h, wo_h, wu_h, wd_h, qvb_h, bo_h, g1_h, s1_h, bu_h, bd_h, g2_h, s2_h,
@@ -487,10 +487,23 @@
 
         lax.fori_loop(0, 2 * seqs, add, 0)
 
+    din_out = pltpu.make_async_copy(x1.at[0], din_hbm, xs.at[4])
+
+    def input_out():
+        cx2.wait_recv()
+
+        def out_x(i, carry):
+            r = pl.ds(pl.multiple_of(i * quarter, quarter), quarter)
+            x1[0, i] = (dsum[r] + dtok[y, c, i].astype(F32) + x2[i].astype(F32)).astype(BF)
+            return carry
+
+        lax.fori_loop(0, seqs, out_x, 0)
+        din_out.start()
+
     units = seqs * pairs
     slots_of_units = -(-units // UNITS)
     extra = {3: [rows_back], 9: [lambda: qkv_piece(0)], 10: [lambda: qkv_piece(1), lambda: qkv_piece(2), sums0],
-             11: [input_part, sums1], 12: [add_x1, sums2], 13: [cx2.start, sums3], 16: [sums4]}
+             11: [input_part, sums1], 12: [add_x1, sums2], 13: [cx2.start, sums3], 16: [sums4], 21: [input_out]}
 
     def drain(p):
         c1(p).wait_send()
@@ -528,16 +541,6 @@
         return carry
 
     lax.fori_loop(3, pieces + LAGS[6], slot, 0)
-    cx2.wait_recv()
-
-    def out_x(i, carry):
-        r = pl.ds(pl.multiple_of(i * quarter, quarter), quarter)
-        x1[0, i] = (dsum[r] + dtok[y, c, i].astype(F32) + x2[i].astype(F32)).astype(BF)
-        return carry
-
-    lax.fori_loop(0, seqs, out_x, 0)
-    din_out = pltpu.make_async_copy(x1.at[0], din_hbm, xs.at[4])
-    din_out.start()
     small(0, 0, core_peer).wait_send()
     small(1, 1, y_peer).wait_send()
     small(2, 2, x_peer).wait_send()

time: 158 us -> 157 us (level)
  no operation moved by 1% of the time
where the time goes in v7:
time: 157 us
  Pallas kernels  156 us (99%)
    pallas_call x1, Pallas kernels, layer_part(): pl.pallas_call(layer_kernel, out_shape=(S(flat, BF), S((nd * R, d), BF),...  151 us
    pallas_call x1, Pallas kernels, finish_part(): pl.pallas_call(finish_kernel, out_shape=shapes, in_specs=[hbm] * 7, out_s...  5.7 us

profile of v7, /device:TPU:0, one launch (start us, length us, event | category | flops | bytes accessed | tf_op | source)
XLA Modules:
  0.0 157.2 jit_solution(15735390984925418181)
XLA Ops:
  0.7 150.6 %layer_part.1 = (bf16[384,768]{1,0:T(8,128)(2,1)}, bf16[768,768]{1,0:T(8,128)(2,1)}, bf16[192,3072]{1,0:T(8,128)(2,1)}, bf16[192,768]{1,0:T(8,128)(2,1)}, bf16[1...) custom-call(s32[3]{0:T(128)} %len_ref.1, bf16[3,128,768]{2,1,0:T(8,128)(2,1)} %tok_h.1, ...), custom_call_target="tpu_custom_call" | custom-call | tf_op jit(solution)/shard_map/layer_part/pallas_call | solution.py:577
  151.3 5.7 %finish_part.1 = (f32[768,768]{1,0:T(8,128)}, f32[192,3072]{1,0:T(8,128)}, f32[192,768]{1,0:T(8,128)}, f32[192,2304]{1,0:T(8,128)}, bf16[384,768]{1,0:T(8,128)(2...) custom-call(bf16[768,768]{1,0:T(8,128)(2,1)} %get-tuple-element.35.d, ...), custom_call_target="tpu_custom_call" | custom-call | tf_op jit(solution)/shard_map/finish_part/pallas_call | solution.py:647

commit v8 on v7

--- a/solution.py
+++ b/solution.py
@@ -19,7 +19,7 @@
 V = pltpu.VMEM
 DMA = pltpu.SemaphoreType.DMA
 ANY = pl.ANY
-UNROLL_ATT = 6
+UNROLL_ATT = 3
 UNROLL_UP = 6
 
 
@@ -167,8 +167,6 @@
     for s in range(seqs):
         copy_to(toks.at[s, far_n], toks.at[s, far_n], fs.at[s], fr.at[s], core_peer).wait_recv()
         project(s, 1 - y)
-        if s + 1 < seqs:
-            fetch_far(s + 1)
         live = lax.broadcasted_iota(jnp.int32, (keys, 2 * quarter), 0) < len_ref[s]
 
         def unit(p, carry):
@@ -183,7 +181,10 @@
             ctx[s * quarter:(s + 1) * quarter, cols] = unstack_heads(dg(vp, probs, 0, 0)).astype(BF)
             return carry
 
-        lax.fori_loop(0, pairs, unit, 0, unroll=UNROLL_ATT)
+        lax.fori_loop(0, pairs // 2, unit, 0, unroll=UNROLL_ATT)
+        if s + 1 < seqs:
+            fetch_far(s + 1)
+        lax.fori_loop(pairs // 2, pairs, unit, 0, unroll=UNROLL_ATT)
 
     part2[...] = jnp.zeros_like(part2)
     chunk = 64

time: 157 us -> 157 us (level)
  no operation moved by 1% of the time
where the time goes in v8:
time: 157 us; the launch traced here: 156 us
  Pallas kernels  156 us (99%)
    pallas_call x1, Pallas kernels, layer_part(): pl.pallas_call(layer_kernel, out_shape=(S(flat, BF), S((nd * R, d), BF),...  150 us
    pallas_call x1, Pallas kernels, finish_part(): pl.pallas_call(finish_kernel, out_shape=shapes, in_specs=[hbm] * 7, out_s...  5.7 us

profile of v8, /device:TPU:0, one launch (start us, length us, event | category | flops | bytes accessed | tf_op | source)
XLA Modules:
  0.0 156.3 jit_solution(10537010678679451875)
XLA Ops:
  0.7 149.8 %layer_part.1 = (bf16[384,768]{1,0:T(8,128)(2,1)}, bf16[768,768]{1,0:T(8,128)(2,1)}, bf16[192,3072]{1,0:T(8,128)(2,1)}, bf16[192,768]{1,0:T(8,128)(2,1)}, bf16[1...) custom-call(s32[3]{0:T(128)} %len_ref.1, bf16[3,128,768]{2,1,0:T(8,128)(2,1)} %tok_h.1, ...), custom_call_target="tpu_custom_call" | custom-call | tf_op jit(solution)/shard_map/layer_part/pallas_call | solution.py:578
  150.5 5.7 %finish_part.1 = (f32[768,768]{1,0:T(8,128)}, f32[192,3072]{1,0:T(8,128)}, f32[192,768]{1,0:T(8,128)}, f32[192,2304]{1,0:T(8,128)}, bf16[384,768]{1,0:T(8,128)(2...) custom-call(bf16[768,768]{1,0:T(8,128)(2,1)} %get-tuple-element.35.d, ...), custom_call_target="tpu_custom_call" | custom-call | tf_op jit(solution)/shard_map/finish_part/pallas_call | solution.py:648
